TPU v7x, 256 devices: a whole 4x4x8 slice. The times are simulated.
256 devices in a mesh: doc: 8 (over y, core), term: 32 (over x, z).
Axes of the slice: x: 4, y: 4, z: 8, core: 2. Of those that a mesh axis runs over, the one named last changes fastest.
Arguments:
- slab: float32 [8192, 32768], P('doc', 'term'), may hold values from 0.05 to 4
- doc_factor: float32 [8192, 128], P('doc'), may hold values from 0.02 to 5, as said below
- term_factor: float32 [32768, 128], P('term'), may hold values from 0.005 to 5, as said below
Outputs:
- doc_out: float32 [8192, 128], P('doc')
- term_out: float32 [32768, 128], P('term')
Inputs may be any that keep to these rules, and one draw needn't show every extreme that they name: `doc_factor`: positive entries. `term_factor`: positive entries.
All inputs are finite; a program needn't handle non-finite values.
Results may differ from a plain program's by a relative error of at most 0.0001.
Values sent between devices are 32-bit elements; how exact they have to be, the bound alone decides.
No kernel may reach another device: no remote copies, remote signals or barrier semaphores. Data moves between devices by JAX's collectives and lax.ppermute only.
A program may use at most 64 MiB of HBM per device.

v0:
```python
import jax
import jax.numpy as jnp
from jax import lax
from jax.sharding import PartitionSpec as P

OUTER = 2
INNER = 2


def sent_to_all(value, axis):
    copies = jnp.broadcast_to(value, (lax.axis_size(axis), *value.shape))
    return lax.all_to_all(copies, axis, split_axis=0, concat_axis=0, tiled=True)


def over_copies(value, axis):
    everything = sent_to_all(value, axis)
    return jnp.sum(everything, axis=0)


def cut_along(value, dim, length):
    before, after = (value.shape[:dim], value.shape[dim + 1 :])
    return jnp.moveaxis(value.reshape(*before, length, -1, *after), dim, 0)


def summed_on_arrival(value, axis, dim):
    blocks = cut_along(value, dim, lax.axis_size(axis))
    arrived = lax.all_to_all(blocks, axis, split_axis=0, concat_axis=0, tiled=True)
    return arrived.sum(axis=0)


def joined_along(blocks, dim):
    dims = list(blocks.shape[1:])
    dims[dim] *= blocks.shape[0]
    return jnp.moveaxis(blocks, 0, dim).reshape(dims)


def gathered_copies(value, axis, dim):
    return joined_along(sent_to_all(value, axis), dim)


def total_of_pieces(value, axis):
    blocks = lax.all_gather(value, axis)
    return blocks.sum(axis=0)


def quotient(slab, doc_factor, term_factor):
    product = jnp.dot(
        doc_factor,
        term_factor.T,
        precision=lax.Precision.HIGHEST,
        preferred_element_type=jnp.float32,
    )
    return slab / product


def on_device(slab, doc_factor, term_factor):
    for _ in range(OUTER):
        term_mass = over_copies(jnp.sum(term_factor, axis=0), "term")
        for _ in range(INNER):
            ratios = quotient(slab, doc_factor, term_factor)
            partial_value = jnp.dot(
                ratios,
                term_factor,
                precision=lax.Precision.HIGHEST,
                preferred_element_type=jnp.float32,
            )
            shared = summed_on_arrival(partial_value, "term", 0)
            count_rows = shared.shape[0]
            offset = lax.axis_index("term") * count_rows
            own_rows = lax.dynamic_slice_in_dim(doc_factor, offset, count_rows, 0)
            doc_factor = gathered_copies(own_rows * shared / term_mass, "term", 0)
        ratios = quotient(slab, doc_factor, term_factor)
        local_terms = jnp.dot(
            ratios.T,
            doc_factor,
            precision=lax.Precision.HIGHEST,
            preferred_element_type=jnp.float32,
        )
        numerator, doc_mass = (
            total_of_pieces(local_terms, "doc"),
            total_of_pieces(jnp.sum(doc_factor, axis=0), "doc"),
        )
        term_factor = term_factor * numerator / doc_mass
    return (doc_factor, term_factor)


def solution(mesh):
    return jax.shard_map(
        on_device,
        mesh=mesh,
        in_specs=(P("doc", "term"), P("doc", None), P("term", None)),
        out_specs=(P("doc", None), P("term", None)),
        check_vma=False,
    )
```

profile of v0, /device:TPU:1, one launch (start us, length us, event | category | flops | bytes accessed | tf_op | source)
XLA Modules:
  0.0 350.4 jit_solution(8902404061205691194)
XLA Ops:
  7.2 1.3 reduce_sum.127
  8.4 0.6 broadcast_in_dim.24
  9.0 11.9 %all-to-all-start.1 = ((f32[32,1,128]{2,1,0:T(1,128)}), f32[32,1,128]{2,1,0:T(1,128)S(1)}, u32[]{:S(2)}, u32[]{:S(2)}) async-start(f32[32,1,128]{2,1,0:T(1,128)} %broadcast_in_dim.24), calls=%async_computation.1 | async-start | bytes 32768 | tf_op jit(solution)/shard_map/all_to_all | solution.py:12
  20.9 4.8 %fusion.13 = f32[1024,1024]{1,0:T(8,128)S(1)} fusion(f32[1024,128]{1,0:T(8,128)} %param.4, f32[1024,128]{1,0:T(8,128)} %param.5), kind=kOutput, calls=%fused_computation.19 | convolution fusion | flops 1610612736 | bytes 5242880 | tf_op jit(solution)/shard_map/dot_general | solution.py:47
  25.8 4.3 %fusion.10 = f32[1024,128]{1,0:T(8,128)} fusion(f32[1024,128]{1,0:T(8,128)S(1)} %copy-done, f32[1024,1024]{1,0:T(8,128)S(1)} %copy-done.1, f32[1024,1024]{1,0:T(8,128)S(1)} %fusion.13), kind=kOutput, calls=%fused_computation.10 | convolution fusion | flops 1611661312 | bytes 9437184 | tf_op jit(solution)/shard_map/dot_general | solution.py:61
  30.0 9.2 %all-to-all-start = ((f32[32,32,128]{2,1,0:T(8,128)}), f32[32,32,128]{2,1,0:T(8,128)S(1)}, u32[]{:S(2)}, u32[]{:S(2)}) async-start(f32[32,32,128]{2,1,0:T(8,128)} %bitcast), calls=%async_computation | async-start | bytes 1048576 | tf_op jit(solution)/shard_map/all_to_all | solution.py:27
  39.3 0.0 all-gather.9.cloned.1.call-start
  39.3 13.9 %all-to-all-done = f32[32,32,128]{2,1,0:T(8,128)S(1)} async-done(((f32[32,32,128]{2,1,0:T(8,128)}), f32[32,32,128]{2,1,0:T(8,128)S(1)}, u32[]{:S(2)}, u32[]{:S(2)}) %all-to-all-start) | async-done | bytes 524320 | tf_op jit(solution)/shard_map/all_to_all | solution.py:27
  53.3 0.9 multiply_divide_fusion.5
  54.2 0.1 broadcast_in_dim.25
  54.3 21.3 %all_to_all.52 = f32[32,32,128]{2,1,0:T(8,128)S(1)} all-to-all(f32[32,32,128]{2,1,0:T(8,128)S(1)} %broadcast_in_dim.25), channel_id=1, replica_groups=mesh['doc'=8,'term'=32] {'term'}, dimensions={0} | all-to-all | bytes 1048576 | tf_op jit(solution)/shard_map/all_to_all | solution.py:12
  75.5 3.5 fusion.14
  79.0 3.5 fusion.8
  82.5 21.2 %all_to_all.53 = f32[32,32,128]{2,1,0:T(8,128)S(1)} all-to-all(f32[32,32,128]{2,1,0:T(8,128)S(1)} %bitcast.45), channel_id=1, replica_groups=mesh['doc'=8,'term'=32] {'term'}, dimensions={0} | all-to-all | bytes 1048576 | tf_op jit(solution)/shard_map/all_to_all | solution.py:27
  103.7 0.1 broadcast_in_dim.26
  103.8 21.8 %all_to_all.54 = f32[32,32,128]{2,1,0:T(8,128)S(1)} all-to-all(f32[32,32,128]{2,1,0:T(8,128)S(1)} %broadcast_in_dim.26), channel_id=1, replica_groups=mesh['doc'=8,'term'=32] {'term'}, dimensions={0} | all-to-all | bytes 1048576 | tf_op jit(solution)/shard_map/all_to_all | solution.py:12
  125.6 3.5 fusion.15
  129.1 7.5 %fusion.6 = f32[1024,128]{1,0:T(8,128)} fusion(f32[1024,128]{1,0:T(8,128)S(1)} %bitcast.33, f32[1024,1024]{1,0:T(8,128)S(1)} %copy-done.3, f32[1024,1024]{1,0:T(8,128)S(1)} %fusion.15), kind=kOutput, calls=%fused_computation.6 | convolution fusion | flops 1611661312 | bytes 9437184 | tf_op jit(solution)/shard_map/dot_general | solution.py:73
  136.6 0.0 all-gather.9.cloned.1.call-update
  136.7 0.2 reduce_sum.131
  136.8 16.1 %all-gather.4 = f32[8,1,128]{2,1,0:T(1,128)S(1)} all-gather(f32[1,1,128]{2,1,0:T(1,128)S(1)} %bitcast.49), channel_id=3, replica_groups=mesh['doc'=8,'term'=32] {'doc'}, dimensions={0}, use_global_device_ids=true | all-gather | bytes 4608 | tf_op jit(solution)/shard_map/all_gather | solution.py:42
  153.0 20.3 %all-gather.9.cloned.1.call-done = f32[8192,128]{1,0:T(8,128)} async-done(((f32[1024,128]{1,0:T(8,128)}), f32[8192,128]{1,0:T(8,128)}) %all-gather.9.cloned.1.call-update) | async-done | bytes 4194320 | tf_op jit(solution)/shard_map/all_gather | solution.py:42
  173.3 2.5 reduce_sum.130
  175.8 0.2 fusion.12
  175.9 5.0 %fusion.16 = f32[1024,1024]{1,0:T(8,128)} fusion(f32[1024,128]{1,0:T(8,128)S(1)} %bitcast.34, f32[1024,128]{1,0:T(8,128)S(1)} %get-tuple-element.3), kind=kOutput, calls=%fused_computation.22 | convolution fusion | flops 1610612736 | bytes 5242880 | tf_op jit(solution)/shard_map/dot_general | solution.py:47
  180.9 0.6 broadcast_in_dim.27
  181.5 9.5 %all-to-all-start.6 = ((f32[32,1,128]{2,1,0:T(1,128)}), f32[32,1,128]{2,1,0:T(1,128)S(1)}, u32[]{:S(2)}, u32[]{:S(2)}) async-start(f32[32,1,128]{2,1,0:T(1,128)} %broadcast_in_dim.27), calls=%async_computation.6 | async-start | bytes 32768 | tf_op jit(solution)/shard_map/all_to_all | solution.py:12
  191.1 6.7 %fusion.4 = f32[1024,128]{1,0:T(8,128)} fusion(f32[1024,128]{1,0:T(8,128)S(1)} %get-tuple-element.3, f32[1024,1024]{1,0:T(8,128)} %param.3, f32[1024,1024]{1,0:T(8,128)} %fusion.16), kind=kOutput, calls=%fused_computation.4 | convolution fusion | flops 1611661312 | bytes 9437184 | tf_op jit(solution)/shard_map/dot_general | solution.py:61
  197.7 1.9 all-to-all-done.6
  199.7 7.3 %all-to-all-start.5 = ((f32[32,32,128]{2,1,0:T(8,128)}), f32[32,32,128]{2,1,0:T(8,128)S(1)}, u32[]{:S(2)}, u32[]{:S(2)}) async-start(f32[32,32,128]{2,1,0:T(8,128)} %bitcast.7), calls=%async_computation.5 | async-start | bytes 1048576 | tf_op jit(solution)/shard_map/all_to_all | solution.py:27
  207.0 0.0 all-gather.11.cloned.1.call-start
  207.0 14.5 %all-to-all-done.5 = f32[32,32,128]{2,1,0:T(8,128)S(1)} async-done(((f32[32,32,128]{2,1,0:T(8,128)}), f32[32,32,128]{2,1,0:T(8,128)S(1)}, u32[]{:S(2)}, u32[]{:S(2)}) %all-to-all-start.5) | async-done | bytes 524320 | tf_op jit(solution)/shard_map/all_to_all | solution.py:27
  221.6 0.1 broadcast_in_dim.28
  221.7 21.5 %all_to_all.55 = f32[32,32,128]{2,1,0:T(8,128)S(1)} all-to-all(f32[32,32,128]{2,1,0:T(8,128)S(1)} %broadcast_in_dim.28), channel_id=1, replica_groups=mesh['doc'=8,'term'=32] {'term'}, dimensions={0} | all-to-all | bytes 1048576 | tf_op jit(solution)/shard_map/all_to_all | solution.py:12
  243.2 3.5 fusion.17
  246.7 3.5 fusion.2
  250.2 20.8 %all_to_all.56 = f32[32,32,128]{2,1,0:T(8,128)S(1)} all-to-all(f32[32,32,128]{2,1,0:T(8,128)S(1)} %bitcast.46), channel_id=1, replica_groups=mesh['doc'=8,'term'=32] {'term'}, dimensions={0} | all-to-all | bytes 1048576 | tf_op jit(solution)/shard_map/all_to_all | solution.py:27
  271.0 0.1 broadcast_in_dim.29
  271.0 21.7 %all_to_all.57 = f32[32,32,128]{2,1,0:T(8,128)S(1)} all-to-all(f32[32,32,128]{2,1,0:T(8,128)S(1)} %broadcast_in_dim.29), channel_id=1, replica_groups=mesh['doc'=8,'term'=32] {'term'}, dimensions={0} | all-to-all | bytes 1048576 | tf_op jit(solution)/shard_map/all_to_all | solution.py:12
  292.7 3.5 fusion.18
  296.2 7.5 %fusion = f32[1024,128]{1,0:T(8,128)} fusion(f32[1024,128]{1,0:T(8,128)S(1)} %bitcast.37, f32[1024,1024]{1,0:T(8,128)S(1)} %copy-done.5, f32[1024,1024]{1,0:T(8,128)S(1)} %fusion.18), kind=kOutput, calls=%fused_computation | convolution fusion | flops 1611661312 | bytes 9437184 | tf_op jit(solution)/shard_map/dot_general | solution.py:73
  303.8 0.0 all-gather.11.cloned.1.call-update
  303.8 0.2 reduce_sum.138
  303.9 13.8 %all-gather.5 = f32[8,1,128]{2,1,0:T(1,128)S(1)} all-gather(f32[1,1,128]{2,1,0:T(1,128)S(1)} %bitcast.50), channel_id=5, replica_groups=mesh['doc'=8,'term'=32] {'doc'}, dimensions={0}, use_global_device_ids=true | all-gather | bytes 4608 | tf_op jit(solution)/shard_map/all_gather | solution.py:42
  317.8 21.2 %all-gather.11.cloned.1.call-done = f32[8192,128]{1,0:T(8,128)} async-done(((f32[1024,128]{1,0:T(8,128)}), f32[8192,128]{1,0:T(8,128)}) %all-gather.11.cloned.1.call-update) | async-done | bytes 4194320 | tf_op jit(solution)/shard_map/all_gather | solution.py:42
  338.9 2.5 reduce_sum.137
  341.4 0.9 multiply_divide_fusion
  342.3 0.8 copy.8
  (24 shorter events, 0.4 us)
Async XLA Ops:
  7.2 18.6 %copy-start = (f32[1024,128]{1,0:T(8,128)S(1)}, f32[1024,128]{1,0:T(8,128)}, u32[]{:S(2)}) copy-start(f32[1024,128]{1,0:T(8,128)} %param.5) | copy-start | bytes 1572868
  9.0 21.0 %all-to-all-start.1 = ((f32[32,1,128]{2,1,0:T(1,128)}), f32[32,1,128]{2,1,0:T(1,128)S(1)}, u32[]{:S(2)}, u32[]{:S(2)}) async-start(f32[32,1,128]{2,1,0:T(1,128)} %broadcast_in_dim.24), calls=%async_computation.1 | async-start | bytes 32768 | tf_op jit(solution)/shard_map/all_to_all | solution.py:12
  20.9 4.9 %copy-start.1 = (f32[1024,1024]{1,0:T(8,128)S(1)}, f32[1024,1024]{1,0:T(8,128)}, u32[]{:S(2)}) copy-start(f32[1024,1024]{1,0:T(8,128)} %param.3) | copy-start | bytes 12582916
  30.0 23.2 %all-to-all-start = ((f32[32,32,128]{2,1,0:T(8,128)}), f32[32,32,128]{2,1,0:T(8,128)S(1)}, u32[]{:S(2)}, u32[]{:S(2)}) async-start(f32[32,32,128]{2,1,0:T(8,128)} %bitcast), calls=%async_computation | async-start | bytes 1048576 | tf_op jit(solution)/shard_map/all_to_all | solution.py:27
  39.3 134.0 %all-gather.9.cloned.1.call-start = ((), (), s32[]{:S(2)}) async-start(), calls=%async_computation.10 | async-start | bytes 4718592 | tf_op jit(solution)/shard_map/all_gather | solution.py:42
  53.3 25.7 %copy-start.2 = (f32[1024,1024]{1,0:T(8,128)S(1)}, f32[1024,1024]{1,0:T(8,128)}, u32[]{:S(2)}) copy-start(f32[1024,1024]{1,0:T(8,128)} %param.3) | copy-start | bytes 12582916
  103.7 25.4 %copy-start.3 = (f32[1024,1024]{1,0:T(8,128)S(1)}, f32[1024,1024]{1,0:T(8,128)}, u32[]{:S(2)}) copy-start(f32[1024,1024]{1,0:T(8,128)} %param.3) | copy-start | bytes 12582916
  181.5 18.1 %all-to-all-start.6 = ((f32[32,1,128]{2,1,0:T(1,128)}), f32[32,1,128]{2,1,0:T(1,128)S(1)}, u32[]{:S(2)}, u32[]{:S(2)}) async-start(f32[32,1,128]{2,1,0:T(1,128)} %broadcast_in_dim.27), calls=%async_computation.6 | async-start | bytes 32768 | tf_op jit(solution)/shard_map/all_to_all | solution.py:12
  199.7 21.9 %all-to-all-start.5 = ((f32[32,32,128]{2,1,0:T(8,128)}), f32[32,32,128]{2,1,0:T(8,128)S(1)}, u32[]{:S(2)}, u32[]{:S(2)}) async-start(f32[32,32,128]{2,1,0:T(8,128)} %bitcast.7), calls=%async_computation.5 | async-start | bytes 1048576 | tf_op jit(solution)/shard_map/all_to_all | solution.py:27
  207.0 132.0 %all-gather.11.cloned.1.call-start = ((), (), s32[]{:S(2)}) async-start(), calls=%async_computation.11 | async-start | bytes 4718592 | tf_op jit(solution)/shard_map/all_gather | solution.py:42
  221.6 25.1 %copy-start.4 = (f32[1024,1024]{1,0:T(8,128)S(1)}, f32[1024,1024]{1,0:T(8,128)}, u32[]{:S(2)}) copy-start(f32[1024,1024]{1,0:T(8,128)} %param.3) | copy-start | bytes 12582916
  271.0 25.3 %copy-start.5 = (f32[1024,1024]{1,0:T(8,128)S(1)}, f32[1024,1024]{1,0:T(8,128)}, u32[]{:S(2)}) copy-start(f32[1024,1024]{1,0:T(8,128)} %param.3) | copy-start | bytes 12582916
Sparse Core Ops, SparseCore 0:
  136.8 36.4 all-gather.8
  303.9 34.9 all-gather.10
where the time goes:
time: 357 us; the launch traced here: 350 us
  blocking collectives  158 us (44%)
  waiting for transfers between devices  71.8 us (20%)
  matrix products  56.6 us (16%)
  starting transfers between devices  38 us (11%)
  between operations  14.8 us (4%)
  other arithmetic  8.74 us (2%)
    all_to_all x4, blocking collectives, sent_to_all(): return lax.all_to_all(copies, axis, split_axis=0, concat_axis=0, tiled=True)  86.3 us
    all_to_all x2, blocking collectives, summed_on_arrival(): lax.all_to_all(blocks, axis, split_axis=0, concat_axis=0, tiled=True)  41.9 us
    all_gather x2, waiting for transfers between devices, total_of_pieces(): blocks = lax.all_gather(value, axis)  41.5 us
    all_gather x2, blocking collectives, total_of_pieces(): blocks = lax.all_gather(value, axis)  30 us
    all_to_all x2, waiting for transfers between devices, summed_on_arrival(): lax.all_to_all(blocks, axis, split_axis=0, concat_axis=0, tiled=True)  28.4 us
    dot_general x6, matrix products, quotient(): jnp.dot(doc_factor, term_factor.T, precision=lax.Precision.HIGHEST, prefe...  23.7 us
    all_to_all x2, starting transfers between devices, sent_to_all(): return lax.all_to_all(copies, axis, split_axis=0, concat_axis=0, tiled=True)  21.4 us
    dot_general x4, matrix products, on_device(): jnp.dot(ratios, term_factor, precision=lax.Precision.HIGHEST, preferred_e...  17.9 us
  transfers between devices with their start and end apart: 6, of which 5 were waited for; matrix products, arithmetic and copies ran while one was open for 5% of the time, Pallas kernels for 0%

commit v1 on v0

v1 whole, which is shorter than its diff:
```python
import jax
import jax.numpy as jnp
from jax import lax
from jax.sharding import Mesh, PartitionSpec as P

OUTER = 2
INNER = 2
NEAR = ("x", "zl")
FAR = "zh"
DOC = ("y", "core")
TERM = ("x", "zh", "zl")


def exchange(blocks, axis):
    return lax.all_to_all(blocks, axis, split_axis=0, concat_axis=0, tiled=True)


def spread(value, axis):
    return exchange(jnp.broadcast_to(value, (lax.axis_size(axis), *value.shape)), axis)


def dot(a, b, dims):
    return lax.dot_general(
        a, b, (dims, ((), ())), precision=lax.Precision.HIGH, preferred_element_type=jnp.float32
    )


def with_row(blocks, row):
    extra = jnp.zeros((blocks.shape[0], 8, blocks.shape[2]), blocks.dtype)
    extra = extra.at[:, 0, :].set(row)
    return jnp.concatenate([blocks, extra], axis=1)


def own_slice(value, axis):
    rows = value.shape[0] // lax.axis_size(axis)
    return lax.dynamic_slice_in_dim(value, lax.axis_index(axis) * rows, rows, 0)


def on_device(slab, doc_factor, term_factor):
    near, across = lax.axis_size(NEAR), lax.axis_size(DOC)
    rank = doc_factor.shape[1]
    docs = doc_factor.shape[0] // near
    terms = term_factor.shape[0] // across
    doc_own = own_slice(doc_factor, NEAR)
    term_own = own_slice(term_factor, DOC)
    for _ in range(OUTER):
        for inner in range(INNER):
            ratios = slab / dot(doc_factor, term_factor, ((1,), (1,)))
            partial = dot(ratios, term_factor, ((1,), (0,)))
            blocks = partial.reshape(near, docs, rank)
            if inner == 0:
                blocks = with_row(blocks, jnp.sum(term_factor, axis=0))
            share = jnp.sum(exchange(blocks, NEAR), axis=0)
            share = jnp.sum(spread(share, FAR), axis=0)
            if inner == 0:
                term_mass = share[docs]
            doc_own = doc_own * share[:docs] / term_mass
            doc_factor = spread(doc_own, NEAR).reshape(-1, rank)
        ratios = slab / dot(doc_factor, term_factor, ((1,), (1,)))
        partial = dot(ratios, doc_factor, ((0,), (0,)))
        blocks = with_row(partial.reshape(across, terms, rank), jnp.sum(doc_factor, axis=0))
        share = jnp.sum(exchange(blocks, DOC), axis=0)
        term_own = term_own * share[:terms] / share[terms]
        term_factor = spread(term_own, DOC).reshape(-1, rank)
    return (doc_factor, term_factor)


def solution(mesh):
    parts = Mesh(mesh.devices.reshape(4, 2, 4, 4, 2), ("y", "core", "x", "zh", "zl"))
    return jax.shard_map(
        on_device,
        mesh=parts,
        in_specs=(P(DOC, TERM), P(DOC, None), P(TERM, None)),
        out_specs=(P(DOC, None), P(TERM, None)),
        check_vma=False,
    )
```

time: 357 us -> 257 us (0.72); the launches traced: 350 us -> 256 us
  waiting for transfers between devices: 71.8 us -> 19.7 us
  matrix products: 56.6 us -> 38 us
  between operations: 14.8 us -> 0.94 us
  starting transfers between devices: 38 us -> 27.8 us
  local copies, waits for them, and re-layouts: 2.27 us -> 8.78 us
  other arithmetic: 8.74 us -> 2.9 us
    all_gather x2 -> x0, waiting for transfers between devices: 41.5 us -> none  [total_of_pieces(): blocks = lax.all_gather(value, axis)]
    all_to_all x6 -> x13, blocking collectives: 128 us -> 158 us  [exchange(): return lax.all_to_all(blocks, axis, split_axis=0, concat_axis=0, tiled=True)]
    all_gather x2 -> x0, blocking collectives: 30 us -> none  [total_of_pieces(): blocks = lax.all_gather(value, axis)]
    dot_general x12, matrix products: 56.6 us -> 38 us  [dot(): lax.dot_general(a, b, (dims, ((), ())), precision=lax.Precision.HIGH, pre...]
    all_to_all x4 -> x3, waiting for transfers between devices: 30.4 us -> 19.7 us  [exchange(): return lax.all_to_all(blocks, axis, split_axis=0, concat_axis=0, tiled=True)]
    all_to_all x4 -> x3, starting transfers between devices: 37.9 us -> 27.8 us  [exchange(): return lax.all_to_all(blocks, axis, split_axis=0, concat_axis=0, tiled=True)]
    unnamed x13 -> x7, local copies, waits for them, and re-layouts: 0.83 us -> 6.96 us
    reduce_sum x12, other arithmetic: 6.63 us -> 0.55 us  [the longest x2 0.3 us: on_device(): blocks = with_row(blocks, jnp.sum(term_factor, axis=0))]
  transfers between devices with their start and end apart: 6 -> 3, of which waited for: 5 -> 3; matrix products, arithmetic and copies ran while one was open for 5% -> 2% of each run, Pallas kernels for 0% -> 0%
where the time goes in v1:
time: 257 us; the launch traced here: 256 us
  blocking collectives  158 us (61%)
  matrix products  38 us (15%)
  starting transfers between devices  27.8 us (11%)
  waiting for transfers between devices  19.7 us (8%)
  local copies, waits for them, and re-layouts  8.78 us (3%)
  other arithmetic  2.9 us (1%)
    all_to_all x13, blocking collectives, exchange(): return lax.all_to_all(blocks, axis, split_axis=0, concat_axis=0, tiled=True)  158 us
    dot_general x12, matrix products, dot(): lax.dot_general(a, b, (dims, ((), ())), precision=lax.Precision.HIGH, pre...  38 us
    all_to_all x3, starting transfers between devices, exchange(): return lax.all_to_all(blocks, axis, split_axis=0, concat_axis=0, tiled=True)  27.8 us
    all_to_all x3, waiting for transfers between devices, exchange(): return lax.all_to_all(blocks, axis, split_axis=0, concat_axis=0, tiled=True)  19.7 us
    unnamed x7, local copies, waits for them, and re-layouts  6.96 us
  transfers between devices with their start and end apart: 3, of which 3 were waited for; matrix products, arithmetic and copies ran while one was open for 2% of the time, Pallas kernels for 0%

profile of v1, /device:TPU:1, one launch (start us, length us, event | category | flops | bytes accessed | tf_op | source)
XLA Modules:
  0.0 256.3 jit_solution(10896574447551164906)
XLA Ops:
  0.6 0.0 copy-start
  0.6 5.0 %fusion.8 = f32[1024,1024]{1,0:T(8,128)} fusion(f32[1024,128]{1,0:T(8,128)} %param.12, f32[1024,128]{1,0:T(8,128)} %param.13), kind=kOutput, calls=%fused_computation.27 | convolution fusion | flops 805306368 | bytes 5242880 | tf_op jit(solution)/shard_map/dot_general | solution.py:23
  5.6 0.0 copy-done
  5.6 0.1 reduce_sum.126
  5.8 5.3 %fusion.2 = f32[1024,128]{1,0:T(8,128)S(1)} fusion(f32[1024,128]{1,0:T(8,128)S(1)} %copy-done, f32[1024,1024]{1,0:T(8,128)} %param.11, f32[1024,1024]{1,0:T(8,128)} %fusion.8), kind=kOutput, calls=%fused_computation.2 | convolution fusion | flops 806354944 | bytes 9437184 | tf_op jit(solution)/shard_map/dot_general | solution.py:23
  11.1 15.4 %all_to_all.80 = f32[8,136,128]{2,1,0:T(8,128)S(1)} all-to-all(f32[8,136,128]{2,1,0:T(8,128)S(1)} %select_maximum_fusion.3), channel_id=1, replica_groups=mesh['y'=4,'core'=2,'x'=4,'zh'=4,'zl'=2] {'x','zl'}, dimensions={0} | all-to-all | bytes 1114112 | tf_op jit(solution)/shard_map/all_to_all | solution.py:15
  26.5 0.7 broadcast_in_dim.34
  27.3 7.3 %all-to-all-start.1 = ((f32[4,136,128]{2,1,0:T(8,128)}), f32[4,136,128]{2,1,0:T(8,128)S(1)}, u32[]{:S(2)}, u32[]{:S(2)}) async-start(f32[4,136,128]{2,1,0:T(8,128)} %broadcast_in_dim.34), calls=%async_computation.1 | async-start | bytes 557056 | tf_op jit(solution)/shard_map/all_to_all | solution.py:15
  34.6 8.1 %all-to-all-done.1 = f32[4,136,128]{2,1,0:T(8,128)S(1)} async-done(((f32[4,136,128]{2,1,0:T(8,128)}), f32[4,136,128]{2,1,0:T(8,128)S(1)}, u32[]{:S(2)}, u32[]{:S(2)}) %all-to-all-start.1) | async-done | bytes 278560 | tf_op jit(solution)/shard_map/all_to_all | solution.py:15
  42.6 0.0 copy-start.1
  42.7 1.0 fusion.7
  43.7 10.7 %all_to_all.81 = f32[8,128,128]{2,1,0:T(8,128)S(1)} all-to-all(f32[8,128,128]{2,1,0:T(8,128)S(1)} %broadcast_in_dim.35), channel_id=1, replica_groups=mesh['y'=4,'core'=2,'x'=4,'zh'=4,'zl'=2] {'x','zl'}, dimensions={0} | all-to-all | bytes 1048576 | tf_op jit(solution)/shard_map/all_to_all | solution.py:15
  54.4 1.8 fusion.9
  56.2 0.0 copy-done.1
  56.2 1.8 fusion
  58.1 10.0 %all_to_all.82 = f32[8,128,128]{2,1,0:T(8,128)S(1)} all-to-all(f32[8,128,128]{2,1,0:T(8,128)S(1)} %bitcast.70), channel_id=1, replica_groups=mesh['y'=4,'core'=2,'x'=4,'zh'=4,'zl'=2] {'x','zl'}, dimensions={0} | all-to-all | bytes 1048576 | tf_op jit(solution)/shard_map/all_to_all | solution.py:15
  68.1 11.1 %all_to_all.83 = f32[4,128,128]{2,1,0:T(8,128)S(1)} all-to-all(f32[4,128,128]{2,1,0:T(8,128)S(1)} %broadcast_in_dim.36), channel_id=1, replica_groups=mesh['y'=4,'core'=2,'x'=4,'zh'=4,'zl'=2] {'zh'}, dimensions={0} | all-to-all | bytes 524288 | tf_op jit(solution)/shard_map/all_to_all | solution.py:15
  79.2 0.8 broadcast_in_dim.37
  80.0 3.7 %all-to-all-start.5 = ((f32[8,128,128]{2,1,0:T(8,128)}), f32[8,128,128]{2,1,0:T(8,128)S(1)}, u32[]{:S(2)}, u32[]{:S(2)}) async-start(f32[8,128,128]{2,1,0:T(8,128)} %broadcast_in_dim.37), calls=%async_computation.5 | async-start | bytes 1048576 | tf_op jit(solution)/shard_map/all_to_all | solution.py:15
  83.7 5.4 %copy.7 = f32[1024,1024]{0,1:T(8,128)} copy(f32[1024,1024]{1,0:T(8,128)} %param.11) | data formatting | bytes 8388608 | tf_op args[0]
  89.1 1.9 all-to-all-done.5
  91.0 4.2 %convolution_divide_fusion.3 = f32[1024,1024]{0,1:T(8,128)S(1)} fusion(f32[1024,1024]{0,1:T(8,128)} %copy.7, f32[1024,128]{1,0:T(8,128)S(1)} %bitcast.60, f32[1024,128]{1,0:T(8,128)S(1)} %copy-done), kind=kOutput, calls=%fused_computation.7 | convolution fusion | flops 806354944 | bytes 9437184 | tf_op jit(solution)/shard_map/dot_general | solution.py:23
  95.2 1.8 fusion.10
  97.0 0.2 reduce_sum.131
  97.2 0.8 select_maximum_fusion.2
  98.0 16.9 %all-to-all-start.6 = ((f32[8,136,128]{2,1,0:T(8,128)}), f32[8,136,128]{2,1,0:T(8,128)S(1)}, u32[]{:S(2)}, u32[]{:S(2)}) async-start(f32[8,136,128]{2,1,0:T(8,128)} %select_maximum_fusion.2), calls=%async_computation.6 | async-start | bytes 1114112 | tf_op jit(solution)/shard_map/all_to_all | solution.py:15
  114.9 9.7 %all-to-all-done.6 = f32[8,136,128]{2,1,0:T(8,128)S(1)} async-done(((f32[8,136,128]{2,1,0:T(8,128)}), f32[8,136,128]{2,1,0:T(8,128)S(1)}, u32[]{:S(2)}, u32[]{:S(2)}) %all-to-all-start.6) | async-done | bytes 557088 | tf_op jit(solution)/shard_map/all_to_all | solution.py:15
  124.7 12.7 %all_to_all.84 = f32[8,128,128]{2,1,0:T(8,128)S(1)} all-to-all(f32[8,128,128]{2,1,0:T(8,128)S(1)} %broadcast_in_dim.38), channel_id=1, replica_groups=mesh['y'=4,'core'=2,'x'=4,'zh'=4,'zl'=2] {'y','core'}, dimensions={0} | all-to-all | bytes 1048576 | tf_op jit(solution)/shard_map/all_to_all | solution.py:15
  137.4 4.2 %convolution_divide_fusion.2 = f32[1024,1024]{1,0:T(8,128)S(1)} fusion(f32[1024,1024]{1,0:T(8,128)} %param.11, f32[1024,128]{1,0:T(8,128)S(1)} %bitcast.62, f32[1024,128]{1,0:T(8,128)S(1)} %bitcast.52), kind=kOutput, calls=%fused_computation.6 | convolution fusion | flops 806354944 | bytes 9437184 | tf_op jit(solution)/shard_map/dot_general | solution.py:23
  141.7 1.8 fusion.11
  143.5 0.2 reduce_sum.133
  143.7 11.8 %all_to_all.85 = f32[8,136,128]{2,1,0:T(8,128)S(1)} all-to-all(f32[8,136,128]{2,1,0:T(8,128)S(1)} %select_maximum_fusion.1), channel_id=1, replica_groups=mesh['y'=4,'core'=2,'x'=4,'zh'=4,'zl'=2] {'x','zl'}, dimensions={0} | all-to-all | bytes 1114112 | tf_op jit(solution)/shard_map/all_to_all | solution.py:15
  155.6 10.6 %all_to_all.86 = f32[4,136,128]{2,1,0:T(8,128)S(1)} all-to-all(f32[4,136,128]{2,1,0:T(8,128)S(1)} %broadcast_in_dim.39), channel_id=1, replica_groups=mesh['y'=4,'core'=2,'x'=4,'zh'=4,'zl'=2] {'zh'}, dimensions={0} | all-to-all | bytes 557056 | tf_op jit(solution)/shard_map/all_to_all | solution.py:15
  166.3 10.9 %all_to_all.87 = f32[8,128,128]{2,1,0:T(8,128)S(1)} all-to-all(f32[8,128,128]{2,1,0:T(8,128)S(1)} %broadcast_in_dim.40), channel_id=1, replica_groups=mesh['y'=4,'core'=2,'x'=4,'zh'=4,'zl'=2] {'x','zl'}, dimensions={0} | all-to-all | bytes 1048576 | tf_op jit(solution)/shard_map/all_to_all | solution.py:15
  177.2 4.2 %convolution_divide_fusion.1 = f32[1024,1024]{1,0:T(8,128)S(1)} fusion(f32[1024,1024]{1,0:T(8,128)} %param.11, f32[1024,128]{1,0:T(8,128)S(1)} %bitcast.71, f32[1024,128]{1,0:T(8,128)S(1)} %bitcast.54), kind=kOutput, calls=%fused_computation.5 | convolution fusion | flops 806354944 | bytes 9437184 | tf_op jit(solution)/shard_map/dot_general | solution.py:23
  181.4 1.8 fusion.12
  183.2 10.0 %all_to_all.88 = f32[8,128,128]{2,1,0:T(8,128)S(1)} all-to-all(f32[8,128,128]{2,1,0:T(8,128)S(1)} %fusion.12), channel_id=1, replica_groups=mesh['y'=4,'core'=2,'x'=4,'zh'=4,'zl'=2] {'x','zl'}, dimensions={0} | all-to-all | bytes 1048576 | tf_op jit(solution)/shard_map/all_to_all | solution.py:15
  193.2 12.5 %all_to_all.89 = f32[4,128,128]{2,1,0:T(8,128)S(1)} all-to-all(f32[4,128,128]{2,1,0:T(8,128)S(1)} %broadcast_in_dim.41), channel_id=1, replica_groups=mesh['y'=4,'core'=2,'x'=4,'zh'=4,'zl'=2] {'zh'}, dimensions={0} | all-to-all | bytes 524288 | tf_op jit(solution)/shard_map/all_to_all | solution.py:15
  205.8 10.1 %all_to_all.90 = f32[8,128,128]{2,1,0:T(8,128)S(1)} all-to-all(f32[8,128,128]{2,1,0:T(8,128)S(1)} %broadcast_in_dim.42), channel_id=1, replica_groups=mesh['y'=4,'core'=2,'x'=4,'zh'=4,'zl'=2] {'x','zl'}, dimensions={0} | all-to-all | bytes 1048576 | tf_op jit(solution)/shard_map/all_to_all | solution.py:15
  215.9 4.2 %convolution_divide_fusion = f32[1024,1024]{0,1:T(8,128)S(1)} fusion(f32[1024,1024]{0,1:T(8,128)} %copy.7, f32[1024,128]{1,0:T(8,128)S(1)} %bitcast.57, f32[1024,128]{1,0:T(8,128)S(1)} %bitcast.56), kind=kOutput, calls=%fused_computation.4 | convolution fusion | flops 806354944 | bytes 9437184 | tf_op jit(solution)/shard_map/dot_general | solution.py:23
  220.2 1.8 fusion.13
  222.0 0.2 reduce_sum.138
  222.2 20.2 %all_to_all.91 = f32[8,136,128]{2,1,0:T(8,128)S(1)} all-to-all(f32[8,136,128]{2,1,0:T(8,128)S(1)} %select_maximum_fusion), channel_id=1, replica_groups=mesh['y'=4,'core'=2,'x'=4,'zh'=4,'zl'=2] {'y','core'}, dimensions={0} | all-to-all | bytes 1114112 | tf_op jit(solution)/shard_map/all_to_all | solution.py:15
  242.5 12.3 %all_to_all.92 = f32[8,128,128]{2,1,0:T(8,128)S(1)} all-to-all(f32[8,128,128]{2,1,0:T(8,128)S(1)} %broadcast_in_dim.43), channel_id=1, replica_groups=mesh['y'=4,'core'=2,'x'=4,'zh'=4,'zl'=2] {'y','core'}, dimensions={0} | all-to-all | bytes 1048576 | tf_op jit(solution)/shard_map/all_to_all | solution.py:15
  254.8 0.8 copy.11
  255.5 0.8 copy.12
  (34 shorter events, 0.7 us)
Async XLA Ops:
  0.6 5.0 %copy-start = (f32[1024,128]{1,0:T(8,128)S(1)}, f32[1024,128]{1,0:T(8,128)}, u32[]{:S(2)}) copy-start(f32[1024,128]{1,0:T(8,128)} %param.13) | copy-start | bytes 1572868
  27.3 15.4 %all-to-all-start.1 = ((f32[4,136,128]{2,1,0:T(8,128)}), f32[4,136,128]{2,1,0:T(8,128)S(1)}, u32[]{:S(2)}, u32[]{:S(2)}) async-start(f32[4,136,128]{2,1,0:T(8,128)} %broadcast_in_dim.34), calls=%async_computation.1 | async-start | bytes 557056 | tf_op jit(solution)/shard_map/all_to_all | solution.py:15
  42.6 13.6 %copy-start.1 = (f32[1024,1024]{1,0:T(8,128)S(1)}, f32[1024,1024]{1,0:T(8,128)}, u32[]{:S(2)}) copy-start(f32[1024,1024]{1,0:T(8,128)} %param.11) | copy-start | bytes 12582916
  80.0 11.0 %all-to-all-start.5 = ((f32[8,128,128]{2,1,0:T(8,128)}), f32[8,128,128]{2,1,0:T(8,128)S(1)}, u32[]{:S(2)}, u32[]{:S(2)}) async-start(f32[8,128,128]{2,1,0:T(8,128)} %broadcast_in_dim.37), calls=%async_computation.5 | async-start | bytes 1048576 | tf_op jit(solution)/shard_map/all_to_all | solution.py:15
  98.0 26.6 %all-to-all-start.6 = ((f32[8,136,128]{2,1,0:T(8,128)}), f32[8,136,128]{2,1,0:T(8,128)S(1)}, u32[]{:S(2)}, u32[]{:S(2)}) async-start(f32[8,136,128]{2,1,0:T(8,128)} %select_maximum_fusion.2), calls=%async_computation.6 | async-start | bytes 1114112 | tf_op jit(solution)/shard_map/all_to_all | solution.py:15

commit v2 on v1

v2 whole, which is shorter than its diff:
```python
import functools

import jax
import jax.numpy as jnp
from jax import lax
from jax.experimental import pallas as pl
from jax.experimental.pallas import tpu as pltpu
from jax.sharding import Mesh, PartitionSpec as P

OUTER = 2
INNER = 2
NEAR = ("x", "zl")
FAR = "zh"
DOC = ("y", "core")
TERM = ("x", "zh", "zl")
F32 = jnp.float32
PAD = 8
HELD = 512
DOC_STEP = 256
TERM_STEP = 512
LIMIT = 50


def exchange(blocks, axis):
    return lax.all_to_all(blocks, axis, split_axis=0, concat_axis=0, tiled=True)


def spread(value, axis):
    return exchange(jnp.broadcast_to(value, (lax.axis_size(axis), *value.shape)), axis)


def swap(value, axis, by=1):
    return lax.ppermute(value, axis, [(at, at ^ by) for at in range(lax.axis_size(axis))])


def total_over(value, axis):
    return sum([swap(value, axis, by) for by in range(1, lax.axis_size(axis))], value)


def own_slice(value, axis):
    rows = value.shape[0] // lax.axis_size(axis)
    return lax.dynamic_slice_in_dim(value, lax.axis_index(axis) * rows, rows, 0)


def halves(value):
    high = value.astype(jnp.bfloat16)
    return high, (value - high.astype(F32)).astype(jnp.bfloat16)


def product_of(doc, term_cat):
    high, low = doc
    return lax.dot_general(
        jnp.concatenate([high, low, high, low], axis=1),
        term_cat,
        (((1,), (1,)), ((), ())),
        preferred_element_type=F32,
    )


def term_operand(term):
    high, low = term
    return jnp.concatenate([high, high, low, low], axis=1)


def quotients(first, slab_ref, near_ref, docs, term_cat, held, arrived):
    split, step = near_ref.shape[0], docs[0][0].shape[0]
    head = pltpu.make_async_copy(slab_ref.at[pl.ds(0, split)], near_ref, arrived.at[0])
    tail = pltpu.make_async_copy(
        slab_ref.at[pl.ds(split, held.shape[0])], held, arrived.at[1]
    )
    if first:
        head.start()
    tail.start()
    products = [product_of(doc, term_cat) for doc in docs]
    if first:
        head.wait()
    for at, product in enumerate(products):
        start = at * step
        if start == split:
            tail.wait()
        source = near_ref if start < split else held
        yield halves(source[pl.ds(start % split, step), :] / product)


def doc_blocks(doc_ref, step):
    return [halves(doc_ref[start : start + step, :]) for start in range(0, doc_ref.shape[0], step)]


def doc_kernel(first, mass, slab_ref, near_ref, doc_ref, term_ref, out_ref, held, arrived):
    term = halves(term_ref[...])
    pair = jnp.concatenate(term, axis=1)
    pair = jnp.concatenate([pair, pair], axis=0)
    rank = doc_ref.shape[1]
    rows = out_ref.shape[1] - (PAD if mass else 0)
    docs = doc_blocks(doc_ref, DOC_STEP)
    start = 0
    for quotient in quotients(first, slab_ref, near_ref, docs, term_operand(term), held, arrived):
        both = jnp.dot(jnp.concatenate(quotient, axis=1), pair, preferred_element_type=F32)
        result = both[:, :rank] + both[:, rank:]
        for offset in range(0, DOC_STEP, rows):
            out_ref[(start + offset) // rows, :rows, :] = result[offset : offset + rows, :]
        start += DOC_STEP
    if mass:
        total = jnp.sum(term_ref[...], axis=0, keepdims=True)
        for at in range(out_ref.shape[0]):
            out_ref[at, rows:, :] = jnp.broadcast_to(total, (PAD, rank))


def term_kernel(first, mass, slab_ref, near_ref, doc_ref, term_ref, out_ref, held, arrived):
    rank = doc_ref.shape[1]
    term_cat = term_operand(halves(term_ref[...]))
    docs = doc_blocks(doc_ref, TERM_STEP)
    total = None
    for doc, quotient in zip(docs, quotients(first, slab_ref, near_ref, docs, term_cat, held, arrived)):
        pair = jnp.concatenate(doc, axis=1)
        part = lax.dot_general(
            jnp.concatenate(quotient, axis=0),
            jnp.concatenate([pair, pair], axis=0),
            (((0,), (0,)), ((), ())),
            preferred_element_type=F32,
        )
        total = part if total is None else total + part
    result = total[:, :rank] + total[:, rank:]
    sums = jnp.sum(doc_ref[...], axis=0, keepdims=True)
    count, rows = out_ref.shape[0], out_ref.shape[1] - PAD
    for at in range(count):
        out_ref[at, :rows, :] = result[at * rows : (at + 1) * rows, :]
        out_ref[at, rows:, :] = jnp.broadcast_to(sums, (PAD, rank))


def first_kernel(kernel, mass, slab_ref, doc_ref, term_ref, out_ref, near_ref, held, arrived):
    kernel(True, mass, slab_ref, near_ref, doc_ref, term_ref, out_ref, held, arrived)


def call(kernel, mass, shape, slab, near, doc, term):
    whole = pl.BlockSpec(memory_space=pltpu.VMEM)
    apart = pl.BlockSpec(memory_space=pltpu.HBM)
    first = near is None
    out = jax.ShapeDtypeStruct(shape, F32)
    kept = jax.ShapeDtypeStruct((HELD, slab.shape[1]), F32)
    return pl.pallas_call(
        functools.partial(first_kernel, kernel, mass) if first else functools.partial(kernel, False, mass),
        out_shape=(out, kept) if first else out,
        in_specs=[apart, whole, whole] if first else [apart, whole, whole, whole],
        out_specs=(whole, whole) if first else whole,
        scratch_shapes=[
            pltpu.VMEM((slab.shape[0] - HELD, slab.shape[1]), F32),
            pltpu.SemaphoreType.DMA((2,)),
        ],
        compiler_params=pltpu.CompilerParams(vmem_limit_bytes=LIMIT * 2**20),
    )(*((slab, doc, term) if first else (slab, near, doc, term)))


def on_device(slab, doc_factor, term_factor):
    near = lax.axis_size(NEAR)
    rank = doc_factor.shape[1]
    docs = doc_factor.shape[0] // near
    across = lax.axis_size("y")
    terms = term_factor.shape[0] // (2 * across)
    core, row = (lax.axis_index(axis).astype(jnp.uint32) for axis in ("core", "y"))
    here, away = core * across, (1 - core) * across
    partner = [row ^ at for at in range(across)]
    doc_own = own_slice(doc_factor, NEAR)
    term_own = own_slice(term_factor, ("core", "y"))
    slab, doc_factor, term_factor, doc_own, term_own, core, here, away, partner = lax.optimization_barrier(
        (slab, doc_factor, term_factor, doc_own, term_own, core, here, away, partner)
    )
    held = None
    for _ in range(OUTER):
        for inner in range(INNER):
            mass = inner == 0
            shape = (near, docs + (PAD if mass else 0), rank)
            blocks = call(doc_kernel, mass, shape, slab, held, doc_factor, term_factor)
            if held is None:
                blocks, held = blocks
            share = jnp.sum(exchange(blocks, NEAR), axis=0)
            share = total_over(share, FAR)
            if mass:
                term_mass = share[docs]
            doc_own = doc_own * share[:docs] / term_mass
            doc_factor = spread(doc_own, NEAR).reshape(-1, rank)
        shape = (2 * across, terms + PAD, rank)
        blocks = call(term_kernel, True, shape, slab, held, doc_factor, term_factor)
        mine = lax.dynamic_slice_in_dim(blocks, here, across, 0)
        other = lax.dynamic_slice_in_dim(blocks, away, across, 0)
        mine = mine + swap(other, "core")
        pieces = [lax.dynamic_index_in_dim(mine, at, 0, keepdims=False) for at in partner]
        share = sum([swap(pieces[by], "y", by) for by in range(1, across)], pieces[0])
        term_own = term_own * share[:terms] / share[terms]
        pieces = jnp.stack([term_own] + [swap(term_own, "y", by) for by in range(1, across)])
        mine = jnp.concatenate([lax.dynamic_index_in_dim(pieces, at, 0, keepdims=False) for at in partner], axis=0)
        other = swap(mine, "core")
        first = core == 0
        term_factor = jnp.concatenate(
            [jnp.where(first, mine, other), jnp.where(first, other, mine)], axis=0
        )
    return (doc_factor, term_factor)


def solution(mesh):
    parts = Mesh(mesh.devices.reshape(4, 2, 4, 4, 2), ("y", "core", "x", "zh", "zl"))
    return jax.shard_map(
        on_device,
        mesh=parts,
        in_specs=(P(DOC, TERM), P(DOC, None), P(TERM, None)),
        out_specs=(P(DOC, None), P(TERM, None)),
        check_vma=False,
    )
```

time: 257 us -> 216 us (0.84)
  blocking collectives: 158 us -> 92.1 us
  matrix products: 38 us -> 0 us
  starting transfers between devices: 27.8 us -> 57.9 us
  waiting for transfers between devices: 19.7 us -> 41.7 us
  Pallas kernels: 0 us -> 16.8 us
  local copies, waits for them, and re-layouts: 8.78 us -> 4.08 us
    all_to_all x13 -> x8, blocking collectives: 158 us -> 92.1 us  [exchange(): return lax.all_to_all(blocks, axis, split_axis=0, concat_axis=0, tiled=True)]
    ppermute x0 -> x28, starting transfers between devices: none -> 57.9 us  [swap(): lax.ppermute(value, axis, [(at, at ^ by) for at in range(lax.axis_size(ax...]
    ppermute x0 -> x28, waiting for transfers between devices: none -> 41.7 us  [swap(): lax.ppermute(value, axis, [(at, at ^ by) for at in range(lax.axis_size(ax...]
    dot_general x12 -> x0, matrix products: 38 us -> none  [dot(): lax.dot_general(a, b, (dims, ((), ())), precision=lax.Precision.HIGH, pre...]
    all_to_all x3 -> x0, starting transfers between devices: 27.8 us -> none  [exchange(): return lax.all_to_all(blocks, axis, split_axis=0, concat_axis=0, tiled=True)]
    all_to_all x3 -> x0, waiting for transfers between devices: 19.7 us -> none  [exchange(): return lax.all_to_all(blocks, axis, split_axis=0, concat_axis=0, tiled=True)]
    pallas_call x0 -> x6, Pallas kernels: none -> 16.8 us  [call(): pl.pallas_call(functools.partial(first_kernel, kernel, mass) if first els...]
    unnamed x7, local copies, waits for them, and re-layouts: 6.96 us -> 2.87 us
  transfers between devices with their start and end apart: 3 -> 28, of which waited for: 3 -> 19; matrix products, arithmetic and copies ran while one was open for 2% -> 0% of each run, Pallas kernels for 0% -> 0%
where the time goes in v2:
time: 216 us
  blocking collectives  92.1 us (43%)
  starting transfers between devices  57.9 us (27%)
  waiting for transfers between devices  41.7 us (19%)
  Pallas kernels  16.8 us (8%)
  local copies, waits for them, and re-layouts  4.08 us (2%)
  other arithmetic  2.34 us (1%)
    all_to_all x8, blocking collectives, exchange(): return lax.all_to_all(blocks, axis, split_axis=0, concat_axis=0, tiled=True)  92.1 us
    ppermute x28, starting transfers between devices, swap(): lax.ppermute(value, axis, [(at, at ^ by) for at in range(lax.axis_size(ax...  57.9 us
    ppermute x28, waiting for transfers between devices, swap(): lax.ppermute(value, axis, [(at, at ^ by) for at in range(lax.axis_size(ax...  41.7 us
    pallas_call x6, Pallas kernels, call(): pl.pallas_call(functools.partial(first_kernel, kernel, mass) if first els...  16.8 us
  transfers between devices with their start and end apart: 28, of which 19 were waited for; matrix products, arithmetic and copies ran while one was open for 0% of the time, Pallas kernels for 0%

profile of v2, /device:TPU:1, one launch (start us, length us, event | category | flops | bytes accessed | tf_op | source)
XLA Modules:
  0.0 215.8 jit_solution(1722160960568701098)
XLA Ops:
  3.6 3.2 %shard_map.50 = (f32[8,136,128]{2,1,0:T(8,128)S(1)}, f32[512,1024]{1,0:T(8,128)S(1)}) custom-call(f32[1024,1024]{1,0:T(8,128)} %slab_ref.5, f32[1024,128]{1,0:T(8,128)S(1)} %copy-done.2, f32[1024,128]{1,0:T(8,128)S(1)} %copy-done), custom_call_target="tpu_custom_call" | custom-call | tf_op jit(solution)/shard_map/pallas_call | solution.py:141
  6.8 15.4 %all_to_all.40 = f32[8,136,128]{2,1,0:T(8,128)S(1)} all-to-all(f32[8,136,128]{2,1,0:T(8,128)S(1)} %get-tuple-element.20), channel_id=1, replica_groups=mesh['y'=4,'core'=2,'x'=4,'zh'=4,'zl'=2] {'x','zl'}, dimensions={0} | all-to-all | bytes 1114112 | tf_op jit(solution)/shard_map/all_to_all | solution.py:25
  22.2 5.2 %collective-permute-start.2 = (f32[136,128]{1,0:T(8,128)S(1)}, f32[136,128]{1,0:T(8,128)S(1)}, u32[]{:S(2)}, u32[]{:S(2)}) collective-permute-start(f32[136,128]{1,0:T(8,128)S(1)} %reduce_sum.36), channel_id=1, source_target_pairs={{0,6},{2,4},{4,2},{6,0},{1,7},{3,5},{5,3},{7,1},{8,14},{10,12},{12... | collective-permute-start | bytes 208904 | tf_op jit(solution)/shard_map/ppermute | solution.py:33
  27.4 1.2 collective-permute-start.1
  29.6 6.2 %collective-permute-done.1 = f32[136,128]{1,0:T(8,128)S(1)} collective-permute-done((f32[136,128]{1,0:T(8,128)S(1)}, f32[136,128]{1,0:T(8,128)S(1)}, u32[]{:S(2)}, u32[]{:S(2)}) %collective-permute-start.1) | collective-permute-done | bytes 69664 | tf_op jit(solution)/shard_map/ppermute | solution.py:33
  35.9 10.0 %all_to_all.41 = f32[8,128,128]{2,1,0:T(8,128)S(1)} all-to-all(f32[8,128,128]{2,1,0:T(8,128)S(1)} %broadcast_in_dim.12), channel_id=1, replica_groups=mesh['y'=4,'core'=2,'x'=4,'zh'=4,'zl'=2] {'x','zl'}, dimensions={0} | all-to-all | bytes 1048576 | tf_op jit(solution)/shard_map/all_to_all | solution.py:25
  45.9 2.6 %shard_map.51 = f32[8,128,128]{2,1,0:T(8,128)S(1)} custom-call(f32[1024,1024]{1,0:T(8,128)} %slab_ref.5, f32[512,1024]{1,0:T(8,128)S(1)} %get-tuple-element.21.near_ref, f32[1024,128]{1,0:T(8,128)S(1)} %bitcast.64, f32[1024,128]{1,0:T(8,128)S(1)} %copy-done.1), custom_call_target="tpu_custom_call" | custom-call | tf_op jit(solution)/shard_map/pallas_call | solution.py:141
  48.5 10.1 %all_to_all.42 = f32[8,128,128]{2,1,0:T(8,128)S(1)} all-to-all(f32[8,128,128]{2,1,0:T(8,128)S(1)} %shard_map.51), channel_id=1, replica_groups=mesh['y'=4,'core'=2,'x'=4,'zh'=4,'zl'=2] {'x','zl'}, dimensions={0} | all-to-all | bytes 1048576 | tf_op jit(solution)/shard_map/all_to_all | solution.py:25
  58.6 5.3 %collective-permute-start.5 = (f32[128,128]{1,0:T(8,128)S(1)}, f32[128,128]{1,0:T(8,128)S(1)}, u32[]{:S(2)}, u32[]{:S(2)}) collective-permute-start(f32[128,128]{1,0:T(8,128)S(1)} %reduce_sum.37), channel_id=1, source_target_pairs={{0,6},{2,4},{4,2},{6,0},{1,7},{3,5},{5,3},{7,1},{8,14},{10,12},{12... | collective-permute-start | bytes 196616 | tf_op jit(solution)/shard_map/ppermute | solution.py:33
  63.9 2.2 %collective-permute-start.3 = (f32[128,128]{1,0:T(8,128)S(1)}, f32[128,128]{1,0:T(8,128)S(1)}, u32[]{:S(2)}, u32[]{:S(2)}) collective-permute-start(f32[128,128]{1,0:T(8,128)S(1)} %reduce_sum.37), channel_id=1, source_target_pairs={{0,2},{2,0},{4,6},{6,4},{1,3},{3,1},{5,7},{7,5},{8,10},{10,8},{12,... | collective-permute-start | bytes 196616 | tf_op jit(solution)/shard_map/ppermute | solution.py:33
  66.5 5.8 %collective-permute-done.4 = f32[128,128]{1,0:T(8,128)S(1)} collective-permute-done((f32[128,128]{1,0:T(8,128)S(1)}, f32[128,128]{1,0:T(8,128)S(1)}, u32[]{:S(2)}, u32[]{:S(2)}) %collective-permute-start.4) | collective-permute-done | bytes 65568 | tf_op jit(solution)/shard_map/ppermute | solution.py:33
  72.4 10.0 %all_to_all.43 = f32[8,128,128]{2,1,0:T(8,128)S(1)} all-to-all(f32[8,128,128]{2,1,0:T(8,128)S(1)} %broadcast_in_dim.13), channel_id=1, replica_groups=mesh['y'=4,'core'=2,'x'=4,'zh'=4,'zl'=2] {'x','zl'}, dimensions={0} | all-to-all | bytes 1048576 | tf_op jit(solution)/shard_map/all_to_all | solution.py:25
  82.3 2.9 %shard_map.52 = f32[8,136,128]{2,1,0:T(8,128)S(1)} custom-call(f32[1024,1024]{1,0:T(8,128)} %slab_ref.5, f32[512,1024]{1,0:T(8,128)S(1)} %get-tuple-element.21.near_ref, f32[1024,128]{1,0:T(8,128)S(1)} %bitcast.62, f32[1024,128]{1,0:T(8,128)S(1)} %copy-done.1), custom_call_target="tpu_custom_call" | custom-call | tf_op jit(solution)/shard_map/pallas_call | solution.py:141
  85.3 5.5 %collective-permute-start.6 = (f32[4,136,128]{2,1,0:T(8,128)S(1)}, f32[4,136,128]{2,1,0:T(8,128)S(1)}, u32[]{:S(2)}, u32[]{:S(2)}) collective-permute-start(f32[4,136,128]{2,1,0:T(8,128)S(1)} %constant_dynamic-slice_fusion.1), channel_id=1, source_target_pairs={{0,32},{32,0},{1,33},{33,1},{2,34},{34,2},{3,35},{35,3},{4,36},{36... | collective-permute-start | bytes 835592 | tf_op jit(solution)/shard_map/ppermute | solution.py:33
  90.8 1.2 collective-permute-done.6
  92.1 1.6 collective-permute-start.7
  93.7 1.9 collective-permute-start.9
  96.3 1.7 collective-permute-done.9
  98.0 2.2 %collective-permute-done.8 = f32[136,128]{1,0:T(8,128)S(1)} collective-permute-done((f32[136,128]{1,0:T(8,128)S(1)}, f32[136,128]{1,0:T(8,128)S(1)}, u32[]{:S(2)}, u32[]{:S(2)}) %collective-permute-start.8) | collective-permute-done | bytes 69664 | tf_op jit(solution)/shard_map/ppermute | solution.py:33
  101.2 1.3 collective-permute-start.11
  104.7 1.1 collective-permute-done.11
  106.1 3.6 %collective-permute-start.13 = (f32[512,128]{1,0:T(8,128)S(1)}, f32[512,128]{1,0:T(8,128)}, u32[]{:S(2)}, u32[]{:S(2)}) collective-permute-start(f32[512,128]{1,0:T(8,128)S(1)} %pad_maximum_fusion.3), channel_id=1, source_target_pairs={{0,32},{32,0},{1,33},{33,1},{2,34},{34,2},{3,35},{35,3},{4,36},{36... | collective-permute-start | bytes 786440 | tf_op jit(solution)/shard_map/ppermute | solution.py:33
  109.7 1.3 collective-permute-done.13
  112.0 2.6 %shard_map.53 = f32[8,136,128]{2,1,0:T(8,128)S(1)} custom-call(f32[1024,1024]{1,0:T(8,128)} %slab_ref.5, f32[512,1024]{1,0:T(8,128)S(1)} %get-tuple-element.21.near_ref, f32[1024,128]{1,0:T(8,128)S(1)} %bitcast.63, f32[1024,128]{1,0:T(8,128)S(1)} %pad_maximum_fusion.term_ref), custom_call_target="tpu_custom_call" | custom-call | tf_op jit(solution)/shard_map/pallas_call | solution.py:141
  114.6 12.5 %all_to_all.44 = f32[8,136,128]{2,1,0:T(8,128)S(1)} all-to-all(f32[8,136,128]{2,1,0:T(8,128)S(1)} %shard_map.53), channel_id=1, replica_groups=mesh['y'=4,'core'=2,'x'=4,'zh'=4,'zl'=2] {'x','zl'}, dimensions={0} | all-to-all | bytes 1114112 | tf_op jit(solution)/shard_map/all_to_all | solution.py:25
  127.2 2.0 collective-permute-start.16
  129.2 2.3 %collective-permute-start.15 = (f32[136,128]{1,0:T(8,128)S(1)}, f32[136,128]{1,0:T(8,128)S(1)}, u32[]{:S(2)}, u32[]{:S(2)}) collective-permute-start(f32[136,128]{1,0:T(8,128)S(1)} %reduce_sum.38), channel_id=1, source_target_pairs={{0,4},{2,6},{4,0},{6,2},{1,5},{3,7},{5,1},{7,3},{8,12},{10,14},{12... | collective-permute-start | bytes 208904 | tf_op jit(solution)/shard_map/ppermute | solution.py:33
  131.5 1.4 collective-permute-start.14
  132.9 4.4 %collective-permute-done.15 = f32[136,128]{1,0:T(8,128)S(1)} collective-permute-done((f32[136,128]{1,0:T(8,128)S(1)}, f32[136,128]{1,0:T(8,128)S(1)}, u32[]{:S(2)}, u32[]{:S(2)}) %collective-permute-start.15) | collective-permute-done | bytes 69664 | tf_op jit(solution)/shard_map/ppermute | solution.py:33
  137.3 2.6 %collective-permute-done.14 = f32[136,128]{1,0:T(8,128)S(1)} collective-permute-done((f32[136,128]{1,0:T(8,128)S(1)}, f32[136,128]{1,0:T(8,128)S(1)}, u32[]{:S(2)}, u32[]{:S(2)}) %collective-permute-start.14) | collective-permute-done | bytes 69664 | tf_op jit(solution)/shard_map/ppermute | solution.py:33
  139.9 11.4 %all_to_all.45 = f32[8,128,128]{2,1,0:T(8,128)S(1)} all-to-all(f32[8,128,128]{2,1,0:T(8,128)S(1)} %broadcast_in_dim.14), channel_id=1, replica_groups=mesh['y'=4,'core'=2,'x'=4,'zh'=4,'zl'=2] {'x','zl'}, dimensions={0} | all-to-all | bytes 1048576 | tf_op jit(solution)/shard_map/all_to_all | solution.py:25
  151.3 2.6 %shard_map.54 = f32[8,128,128]{2,1,0:T(8,128)S(1)} custom-call(f32[1024,1024]{1,0:T(8,128)} %slab_ref.5, f32[512,1024]{1,0:T(8,128)S(1)} %get-tuple-element.21.near_ref, f32[1024,128]{1,0:T(8,128)S(1)} %bitcast.65, f32[1024,128]{1,0:T(8,128)S(1)} %pad_maximum_fusion.term_ref), custom_call_target="tpu_custom_call" | custom-call | tf_op jit(solution)/shard_map/pallas_call | solution.py:141
  153.9 11.4 %all_to_all.46 = f32[8,128,128]{2,1,0:T(8,128)S(1)} all-to-all(f32[8,128,128]{2,1,0:T(8,128)S(1)} %shard_map.54), channel_id=1, replica_groups=mesh['y'=4,'core'=2,'x'=4,'zh'=4,'zl'=2] {'x','zl'}, dimensions={0} | all-to-all | bytes 1048576 | tf_op jit(solution)/shard_map/all_to_all | solution.py:25
  165.4 2.9 %collective-permute-start.19 = (f32[128,128]{1,0:T(8,128)S(1)}, f32[128,128]{1,0:T(8,128)S(1)}, u32[]{:S(2)}, u32[]{:S(2)}) collective-permute-start(f32[128,128]{1,0:T(8,128)S(1)} %reduce_sum.39), channel_id=1, source_target_pairs={{0,6},{2,4},{4,2},{6,0},{1,7},{3,5},{5,3},{7,1},{8,14},{10,12},{12... | collective-permute-start | bytes 196616 | tf_op jit(solution)/shard_map/ppermute | solution.py:33
  168.3 2.4 %collective-permute-start.18 = (f32[128,128]{1,0:T(8,128)S(1)}, f32[128,128]{1,0:T(8,128)S(1)}, u32[]{:S(2)}, u32[]{:S(2)}) collective-permute-start(f32[128,128]{1,0:T(8,128)S(1)} %reduce_sum.39), channel_id=1, source_target_pairs={{0,4},{2,6},{4,0},{6,2},{1,5},{3,7},{5,1},{7,3},{8,12},{10,14},{12... | collective-permute-start | bytes 196616 | tf_op jit(solution)/shard_map/ppermute | solution.py:33
  171.1 5.0 %collective-permute-done.18 = f32[128,128]{1,0:T(8,128)S(1)} collective-permute-done((f32[128,128]{1,0:T(8,128)S(1)}, f32[128,128]{1,0:T(8,128)S(1)}, u32[]{:S(2)}, u32[]{:S(2)}) %collective-permute-start.18) | collective-permute-done | bytes 65568 | tf_op jit(solution)/shard_map/ppermute | solution.py:33
  176.2 11.3 %all_to_all.47 = f32[8,128,128]{2,1,0:T(8,128)S(1)} all-to-all(f32[8,128,128]{2,1,0:T(8,128)S(1)} %broadcast_in_dim.15), channel_id=1, replica_groups=mesh['y'=4,'core'=2,'x'=4,'zh'=4,'zl'=2] {'x','zl'}, dimensions={0} | all-to-all | bytes 1048576 | tf_op jit(solution)/shard_map/all_to_all | solution.py:25
  187.5 2.9 %shard_map.55 = f32[8,136,128]{2,1,0:T(8,128)S(1)} custom-call(f32[1024,1024]{1,0:T(8,128)} %slab_ref.5, f32[512,1024]{1,0:T(8,128)S(1)} %get-tuple-element.21.near_ref, f32[1024,128]{1,0:T(8,128)S(1)} %bitcast.60, f32[1024,128]{1,0:T(8,128)S(1)} %pad_maximum_fusion.term_ref), custom_call_target="tpu_custom_call" | custom-call | tf_op jit(solution)/shard_map/pallas_call | solution.py:141
  190.5 4.6 %collective-permute-start.20 = (f32[4,136,128]{2,1,0:T(8,128)S(1)}, f32[4,136,128]{2,1,0:T(8,128)S(1)}, u32[]{:S(2)}, u32[]{:S(2)}) collective-permute-start(f32[4,136,128]{2,1,0:T(8,128)S(1)} %constant_dynamic-slice_fusion), channel_id=1, source_target_pairs={{0,32},{32,0},{1,33},{33,1},{2,34},{34,2},{3,35},{35,3},{4,36},{36... | collective-permute-start | bytes 835592 | tf_op jit(solution)/shard_map/ppermute | solution.py:33
  195.1 1.2 collective-permute-done.20
  198.4 1.3 collective-permute-start.22
  199.7 1.9 collective-permute-done.23
  201.6 1.5 collective-permute-done.22
  203.2 1.6 collective-permute-start.26
  205.3 1.2 collective-permute-start.24
  207.6 1.8 collective-permute-done.25
  209.4 3.6 %collective-permute-start.27 = (f32[512,128]{1,0:T(8,128)S(1)}, f32[512,128]{1,0:T(8,128)S(1)}, u32[]{:S(2)}, u32[]{:S(2)}) collective-permute-start(f32[512,128]{1,0:T(8,128)S(1)} %pad_maximum_fusion.5), channel_id=1, source_target_pairs={{0,32},{32,0},{1,33},{33,1},{2,34},{34,2},{3,35},{35,3},{4,36},{36... | collective-permute-start | bytes 786440 | tf_op jit(solution)/shard_map/ppermute | solution.py:33
  213.0 1.2 collective-permute-done.27
  (68 shorter events, 15.9 us)
Async XLA Ops:
  1.5 1.0 copy-start
  2.6 1.0 copy-start.2
  3.6 42.2 %copy-start.1 = (f32[1024,128]{1,0:T(8,128)S(1)}, f32[1024,128]{1,0:T(8,128)}, u32[]{:S(2)}) copy-start(f32[1024,128]{1,0:T(8,128)} %term_ref.2) | copy-start | bytes 1572868
  22.2 7.4 %collective-permute-start.2 = (f32[136,128]{1,0:T(8,128)S(1)}, f32[136,128]{1,0:T(8,128)S(1)}, u32[]{:S(2)}, u32[]{:S(2)}) collective-permute-start(f32[136,128]{1,0:T(8,128)S(1)} %reduce_sum.36), channel_id=1, source_target_pairs={{0,6},{2,4},{4,2},{6,0},{1,7},{3,5},{5,3},{7,1},{8,14},{10,12},{12... | collective-permute-start | bytes 208904 | tf_op jit(solution)/shard_map/ppermute | solution.py:33
  27.4 8.4 %collective-permute-start.1 = (f32[136,128]{1,0:T(8,128)S(1)}, f32[136,128]{1,0:T(8,128)S(1)}, u32[]{:S(2)}, u32[]{:S(2)}) collective-permute-start(f32[136,128]{1,0:T(8,128)S(1)} %reduce_sum.36), channel_id=1, source_target_pairs={{0,4},{2,6},{4,0},{6,2},{1,5},{3,7},{5,1},{7,3},{8,12},{10,14},{12... | collective-permute-start | bytes 208904 | tf_op jit(solution)/shard_map/ppermute | solution.py:33
  28.6 7.2 %collective-permute-start = (f32[136,128]{1,0:T(8,128)S(1)}, f32[136,128]{1,0:T(8,128)S(1)}, u32[]{:S(2)}, u32[]{:S(2)}) collective-permute-start(f32[136,128]{1,0:T(8,128)S(1)} %reduce_sum.36), channel_id=1, source_target_pairs={{0,2},{2,0},{4,6},{6,4},{1,3},{3,1},{5,7},{7,5},{8,10},{10,8},{12,... | collective-permute-start | bytes 208904 | tf_op jit(solution)/shard_map/ppermute | solution.py:33
  58.6 7.9 %collective-permute-start.5 = (f32[128,128]{1,0:T(8,128)S(1)}, f32[128,128]{1,0:T(8,128)S(1)}, u32[]{:S(2)}, u32[]{:S(2)}) collective-permute-start(f32[128,128]{1,0:T(8,128)S(1)} %reduce_sum.37), channel_id=1, source_target_pairs={{0,6},{2,4},{4,2},{6,0},{1,7},{3,5},{5,3},{7,1},{8,14},{10,12},{12... | collective-permute-start | bytes 196616 | tf_op jit(solution)/shard_map/ppermute | solution.py:33
  63.9 8.4 %collective-permute-start.4 = (f32[128,128]{1,0:T(8,128)S(1)}, f32[128,128]{1,0:T(8,128)S(1)}, u32[]{:S(2)}, u32[]{:S(2)}) collective-permute-start(f32[128,128]{1,0:T(8,128)S(1)} %reduce_sum.37), channel_id=1, source_target_pairs={{0,4},{2,6},{4,0},{6,2},{1,5},{3,7},{5,1},{7,3},{8,12},{10,14},{12... | collective-permute-start | bytes 196616 | tf_op jit(solution)/shard_map/ppermute | solution.py:33
  63.9 8.4 %collective-permute-start.3 = (f32[128,128]{1,0:T(8,128)S(1)}, f32[128,128]{1,0:T(8,128)S(1)}, u32[]{:S(2)}, u32[]{:S(2)}) collective-permute-start(f32[128,128]{1,0:T(8,128)S(1)} %reduce_sum.37), channel_id=1, source_target_pairs={{0,2},{2,0},{4,6},{6,4},{1,3},{3,1},{5,7},{7,5},{8,10},{10,8},{12,... | collective-permute-start | bytes 196616 | tf_op jit(solution)/shard_map/ppermute | solution.py:33
  85.3 6.7 %collective-permute-start.6 = (f32[4,136,128]{2,1,0:T(8,128)S(1)}, f32[4,136,128]{2,1,0:T(8,128)S(1)}, u32[]{:S(2)}, u32[]{:S(2)}) collective-permute-start(f32[4,136,128]{2,1,0:T(8,128)S(1)} %constant_dynamic-slice_fusion.1), channel_id=1, source_target_pairs={{0,32},{32,0},{1,33},{33,1},{2,34},{34,2},{3,35},{35,3},{4,36},{36... | collective-permute-start | bytes 835592 | tf_op jit(solution)/shard_map/ppermute | solution.py:33
  92.1 4.2 %collective-permute-start.7 = (f32[136,128]{1,0:T(8,128)S(1)}, f32[136,128]{1,0:T(8,128)S(1)}, u32[]{:S(2)}, u32[]{:S(2)}) collective-permute-start(f32[136,128]{1,0:T(8,128)S(1)} %get-tuple-element.37), channel_id=1, source_target_pairs={{0,64},{64,0},{128,192},{192,128},{1,65},{65,1},{129,193},{193,129... | collective-permute-start | bytes 208904 | tf_op jit(solution)/shard_map/ppermute | solution.py:33
  93.7 4.4 %collective-permute-start.9 = (f32[136,128]{1,0:T(8,128)S(1)}, f32[136,128]{1,0:T(8,128)S(1)}, u32[]{:S(2)}, u32[]{:S(2)}) collective-permute-start(f32[136,128]{1,0:T(8,128)S(1)} %get-tuple-element.38), channel_id=1, source_target_pairs={{0,192},{64,128},{128,64},{192,0},{1,193},{65,129},{129,65},{193,1... | collective-permute-start | bytes 208904 | tf_op jit(solution)/shard_map/ppermute | solution.py:33
  95.6 4.7 %collective-permute-start.8 = (f32[136,128]{1,0:T(8,128)S(1)}, f32[136,128]{1,0:T(8,128)S(1)}, u32[]{:S(2)}, u32[]{:S(2)}) collective-permute-start(f32[136,128]{1,0:T(8,128)S(1)} %get-tuple-element.39), channel_id=1, source_target_pairs={{0,128},{64,192},{128,0},{192,64},{1,129},{65,193},{129,1},{193,65... | collective-permute-start | bytes 208904 | tf_op jit(solution)/shard_map/ppermute | solution.py:33
  100.3 4.4 %collective-permute-start.12 = (f32[128,128]{1,0:T(8,128)S(1)}, f32[128,128]{1,0:T(8,128)S(1)}, u32[]{:S(2)}, u32[]{:S(2)}) collective-permute-start(f32[128,128]{1,0:T(8,128)S(1)} %fusion.6), channel_id=1, source_target_pairs={{0,192},{64,128},{128,64},{192,0},{1,193},{65,129},{129,65},{193,1... | collective-permute-start | bytes 196616 | tf_op jit(solution)/shard_map/ppermute | solution.py:33
  101.2 4.6 %collective-permute-start.11 = (f32[128,128]{1,0:T(8,128)S(1)}, f32[128,128]{1,0:T(8,128)S(1)}, u32[]{:S(2)}, u32[]{:S(2)}) collective-permute-start(f32[128,128]{1,0:T(8,128)S(1)} %fusion.6), channel_id=1, source_target_pairs={{0,128},{64,192},{128,0},{192,64},{1,129},{65,193},{129,1},{193,65... | collective-permute-start | bytes 196616 | tf_op jit(solution)/shard_map/ppermute | solution.py:33
  102.5 3.4 %collective-permute-start.10 = (f32[128,128]{1,0:T(8,128)S(1)}, f32[128,128]{1,0:T(8,128)S(1)}, u32[]{:S(2)}, u32[]{:S(2)}) collective-permute-start(f32[128,128]{1,0:T(8,128)S(1)} %fusion.6), channel_id=1, source_target_pairs={{0,64},{64,0},{128,192},{192,128},{1,65},{65,1},{129,193},{193,129... | collective-permute-start | bytes 196616 | tf_op jit(solution)/shard_map/ppermute | solution.py:33
  106.1 4.9 %collective-permute-start.13 = (f32[512,128]{1,0:T(8,128)S(1)}, f32[512,128]{1,0:T(8,128)}, u32[]{:S(2)}, u32[]{:S(2)}) collective-permute-start(f32[512,128]{1,0:T(8,128)S(1)} %pad_maximum_fusion.3), channel_id=1, source_target_pairs={{0,32},{32,0},{1,33},{33,1},{2,34},{34,2},{3,35},{35,3},{4,36},{36... | collective-permute-start | bytes 786440 | tf_op jit(solution)/shard_map/ppermute | solution.py:33
  127.2 5.7 %collective-permute-start.16 = (f32[136,128]{1,0:T(8,128)S(1)}, f32[136,128]{1,0:T(8,128)S(1)}, u32[]{:S(2)}, u32[]{:S(2)}) collective-permute-start(f32[136,128]{1,0:T(8,128)S(1)} %reduce_sum.38), channel_id=1, source_target_pairs={{0,6},{2,4},{4,2},{6,0},{1,7},{3,5},{5,3},{7,1},{8,14},{10,12},{12... | collective-permute-start | bytes 208904 | tf_op jit(solution)/shard_map/ppermute | solution.py:33
  129.2 8.1 %collective-permute-start.15 = (f32[136,128]{1,0:T(8,128)S(1)}, f32[136,128]{1,0:T(8,128)S(1)}, u32[]{:S(2)}, u32[]{:S(2)}) collective-permute-start(f32[136,128]{1,0:T(8,128)S(1)} %reduce_sum.38), channel_id=1, source_target_pairs={{0,4},{2,6},{4,0},{6,2},{1,5},{3,7},{5,1},{7,3},{8,12},{10,14},{12... | collective-permute-start | bytes 208904 | tf_op jit(solution)/shard_map/ppermute | solution.py:33
  131.5 8.3 %collective-permute-start.14 = (f32[136,128]{1,0:T(8,128)S(1)}, f32[136,128]{1,0:T(8,128)S(1)}, u32[]{:S(2)}, u32[]{:S(2)}) collective-permute-start(f32[136,128]{1,0:T(8,128)S(1)} %reduce_sum.38), channel_id=1, source_target_pairs={{0,2},{2,0},{4,6},{6,4},{1,3},{3,1},{5,7},{7,5},{8,10},{10,8},{12,... | collective-permute-start | bytes 208904 | tf_op jit(solution)/shard_map/ppermute | solution.py:33
  165.4 5.7 %collective-permute-start.19 = (f32[128,128]{1,0:T(8,128)S(1)}, f32[128,128]{1,0:T(8,128)S(1)}, u32[]{:S(2)}, u32[]{:S(2)}) collective-permute-start(f32[128,128]{1,0:T(8,128)S(1)} %reduce_sum.39), channel_id=1, source_target_pairs={{0,6},{2,4},{4,2},{6,0},{1,7},{3,5},{5,3},{7,1},{8,14},{10,12},{12... | collective-permute-start | bytes 196616 | tf_op jit(solution)/shard_map/ppermute | solution.py:33
  168.3 7.8 %collective-permute-start.18 = (f32[128,128]{1,0:T(8,128)S(1)}, f32[128,128]{1,0:T(8,128)S(1)}, u32[]{:S(2)}, u32[]{:S(2)}) collective-permute-start(f32[128,128]{1,0:T(8,128)S(1)} %reduce_sum.39), channel_id=1, source_target_pairs={{0,4},{2,6},{4,0},{6,2},{1,5},{3,7},{5,1},{7,3},{8,12},{10,14},{12... | collective-permute-start | bytes 196616 | tf_op jit(solution)/shard_map/ppermute | solution.py:33
  170.7 5.4 %collective-permute-start.17 = (f32[128,128]{1,0:T(8,128)S(1)}, f32[128,128]{1,0:T(8,128)S(1)}, u32[]{:S(2)}, u32[]{:S(2)}) collective-permute-start(f32[128,128]{1,0:T(8,128)S(1)} %reduce_sum.39), channel_id=1, source_target_pairs={{0,2},{2,0},{4,6},{6,4},{1,3},{3,1},{5,7},{7,5},{8,10},{10,8},{12,... | collective-permute-start | bytes 196616 | tf_op jit(solution)/shard_map/ppermute | solution.py:33
  190.5 5.8 %collective-permute-start.20 = (f32[4,136,128]{2,1,0:T(8,128)S(1)}, f32[4,136,128]{2,1,0:T(8,128)S(1)}, u32[]{:S(2)}, u32[]{:S(2)}) collective-permute-start(f32[4,136,128]{2,1,0:T(8,128)S(1)} %constant_dynamic-slice_fusion), channel_id=1, source_target_pairs={{0,32},{32,0},{1,33},{33,1},{2,34},{34,2},{3,35},{35,3},{4,36},{36... | collective-permute-start | bytes 835592 | tf_op jit(solution)/shard_map/ppermute | solution.py:33
  196.3 3.3 %collective-permute-start.21 = (f32[136,128]{1,0:T(8,128)S(1)}, f32[136,128]{1,0:T(8,128)S(1)}, u32[]{:S(2)}, u32[]{:S(2)}) collective-permute-start(f32[136,128]{1,0:T(8,128)S(1)} %get-tuple-element.34), channel_id=1, source_target_pairs={{0,64},{64,0},{128,192},{192,128},{1,65},{65,1},{129,193},{193,129... | collective-permute-start | bytes 208904 | tf_op jit(solution)/shard_map/ppermute | solution.py:33
  197.2 4.4 %collective-permute-start.23 = (f32[136,128]{1,0:T(8,128)S(1)}, f32[136,128]{1,0:T(8,128)S(1)}, u32[]{:S(2)}, u32[]{:S(2)}) collective-permute-start(f32[136,128]{1,0:T(8,128)S(1)} %get-tuple-element.35), channel_id=1, source_target_pairs={{0,192},{64,128},{128,64},{192,0},{1,193},{65,129},{129,65},{193,1... | collective-permute-start | bytes 208904 | tf_op jit(solution)/shard_map/ppermute | solution.py:33
  198.4 4.8 %collective-permute-start.22 = (f32[136,128]{1,0:T(8,128)S(1)}, f32[136,128]{1,0:T(8,128)S(1)}, u32[]{:S(2)}, u32[]{:S(2)}) collective-permute-start(f32[136,128]{1,0:T(8,128)S(1)} %get-tuple-element.36), channel_id=1, source_target_pairs={{0,128},{64,192},{128,0},{192,64},{1,129},{65,193},{129,1},{193,65... | collective-permute-start | bytes 208904 | tf_op jit(solution)/shard_map/ppermute | solution.py:33
  203.2 4.4 %collective-permute-start.26 = (f32[128,128]{1,0:T(8,128)S(1)}, f32[128,128]{1,0:T(8,128)S(1)}, u32[]{:S(2)}, u32[]{:S(2)}) collective-permute-start(f32[128,128]{1,0:T(8,128)S(1)} %fusion.4), channel_id=1, source_target_pairs={{0,192},{64,128},{128,64},{192,0},{1,193},{65,129},{129,65},{193,1... | collective-permute-start | bytes 196616 | tf_op jit(solution)/shard_map/ppermute | solution.py:33
  204.7 4.6 %collective-permute-start.25 = (f32[128,128]{1,0:T(8,128)S(1)}, f32[128,128]{1,0:T(8,128)S(1)}, u32[]{:S(2)}, u32[]{:S(2)}) collective-permute-start(f32[128,128]{1,0:T(8,128)S(1)} %fusion.4), channel_id=1, source_target_pairs={{0,128},{64,192},{128,0},{192,64},{1,129},{65,193},{129,1},{193,65... | collective-permute-start | bytes 196616 | tf_op jit(solution)/shard_map/ppermute | solution.py:33
  205.3 4.0 %collective-permute-start.24 = (f32[128,128]{1,0:T(8,128)S(1)}, f32[128,128]{1,0:T(8,128)S(1)}, u32[]{:S(2)}, u32[]{:S(2)}) collective-permute-start(f32[128,128]{1,0:T(8,128)S(1)} %fusion.4), channel_id=1, source_target_pairs={{0,64},{64,0},{128,192},{192,128},{1,65},{65,1},{129,193},{193,129... | collective-permute-start | bytes 196616 | tf_op jit(solution)/shard_map/ppermute | solution.py:33
  209.4 4.7 %collective-permute-start.27 = (f32[512,128]{1,0:T(8,128)S(1)}, f32[512,128]{1,0:T(8,128)S(1)}, u32[]{:S(2)}, u32[]{:S(2)}) collective-permute-start(f32[512,128]{1,0:T(8,128)S(1)} %pad_maximum_fusion.5), channel_id=1, source_target_pairs={{0,32},{32,0},{1,33},{33,1},{2,34},{34,2},{3,35},{35,3},{4,36},{36... | collective-permute-start | bytes 786440 | tf_op jit(solution)/shard_map/ppermute | solution.py:33

commit v3 on v2

v3 whole, which is shorter than its diff:
```python
import functools

import jax
import jax.numpy as jnp
from jax import lax
from jax.experimental import pallas as pl
from jax.experimental.pallas import tpu as pltpu
from jax.sharding import Mesh, PartitionSpec as P

OUTER = 2
INNER = 2
NEAR = ("x", "zl")
FAR = "zh"
DOC = ("y", "core")
TERM = ("x", "zh", "zl")
TERM_OWN = ("core", "y")
F32 = jnp.float32
PAD = 8
ORDER = (1, 3, 2)
HELD = 512
DOC_STEP = 256
TERM_STEP = 512
LIMIT = 50


def exchange(blocks, axis):
    return lax.all_to_all(blocks, axis, split_axis=0, concat_axis=0, tiled=True)


def spread(value, axis):
    return exchange(jnp.broadcast_to(value, (lax.axis_size(axis), *value.shape)), axis)


def swap(value, axis, by=1):
    return lax.ppermute(value, axis, [(at, at ^ by) for at in range(lax.axis_size(axis))])


def total_over(value, axis):
    return sum([swap(value, axis, by) for by in ORDER], value)


def halves(value):
    high = value.astype(jnp.bfloat16)
    return high, (value - high.astype(F32)).astype(jnp.bfloat16)


def product_of(doc, term_cat):
    high, low = doc
    return lax.dot_general(
        jnp.concatenate([high, low, high, low], axis=1),
        term_cat,
        (((1,), (1,)), ((), ())),
        preferred_element_type=F32,
    )


def term_operand(term):
    high, low = term
    return jnp.concatenate([high, high, low, low], axis=1)


def quotients(first, slab_ref, near_ref, docs, term_cat, held, arrived):
    split, step = near_ref.shape[0], docs[0][0].shape[0]
    if first:
        head = pltpu.make_async_copy(slab_ref.at[pl.ds(0, split)], near_ref, arrived.at[0])
        head.start()
    tail = pltpu.make_async_copy(
        slab_ref.at[pl.ds(split, held.shape[0])], held, arrived.at[1]
    )
    tail.start()
    products = [product_of(doc, term_cat) for doc in docs]
    if first:
        head.wait()
    for at, product in enumerate(products):
        start = at * step
        if start == split:
            tail.wait()
        source = near_ref if start < split else held
        yield halves(source[pl.ds(start % split, step), :] / product)


def loaded(term_refs):
    if len(term_refs) == 1:
        return term_refs[0][...]
    mine, other = (ref[...] for ref in term_refs)
    first = lax.axis_index("core") == 0
    return jnp.concatenate([jnp.where(first, mine, other), jnp.where(first, other, mine)], axis=0)


def doc_blocks(doc_ref, step):
    return [halves(doc_ref[start : start + step, :]) for start in range(0, doc_ref.shape[0], step)]


def doc_kernel(first, mass, slab_ref, near_ref, doc_ref, term_refs, out_ref, held, arrived):
    term_value = loaded(term_refs)
    term = halves(term_value)
    pair = jnp.concatenate(term, axis=1)
    pair = jnp.concatenate([pair, pair], axis=0)
    rank = doc_ref.shape[1]
    rows = out_ref.shape[1] - (PAD if mass else 0)
    docs = doc_blocks(doc_ref, DOC_STEP)
    start = 0
    for quotient in quotients(first, slab_ref, near_ref, docs, term_operand(term), held, arrived):
        both = jnp.dot(jnp.concatenate(quotient, axis=1), pair, preferred_element_type=F32)
        result = both[:, :rank] + both[:, rank:]
        for offset in range(0, DOC_STEP, rows):
            out_ref[(start + offset) // rows, :rows, :] = result[offset : offset + rows, :]
        start += DOC_STEP
    if mass:
        total = jnp.sum(term_value, axis=0, keepdims=True)
        for at in range(out_ref.shape[0]):
            out_ref[at, rows:, :] = jnp.broadcast_to(total, (PAD, rank))


def term_kernel(slab_ref, near_ref, doc_ref, term_refs, out_ref, held, arrived):
    rank = doc_ref.shape[1]
    term_cat = term_operand(halves(loaded(term_refs)))
    docs = doc_blocks(doc_ref, TERM_STEP)
    total = None
    for doc, quotient in zip(docs, quotients(False, slab_ref, near_ref, docs, term_cat, held, arrived)):
        pair = jnp.concatenate(doc, axis=1)
        part = lax.dot_general(
            jnp.concatenate(quotient, axis=0),
            jnp.concatenate([pair, pair], axis=0),
            (((0,), (0,)), ((), ())),
            preferred_element_type=F32,
        )
        total = part if total is None else total + part
    result = total[:, :rank] + total[:, rank:]
    sums = jnp.sum(doc_ref[...], axis=0, keepdims=True)
    count, rows = out_ref.shape[0], out_ref.shape[1] - PAD
    for at in range(count):
        out_ref[at, :rows, :] = result[at * rows : (at + 1) * rows, :]
        out_ref[at, rows:, :] = jnp.broadcast_to(sums, (PAD, rank))


def first_doc(slab_ref, doc_ref, term_ref, out_ref, near_ref, doc_own, term_own, held, arrived):
    doc_kernel(True, True, slab_ref, near_ref, doc_ref, (term_ref,), out_ref, held, arrived)
    for axis, source, target in ((NEAR, doc_ref, doc_own), (TERM_OWN, term_ref, term_own)):
        rows = target.shape[0]
        start = pl.multiple_of(lax.axis_index(axis) * rows, rows)
        target[...] = source[pl.ds(start, rows), :]


def later_doc(mass, slab_ref, near_ref, doc_ref, *refs):
    *term_refs, out_ref, held, arrived = refs
    doc_kernel(False, mass, slab_ref, near_ref, doc_ref, term_refs, out_ref, held, arrived)


def any_term(last, slab_ref, near_ref, doc_ref, *refs):
    if not last:
        *term_refs, out_ref, held, arrived = refs
        term_kernel(slab_ref, near_ref, doc_ref, term_refs, out_ref, held, arrived)
        return
    *term_refs, out_ref, doc_out, held, arrived = refs
    copy = pltpu.make_async_copy(doc_ref, doc_out, arrived.at[2])
    copy.start()
    term_kernel(slab_ref, near_ref, doc_ref, term_refs, out_ref, held, arrived)
    copy.wait()


WHOLE = pl.BlockSpec(memory_space=pltpu.VMEM)
APART = pl.BlockSpec(memory_space=pltpu.HBM)


def array(*shape):
    return jax.ShapeDtypeStruct(shape, F32)


def call(kernel, arrays, in_specs, outs, out_specs):
    slab = arrays[0]
    return pl.pallas_call(
        kernel,
        out_shape=outs,
        in_specs=in_specs,
        out_specs=out_specs,
        scratch_shapes=[
            pltpu.VMEM((slab.shape[0] - HELD, slab.shape[1]), F32),
            pltpu.SemaphoreType.DMA((3,)),
        ],
        compiler_params=pltpu.CompilerParams(vmem_limit_bytes=LIMIT * 2**20),
    )(*arrays)


def on_device(slab, doc_factor, term_factor):
    near = lax.axis_size(NEAR)
    rank = doc_factor.shape[1]
    docs = doc_factor.shape[0] // near
    across = lax.axis_size("y")
    terms = term_factor.shape[0] // (2 * across)
    core, row = (lax.axis_index(axis).astype(jnp.uint32) for axis in ("core", "y"))
    here, away = core * across, (1 - core) * across
    partner = [row ^ at for at in range(across)]
    slab, doc_factor, term_factor, core, here, away, partner = lax.optimization_barrier(
        (slab, doc_factor, term_factor, core, here, away, partner)
    )
    term_factor = (term_factor,)
    held = None
    for outer in range(OUTER):
        for inner in range(INNER):
            mass = inner == 0
            blocks = array(near, docs + (PAD if mass else 0), rank)
            if held is None:
                blocks, held, doc_own, term_own = call(
                    first_doc,
                    (slab, doc_factor, *term_factor),
                    [APART, WHOLE, WHOLE],
                    (blocks, array(HELD, slab.shape[1]), array(docs, rank), array(terms, rank)),
                    (WHOLE,) * 4,
                )
            else:
                blocks = call(
                    functools.partial(later_doc, mass),
                    (slab, held, doc_factor, *term_factor),
                    [APART] + [WHOLE] * (2 + len(term_factor)),
                    blocks,
                    WHOLE,
                )
            share = jnp.sum(exchange(blocks, NEAR), axis=0)
            share = total_over(share, FAR)
            if mass:
                term_mass = share[docs]
            doc_own = doc_own * share[:docs] / term_mass
            doc_factor = spread(doc_own, NEAR).reshape(-1, rank)
        last = outer == OUTER - 1
        blocks = array(2 * across, terms + PAD, rank)
        blocks = call(
            functools.partial(any_term, last),
            (slab, held, doc_factor, *term_factor),
            [APART] + [WHOLE] * (2 + len(term_factor)),
            (blocks, array(*doc_factor.shape)) if last else blocks,
            (WHOLE, APART) if last else WHOLE,
        )
        if last:
            blocks, doc_factor = blocks
        mine = lax.dynamic_slice_in_dim(blocks, here, across, 0)
        other = lax.dynamic_slice_in_dim(blocks, away, across, 0)
        mine = mine + swap(other, "core")
        pieces = [lax.dynamic_index_in_dim(mine, at, 0, keepdims=False) for at in partner]
        share = sum([swap(pieces[by], "y", by) for by in ORDER], pieces[0])
        term_own = term_own * share[:terms] / share[terms]
        pieces = {by: swap(term_own, "y", by) for by in ORDER}
        pieces = jnp.stack([term_own] + [pieces[by] for by in range(1, across)])
        mine = jnp.concatenate([lax.dynamic_index_in_dim(pieces, at, 0, keepdims=False) for at in partner], axis=0)
        other = swap(mine, "core")
        term_factor = (mine, other)
    first = core == 0
    term_factor = jnp.concatenate([jnp.where(first, mine, other), jnp.where(first, other, mine)], axis=0)
    return (doc_factor, term_factor)


def solution(mesh):
    parts = Mesh(mesh.devices.reshape(4, 2, 4, 4, 2), ("y", "core", "x", "zh", "zl"))
    return jax.shard_map(
        on_device,
        mesh=parts,
        in_specs=(P(DOC, TERM), P(DOC, None), P(TERM, None)),
        out_specs=(P(DOC, None), P(TERM, None)),
        check_vma=False,
    )
```

time: 216 us -> 211 us (0.977)
  waiting for transfers between devices: 41.7 us -> 38.1 us
  blocking collectives: 92.1 us -> 94.6 us
    ppermute x28, waiting for transfers between devices: 41.7 us -> 38.1 us  [swap(): lax.ppermute(value, axis, [(at, at ^ by) for at in range(lax.axis_size(ax...]
    all_to_all x8, blocking collectives: 92.1 us -> 94.6 us  [exchange(): return lax.all_to_all(blocks, axis, split_axis=0, concat_axis=0, tiled=True)]
  transfers between devices with their start and end apart: 28 -> 28, of which waited for: 19 -> 23; matrix products, arithmetic and copies ran while one was open for 0% -> 0% of each run, Pallas kernels for 0% -> 0%
where the time goes in v3:
time: 211 us
  blocking collectives  94.6 us (45%)
  starting transfers between devices  56.2 us (27%)
  waiting for transfers between devices  38.1 us (18%)
  Pallas kernels  17.1 us (8%)
  local copies, waits for them, and re-layouts  2.41 us (1%)
    all_to_all x8, blocking collectives, exchange(): return lax.all_to_all(blocks, axis, split_axis=0, concat_axis=0, tiled=True)  94.6 us
    ppermute x28, starting transfers between devices, swap(): lax.ppermute(value, axis, [(at, at ^ by) for at in range(lax.axis_size(ax...  56.2 us
    ppermute x28, waiting for transfers between devices, swap(): lax.ppermute(value, axis, [(at, at ^ by) for at in range(lax.axis_size(ax...  38.1 us
    pallas_call x6, Pallas kernels, call(): pl.pallas_call(kernel, out_shape=outs, in_specs=in_specs, out_specs=out_s...  17.1 us
  transfers between devices with their start and end apart: 28, of which 23 were waited for; matrix products, arithmetic and copies ran while one was open for 0% of the time, Pallas kernels for 0%

profile of v3, /device:TPU:1, one launch (start us, length us, event | category | flops | bytes accessed | tf_op | source)
XLA Modules:
  0.0 210.6 jit_solution(7504096314669096020)
XLA Ops:
  2.7 3.2 %shard_map.50 = (f32[8,136,128]{2,1,0:T(8,128)S(1)}, f32[512,1024]{1,0:T(8,128)S(1)}, f32[128,128]{1,0:T(8,128)S(1)}, f32[128,128]{1,0:T(8,128)S(1)}) custom-call(f32[1024,1024]{1,0:T(8,128)} %slab_ref.5, f32[1024,128]{1,0:T(8,128)S(1)} %copy-done.2, f32[1024,128]{1,0:T(8,128)S(1)} %copy-done), custom_call_target="tpu_custom_call" | custom-call | tf_op jit(solution)/shard_map/pallas_call | solution.py:172
  5.9 15.4 %all_to_all.40 = f32[8,136,128]{2,1,0:T(8,128)S(1)} all-to-all(f32[8,136,128]{2,1,0:T(8,128)S(1)} %get-tuple-element.23), channel_id=1, replica_groups=mesh['y'=4,'core'=2,'x'=4,'zh'=4,'zl'=2] {'x','zl'}, dimensions={0} | all-to-all | bytes 1114112 | tf_op jit(solution)/shard_map/all_to_all | solution.py:27
  21.3 6.1 %collective-permute-start.2 = (f32[136,128]{1,0:T(8,128)S(1)}, f32[136,128]{1,0:T(8,128)S(1)}, u32[]{:S(2)}, u32[]{:S(2)}) collective-permute-start(f32[136,128]{1,0:T(8,128)S(1)} %reduce_sum.36), channel_id=1, source_target_pairs={{0,4},{2,6},{4,0},{6,2},{1,5},{3,7},{5,1},{7,3},{8,12},{10,14},{12... | collective-permute-start | bytes 208904 | tf_op jit(solution)/shard_map/ppermute | solution.py:35
  29.2 4.3 %collective-permute-done.1 = f32[136,128]{1,0:T(8,128)S(1)} collective-permute-done((f32[136,128]{1,0:T(8,128)S(1)}, f32[136,128]{1,0:T(8,128)S(1)}, u32[]{:S(2)}, u32[]{:S(2)}) %collective-permute-start.1) | collective-permute-done | bytes 69664 | tf_op jit(solution)/shard_map/ppermute | solution.py:35
  34.2 10.8 %all_to_all.41 = f32[8,128,128]{2,1,0:T(8,128)S(1)} all-to-all(f32[8,128,128]{2,1,0:T(8,128)S(1)} %broadcast_in_dim.12), channel_id=1, replica_groups=mesh['y'=4,'core'=2,'x'=4,'zh'=4,'zl'=2] {'x','zl'}, dimensions={0} | all-to-all | bytes 1048576 | tf_op jit(solution)/shard_map/all_to_all | solution.py:27
  45.0 2.6 %shard_map.51 = f32[8,128,128]{2,1,0:T(8,128)S(1)} custom-call(f32[1024,1024]{1,0:T(8,128)} %slab_ref.5, f32[512,1024]{1,0:T(8,128)S(1)} %get-tuple-element.21.near_ref, f32[1024,128]{1,0:T(8,128)S(1)} %bitcast.63, f32[1024,128]{1,0:T(8,128)S(1)} %copy-done.1), custom_call_target="tpu_custom_call" | custom-call | tf_op jit(solution)/shard_map/pallas_call | solution.py:172
  47.6 10.1 %all_to_all.42 = f32[8,128,128]{2,1,0:T(8,128)S(1)} all-to-all(f32[8,128,128]{2,1,0:T(8,128)S(1)} %shard_map.51), channel_id=1, replica_groups=mesh['y'=4,'core'=2,'x'=4,'zh'=4,'zl'=2] {'x','zl'}, dimensions={0} | all-to-all | bytes 1048576 | tf_op jit(solution)/shard_map/all_to_all | solution.py:27
  57.8 2.9 %collective-permute-start.5 = (f32[128,128]{1,0:T(8,128)S(1)}, f32[128,128]{1,0:T(8,128)S(1)}, u32[]{:S(2)}, u32[]{:S(2)}) collective-permute-start(f32[128,128]{1,0:T(8,128)S(1)} %reduce_sum.37), channel_id=1, source_target_pairs={{0,4},{2,6},{4,0},{6,2},{1,5},{3,7},{5,1},{7,3},{8,12},{10,14},{12... | collective-permute-start | bytes 196616 | tf_op jit(solution)/shard_map/ppermute | solution.py:35
  60.7 4.9 %collective-permute-start.4 = (f32[128,128]{1,0:T(8,128)S(1)}, f32[128,128]{1,0:T(8,128)S(1)}, u32[]{:S(2)}, u32[]{:S(2)}) collective-permute-start(f32[128,128]{1,0:T(8,128)S(1)} %reduce_sum.37), channel_id=1, source_target_pairs={{0,6},{2,4},{4,2},{6,0},{1,7},{3,5},{5,3},{7,1},{8,14},{10,12},{12... | collective-permute-start | bytes 196616 | tf_op jit(solution)/shard_map/ppermute | solution.py:35
  65.6 3.1 %collective-permute-done.4 = f32[128,128]{1,0:T(8,128)S(1)} collective-permute-done((f32[128,128]{1,0:T(8,128)S(1)}, f32[128,128]{1,0:T(8,128)S(1)}, u32[]{:S(2)}, u32[]{:S(2)}) %collective-permute-start.4) | collective-permute-done | bytes 65568 | tf_op jit(solution)/shard_map/ppermute | solution.py:35
  68.7 2.7 %collective-permute-done.3 = f32[128,128]{1,0:T(8,128)S(1)} collective-permute-done((f32[128,128]{1,0:T(8,128)S(1)}, f32[128,128]{1,0:T(8,128)S(1)}, u32[]{:S(2)}, u32[]{:S(2)}) %collective-permute-start.3) | collective-permute-done | bytes 65568 | tf_op jit(solution)/shard_map/ppermute | solution.py:35
  71.5 10.4 %all_to_all.43 = f32[8,128,128]{2,1,0:T(8,128)S(1)} all-to-all(f32[8,128,128]{2,1,0:T(8,128)S(1)} %broadcast_in_dim.13), channel_id=1, replica_groups=mesh['y'=4,'core'=2,'x'=4,'zh'=4,'zl'=2] {'x','zl'}, dimensions={0} | all-to-all | bytes 1048576 | tf_op jit(solution)/shard_map/all_to_all | solution.py:27
  81.9 2.9 %shard_map.52 = f32[8,136,128]{2,1,0:T(8,128)S(1)} custom-call(f32[1024,1024]{1,0:T(8,128)} %slab_ref.5, f32[512,1024]{1,0:T(8,128)S(1)} %get-tuple-element.21.near_ref, f32[1024,128]{1,0:T(8,128)S(1)} %bitcast.60, f32[1024,128]{1,0:T(8,128)S(1)} %copy-done.1), custom_call_target="tpu_custom_call" | custom-call | tf_op jit(solution)/shard_map/pallas_call | solution.py:172
  84.9 4.1 %collective-permute-start.6 = (f32[4,136,128]{2,1,0:T(8,128)S(1)}, f32[4,136,128]{2,1,0:T(8,128)S(1)}, u32[]{:S(2)}, u32[]{:S(2)}) collective-permute-start(f32[4,136,128]{2,1,0:T(8,128)S(1)} %constant_dynamic-slice_fusion.1), channel_id=1, source_target_pairs={{0,32},{32,0},{1,33},{33,1},{2,34},{34,2},{3,35},{35,3},{4,36},{36... | collective-permute-start | bytes 835592 | tf_op jit(solution)/shard_map/ppermute | solution.py:35
  89.0 1.2 collective-permute-done.6
  90.2 1.6 collective-permute-start.7
  91.8 2.4 %collective-permute-start.9 = (f32[136,128]{1,0:T(8,128)S(1)}, f32[136,128]{1,0:T(8,128)S(1)}, u32[]{:S(2)}, u32[]{:S(2)}) collective-permute-start(f32[136,128]{1,0:T(8,128)S(1)} %get-tuple-element.40), channel_id=1, source_target_pairs={{0,128},{64,192},{128,0},{192,64},{1,129},{65,193},{129,1},{193,65... | collective-permute-start | bytes 208904 | tf_op jit(solution)/shard_map/ppermute | solution.py:35
  94.3 3.0 %collective-permute-done.9 = f32[136,128]{1,0:T(8,128)S(1)} collective-permute-done((f32[136,128]{1,0:T(8,128)S(1)}, f32[136,128]{1,0:T(8,128)S(1)}, u32[]{:S(2)}, u32[]{:S(2)}) %collective-permute-start.9) | collective-permute-done | bytes 69664 | tf_op jit(solution)/shard_map/ppermute | solution.py:35
  97.3 1.6 collective-permute-done.8
  99.0 1.5 collective-permute-start.12
  100.9 1.5 collective-permute-start.10
  103.4 1.7 collective-permute-done.11
  105.2 2.9 %collective-permute-start.13 = (f32[512,128]{1,0:T(8,128)S(1)}, f32[512,128]{1,0:T(8,128)S(1)}, u32[]{:S(2)}, u32[]{:S(2)}) collective-permute-start(f32[512,128]{1,0:T(8,128)S(1)} %pad_maximum_fusion.2.refs_0_), channel_id=1, source_target_pairs={{0,32},{32,0},{1,33},{33,1},{2,34},{34,2},{3,35},{35,3},{4,36},{36... | collective-permute-start | bytes 786440 | tf_op jit(solution)/shard_map/ppermute | solution.py:35
  108.1 1.2 collective-permute-done.13.refs_1_
  109.2 2.6 %shard_map.53 = f32[8,136,128]{2,1,0:T(8,128)S(1)} custom-call(f32[1024,1024]{1,0:T(8,128)} %slab_ref.5, f32[512,1024]{1,0:T(8,128)S(1)} %get-tuple-element.21.near_ref, f32[1024,128]{1,0:T(8,128)S(1)} %bitcast.61, f32[512,128]{1,0:T(8,128)S(1)} %pad_maximum_fusion.2.refs_0_, f32[512,128]{1,0:T(8,128)S(1)} %collective-permute-done.13.refs_1_), custom_call_target="tpu_custom_call" | custom-call | tf_op jit(solution)/shard_map/pallas_call | solution.py:172
  111.9 12.5 %all_to_all.44 = f32[8,136,128]{2,1,0:T(8,128)S(1)} all-to-all(f32[8,136,128]{2,1,0:T(8,128)S(1)} %shard_map.53), channel_id=1, replica_groups=mesh['y'=4,'core'=2,'x'=4,'zh'=4,'zl'=2] {'x','zl'}, dimensions={0} | all-to-all | bytes 1114112 | tf_op jit(solution)/shard_map/all_to_all | solution.py:27
  124.4 3.4 %collective-permute-start.16 = (f32[136,128]{1,0:T(8,128)S(1)}, f32[136,128]{1,0:T(8,128)S(1)}, u32[]{:S(2)}, u32[]{:S(2)}) collective-permute-start(f32[136,128]{1,0:T(8,128)S(1)} %reduce_sum.38), channel_id=1, source_target_pairs={{0,4},{2,6},{4,0},{6,2},{1,5},{3,7},{5,1},{7,3},{8,12},{10,14},{12... | collective-permute-start | bytes 208904 | tf_op jit(solution)/shard_map/ppermute | solution.py:35
  127.8 1.3 collective-permute-start.15
  130.2 1.4 collective-permute-done.16
  131.6 2.4 %collective-permute-done.15 = f32[136,128]{1,0:T(8,128)S(1)} collective-permute-done((f32[136,128]{1,0:T(8,128)S(1)}, f32[136,128]{1,0:T(8,128)S(1)}, u32[]{:S(2)}, u32[]{:S(2)}) %collective-permute-start.15) | collective-permute-done | bytes 69664 | tf_op jit(solution)/shard_map/ppermute | solution.py:35
  135.0 13.7 %all_to_all.45 = f32[8,128,128]{2,1,0:T(8,128)S(1)} all-to-all(f32[8,128,128]{2,1,0:T(8,128)S(1)} %broadcast_in_dim.14), channel_id=1, replica_groups=mesh['y'=4,'core'=2,'x'=4,'zh'=4,'zl'=2] {'x','zl'}, dimensions={0} | all-to-all | bytes 1048576 | tf_op jit(solution)/shard_map/all_to_all | solution.py:27
  148.7 2.6 %shard_map.54 = f32[8,128,128]{2,1,0:T(8,128)S(1)} custom-call(f32[1024,1024]{1,0:T(8,128)} %slab_ref.5, f32[512,1024]{1,0:T(8,128)S(1)} %get-tuple-element.21.near_ref, f32[1024,128]{1,0:T(8,128)S(1)} %bitcast.64, f32[512,128]{1,0:T(8,128)S(1)} %pad_maximum_fusion.2.refs_0_, f32[512,128]{1,0:T(8,128)S(1)} %collective-permute-done.13.refs_1_), custom_call_target="tpu_custom_call" | custom-call | tf_op jit(solution)/shard_map/pallas_call | solution.py:172
  151.4 10.6 %all_to_all.46 = f32[8,128,128]{2,1,0:T(8,128)S(1)} all-to-all(f32[8,128,128]{2,1,0:T(8,128)S(1)} %shard_map.54), channel_id=1, replica_groups=mesh['y'=4,'core'=2,'x'=4,'zh'=4,'zl'=2] {'x','zl'}, dimensions={0} | all-to-all | bytes 1048576 | tf_op jit(solution)/shard_map/all_to_all | solution.py:27
  162.0 3.0 %collective-permute-start.19 = (f32[128,128]{1,0:T(8,128)S(1)}, f32[128,128]{1,0:T(8,128)S(1)}, u32[]{:S(2)}, u32[]{:S(2)}) collective-permute-start(f32[128,128]{1,0:T(8,128)S(1)} %reduce_sum.39), channel_id=1, source_target_pairs={{0,4},{2,6},{4,0},{6,2},{1,5},{3,7},{5,1},{7,3},{8,12},{10,14},{12... | collective-permute-start | bytes 196616 | tf_op jit(solution)/shard_map/ppermute | solution.py:35
  165.0 1.8 collective-permute-start.18
  167.7 1.4 collective-permute-done.19
  170.2 1.4 collective-permute-done.17
  171.7 11.0 %all_to_all.47 = f32[8,128,128]{2,1,0:T(8,128)S(1)} all-to-all(f32[8,128,128]{2,1,0:T(8,128)S(1)} %broadcast_in_dim.15), channel_id=1, replica_groups=mesh['y'=4,'core'=2,'x'=4,'zh'=4,'zl'=2] {'x','zl'}, dimensions={0} | all-to-all | bytes 1048576 | tf_op jit(solution)/shard_map/all_to_all | solution.py:27
  182.7 3.1 %shard_map.55 = (f32[8,136,128]{2,1,0:T(8,128)S(1)}, f32[1024,128]{1,0:T(8,128)}) custom-call(f32[1024,1024]{1,0:T(8,128)} %slab_ref.5, f32[512,1024]{1,0:T(8,128)S(1)} %get-tuple-element.21.near_ref, f32[1024,128]{1,0:T(8,128)S(1)} %bitcast.62, f32[512,128]{1,0:T(8,128)S(1)} %pad_maximum_fusion.2.refs_0_, f32[512,128]{1,0:T(8,128)S(1)} %collective-permute-done.13.refs_1_), custom_call_target="tpu_custom_call" | custom-call | tf_op jit(solution)/shard_map/pallas_call | solution.py:172
  185.9 4.7 %collective-permute-start.20 = (f32[4,136,128]{2,1,0:T(8,128)S(1)}, f32[4,136,128]{2,1,0:T(8,128)S(1)}, u32[]{:S(2)}, u32[]{:S(2)}) collective-permute-start(f32[4,136,128]{2,1,0:T(8,128)S(1)} %constant_dynamic-slice_fusion), channel_id=1, source_target_pairs={{0,32},{32,0},{1,33},{33,1},{2,34},{34,2},{3,35},{35,3},{4,36},{36... | collective-permute-start | bytes 835592 | tf_op jit(solution)/shard_map/ppermute | solution.py:35
  190.5 1.2 collective-permute-done.20
  192.9 1.8 collective-permute-start.23
  195.7 2.6 %collective-permute-done.23 = f32[136,128]{1,0:T(8,128)S(1)} collective-permute-done((f32[136,128]{1,0:T(8,128)S(1)}, f32[136,128]{1,0:T(8,128)S(1)}, u32[]{:S(2)}, u32[]{:S(2)}) %collective-permute-start.23) | collective-permute-done | bytes 69664 | tf_op jit(solution)/shard_map/ppermute | solution.py:35
  198.4 1.1 collective-permute-done.22
  201.1 1.7 collective-permute-start.24
  204.0 1.3 collective-permute-done.25
  205.3 3.2 %collective-permute-start.27 = (f32[512,128]{1,0:T(8,128)S(1)}, f32[512,128]{1,0:T(8,128)S(1)}, u32[]{:S(2)}, u32[]{:S(2)}) collective-permute-start(f32[512,128]{1,0:T(8,128)S(1)} %pad_maximum_fusion.4), channel_id=1, source_target_pairs={{0,32},{32,0},{1,33},{33,1},{2,34},{34,2},{3,35},{35,3},{4,36},{36... | collective-permute-start | bytes 786440 | tf_op jit(solution)/shard_map/ppermute | solution.py:35
  208.5 1.2 collective-permute-done.27
  (64 shorter events, 16.5 us)
Async XLA Ops:
  0.6 1.0 copy-start
  1.7 1.0 copy-start.2
  2.7 42.3 %copy-start.1 = (f32[1024,128]{1,0:T(8,128)S(1)}, f32[1024,128]{1,0:T(8,128)}, u32[]{:S(2)}) copy-start(f32[1024,128]{1,0:T(8,128)} %refs_0_.1) | copy-start | bytes 1572868
  21.3 7.8 %collective-permute-start.2 = (f32[136,128]{1,0:T(8,128)S(1)}, f32[136,128]{1,0:T(8,128)S(1)}, u32[]{:S(2)}, u32[]{:S(2)}) collective-permute-start(f32[136,128]{1,0:T(8,128)S(1)} %reduce_sum.36), channel_id=1, source_target_pairs={{0,4},{2,6},{4,0},{6,2},{1,5},{3,7},{5,1},{7,3},{8,12},{10,14},{12... | collective-permute-start | bytes 208904 | tf_op jit(solution)/shard_map/ppermute | solution.py:35
  27.4 6.1 %collective-permute-start.1 = (f32[136,128]{1,0:T(8,128)S(1)}, f32[136,128]{1,0:T(8,128)S(1)}, u32[]{:S(2)}, u32[]{:S(2)}) collective-permute-start(f32[136,128]{1,0:T(8,128)S(1)} %reduce_sum.36), channel_id=1, source_target_pairs={{0,6},{2,4},{4,2},{6,0},{1,7},{3,5},{5,3},{7,1},{8,14},{10,12},{12... | collective-permute-start | bytes 208904 | tf_op jit(solution)/shard_map/ppermute | solution.py:35
  27.7 6.4 %collective-permute-start = (f32[136,128]{1,0:T(8,128)S(1)}, f32[136,128]{1,0:T(8,128)S(1)}, u32[]{:S(2)}, u32[]{:S(2)}) collective-permute-start(f32[136,128]{1,0:T(8,128)S(1)} %reduce_sum.36), channel_id=1, source_target_pairs={{0,2},{2,0},{4,6},{6,4},{1,3},{3,1},{5,7},{7,5},{8,10},{10,8},{12,... | collective-permute-start | bytes 208904 | tf_op jit(solution)/shard_map/ppermute | solution.py:35
  57.8 7.8 %collective-permute-start.5 = (f32[128,128]{1,0:T(8,128)S(1)}, f32[128,128]{1,0:T(8,128)S(1)}, u32[]{:S(2)}, u32[]{:S(2)}) collective-permute-start(f32[128,128]{1,0:T(8,128)S(1)} %reduce_sum.37), channel_id=1, source_target_pairs={{0,4},{2,6},{4,0},{6,2},{1,5},{3,7},{5,1},{7,3},{8,12},{10,14},{12... | collective-permute-start | bytes 196616 | tf_op jit(solution)/shard_map/ppermute | solution.py:35
  60.7 8.1 %collective-permute-start.4 = (f32[128,128]{1,0:T(8,128)S(1)}, f32[128,128]{1,0:T(8,128)S(1)}, u32[]{:S(2)}, u32[]{:S(2)}) collective-permute-start(f32[128,128]{1,0:T(8,128)S(1)} %reduce_sum.37), channel_id=1, source_target_pairs={{0,6},{2,4},{4,2},{6,0},{1,7},{3,5},{5,3},{7,1},{8,14},{10,12},{12... | collective-permute-start | bytes 196616 | tf_op jit(solution)/shard_map/ppermute | solution.py:35
  65.5 5.9 %collective-permute-start.3 = (f32[128,128]{1,0:T(8,128)S(1)}, f32[128,128]{1,0:T(8,128)S(1)}, u32[]{:S(2)}, u32[]{:S(2)}) collective-permute-start(f32[128,128]{1,0:T(8,128)S(1)} %reduce_sum.37), channel_id=1, source_target_pairs={{0,2},{2,0},{4,6},{6,4},{1,3},{3,1},{5,7},{7,5},{8,10},{10,8},{12,... | collective-permute-start | bytes 196616 | tf_op jit(solution)/shard_map/ppermute | solution.py:35
  84.9 5.3 %collective-permute-start.6 = (f32[4,136,128]{2,1,0:T(8,128)S(1)}, f32[4,136,128]{2,1,0:T(8,128)S(1)}, u32[]{:S(2)}, u32[]{:S(2)}) collective-permute-start(f32[4,136,128]{2,1,0:T(8,128)S(1)} %constant_dynamic-slice_fusion.1), channel_id=1, source_target_pairs={{0,32},{32,0},{1,33},{33,1},{2,34},{34,2},{3,35},{35,3},{4,36},{36... | collective-permute-start | bytes 835592 | tf_op jit(solution)/shard_map/ppermute | solution.py:35
  90.2 4.1 %collective-permute-start.7 = (f32[136,128]{1,0:T(8,128)S(1)}, f32[136,128]{1,0:T(8,128)S(1)}, u32[]{:S(2)}, u32[]{:S(2)}) collective-permute-start(f32[136,128]{1,0:T(8,128)S(1)} %get-tuple-element.39), channel_id=1, source_target_pairs={{0,64},{64,0},{128,192},{192,128},{1,65},{65,1},{129,193},{193,129... | collective-permute-start | bytes 208904 | tf_op jit(solution)/shard_map/ppermute | solution.py:35
  91.8 5.5 %collective-permute-start.9 = (f32[136,128]{1,0:T(8,128)S(1)}, f32[136,128]{1,0:T(8,128)S(1)}, u32[]{:S(2)}, u32[]{:S(2)}) collective-permute-start(f32[136,128]{1,0:T(8,128)S(1)} %get-tuple-element.40), channel_id=1, source_target_pairs={{0,128},{64,192},{128,0},{192,64},{1,129},{65,193},{129,1},{193,65... | collective-permute-start | bytes 208904 | tf_op jit(solution)/shard_map/ppermute | solution.py:35
  94.3 4.7 %collective-permute-start.8 = (f32[136,128]{1,0:T(8,128)S(1)}, f32[136,128]{1,0:T(8,128)S(1)}, u32[]{:S(2)}, u32[]{:S(2)}) collective-permute-start(f32[136,128]{1,0:T(8,128)S(1)} %get-tuple-element.41), channel_id=1, source_target_pairs={{0,192},{64,128},{128,64},{192,0},{1,193},{65,129},{129,65},{193,1... | collective-permute-start | bytes 208904 | tf_op jit(solution)/shard_map/ppermute | solution.py:35
  99.0 4.4 %collective-permute-start.12 = (f32[128,128]{1,0:T(8,128)S(1)}, f32[128,128]{1,0:T(8,128)S(1)}, u32[]{:S(2)}, u32[]{:S(2)}) collective-permute-start(f32[128,128]{1,0:T(8,128)S(1)} %fusion.6), channel_id=1, source_target_pairs={{0,192},{64,128},{128,64},{192,0},{1,193},{65,129},{129,65},{193,1... | collective-permute-start | bytes 196616 | tf_op jit(solution)/shard_map/ppermute | solution.py:35
  100.4 4.6 %collective-permute-start.11 = (f32[128,128]{1,0:T(8,128)S(1)}, f32[128,128]{1,0:T(8,128)S(1)}, u32[]{:S(2)}, u32[]{:S(2)}) collective-permute-start(f32[128,128]{1,0:T(8,128)S(1)} %fusion.6), channel_id=1, source_target_pairs={{0,128},{64,192},{128,0},{192,64},{1,129},{65,193},{129,1},{193,65... | collective-permute-start | bytes 196616 | tf_op jit(solution)/shard_map/ppermute | solution.py:35
  100.9 4.2 %collective-permute-start.10 = (f32[128,128]{1,0:T(8,128)S(1)}, f32[128,128]{1,0:T(8,128)S(1)}, u32[]{:S(2)}, u32[]{:S(2)}) collective-permute-start(f32[128,128]{1,0:T(8,128)S(1)} %fusion.6), channel_id=1, source_target_pairs={{0,64},{64,0},{128,192},{192,128},{1,65},{65,1},{129,193},{193,129... | collective-permute-start | bytes 196616 | tf_op jit(solution)/shard_map/ppermute | solution.py:35
  105.2 4.0 %collective-permute-start.13 = (f32[512,128]{1,0:T(8,128)S(1)}, f32[512,128]{1,0:T(8,128)S(1)}, u32[]{:S(2)}, u32[]{:S(2)}) collective-permute-start(f32[512,128]{1,0:T(8,128)S(1)} %pad_maximum_fusion.2.refs_0_), channel_id=1, source_target_pairs={{0,32},{32,0},{1,33},{33,1},{2,34},{34,2},{3,35},{35,3},{4,36},{36... | collective-permute-start | bytes 786440 | tf_op jit(solution)/shard_map/ppermute | solution.py:35
  124.4 7.2 %collective-permute-start.16 = (f32[136,128]{1,0:T(8,128)S(1)}, f32[136,128]{1,0:T(8,128)S(1)}, u32[]{:S(2)}, u32[]{:S(2)}) collective-permute-start(f32[136,128]{1,0:T(8,128)S(1)} %reduce_sum.38), channel_id=1, source_target_pairs={{0,4},{2,6},{4,0},{6,2},{1,5},{3,7},{5,1},{7,3},{8,12},{10,14},{12... | collective-permute-start | bytes 208904 | tf_op jit(solution)/shard_map/ppermute | solution.py:35
  127.8 6.2 %collective-permute-start.15 = (f32[136,128]{1,0:T(8,128)S(1)}, f32[136,128]{1,0:T(8,128)S(1)}, u32[]{:S(2)}, u32[]{:S(2)}) collective-permute-start(f32[136,128]{1,0:T(8,128)S(1)} %reduce_sum.38), channel_id=1, source_target_pairs={{0,6},{2,4},{4,2},{6,0},{1,7},{3,5},{5,3},{7,1},{8,14},{10,12},{12... | collective-permute-start | bytes 208904 | tf_op jit(solution)/shard_map/ppermute | solution.py:35
  129.1 5.8 %collective-permute-start.14 = (f32[136,128]{1,0:T(8,128)S(1)}, f32[136,128]{1,0:T(8,128)S(1)}, u32[]{:S(2)}, u32[]{:S(2)}) collective-permute-start(f32[136,128]{1,0:T(8,128)S(1)} %reduce_sum.38), channel_id=1, source_target_pairs={{0,2},{2,0},{4,6},{6,4},{1,3},{3,1},{5,7},{7,5},{8,10},{10,8},{12,... | collective-permute-start | bytes 208904 | tf_op jit(solution)/shard_map/ppermute | solution.py:35
  162.0 7.1 %collective-permute-start.19 = (f32[128,128]{1,0:T(8,128)S(1)}, f32[128,128]{1,0:T(8,128)S(1)}, u32[]{:S(2)}, u32[]{:S(2)}) collective-permute-start(f32[128,128]{1,0:T(8,128)S(1)} %reduce_sum.39), channel_id=1, source_target_pairs={{0,4},{2,6},{4,0},{6,2},{1,5},{3,7},{5,1},{7,3},{8,12},{10,14},{12... | collective-permute-start | bytes 196616 | tf_op jit(solution)/shard_map/ppermute | solution.py:35
  165.0 5.2 %collective-permute-start.18 = (f32[128,128]{1,0:T(8,128)S(1)}, f32[128,128]{1,0:T(8,128)S(1)}, u32[]{:S(2)}, u32[]{:S(2)}) collective-permute-start(f32[128,128]{1,0:T(8,128)S(1)} %reduce_sum.39), channel_id=1, source_target_pairs={{0,6},{2,4},{4,2},{6,0},{1,7},{3,5},{5,3},{7,1},{8,14},{10,12},{12... | collective-permute-start | bytes 196616 | tf_op jit(solution)/shard_map/ppermute | solution.py:35
  166.8 4.9 %collective-permute-start.17 = (f32[128,128]{1,0:T(8,128)S(1)}, f32[128,128]{1,0:T(8,128)S(1)}, u32[]{:S(2)}, u32[]{:S(2)}) collective-permute-start(f32[128,128]{1,0:T(8,128)S(1)} %reduce_sum.39), channel_id=1, source_target_pairs={{0,2},{2,0},{4,6},{6,4},{1,3},{3,1},{5,7},{7,5},{8,10},{10,8},{12,... | collective-permute-start | bytes 196616 | tf_op jit(solution)/shard_map/ppermute | solution.py:35
  185.9 5.8 %collective-permute-start.20 = (f32[4,136,128]{2,1,0:T(8,128)S(1)}, f32[4,136,128]{2,1,0:T(8,128)S(1)}, u32[]{:S(2)}, u32[]{:S(2)}) collective-permute-start(f32[4,136,128]{2,1,0:T(8,128)S(1)} %constant_dynamic-slice_fusion), channel_id=1, source_target_pairs={{0,32},{32,0},{1,33},{33,1},{2,34},{34,2},{3,35},{35,3},{4,36},{36... | collective-permute-start | bytes 835592 | tf_op jit(solution)/shard_map/ppermute | solution.py:35
  191.8 3.9 %collective-permute-start.21 = (f32[136,128]{1,0:T(8,128)S(1)}, f32[136,128]{1,0:T(8,128)S(1)}, u32[]{:S(2)}, u32[]{:S(2)}) collective-permute-start(f32[136,128]{1,0:T(8,128)S(1)} %get-tuple-element.36), channel_id=1, source_target_pairs={{0,64},{64,0},{128,192},{192,128},{1,65},{65,1},{129,193},{193,129... | collective-permute-start | bytes 208904 | tf_op jit(solution)/shard_map/ppermute | solution.py:35
  192.9 5.5 %collective-permute-start.23 = (f32[136,128]{1,0:T(8,128)S(1)}, f32[136,128]{1,0:T(8,128)S(1)}, u32[]{:S(2)}, u32[]{:S(2)}) collective-permute-start(f32[136,128]{1,0:T(8,128)S(1)} %get-tuple-element.37), channel_id=1, source_target_pairs={{0,128},{64,192},{128,0},{192,64},{1,129},{65,193},{129,1},{193,65... | collective-permute-start | bytes 208904 | tf_op jit(solution)/shard_map/ppermute | solution.py:35
  194.7 4.8 %collective-permute-start.22 = (f32[136,128]{1,0:T(8,128)S(1)}, f32[136,128]{1,0:T(8,128)S(1)}, u32[]{:S(2)}, u32[]{:S(2)}) collective-permute-start(f32[136,128]{1,0:T(8,128)S(1)} %get-tuple-element.38), channel_id=1, source_target_pairs={{0,192},{64,128},{128,64},{192,0},{1,193},{65,129},{129,65},{193,1... | collective-permute-start | bytes 208904 | tf_op jit(solution)/shard_map/ppermute | solution.py:35
  199.5 4.4 %collective-permute-start.26 = (f32[128,128]{1,0:T(8,128)S(1)}, f32[128,128]{1,0:T(8,128)S(1)}, u32[]{:S(2)}, u32[]{:S(2)}) collective-permute-start(f32[128,128]{1,0:T(8,128)S(1)} %fusion.4), channel_id=1, source_target_pairs={{0,192},{64,128},{128,64},{192,0},{1,193},{65,129},{129,65},{193,1... | collective-permute-start | bytes 196616 | tf_op jit(solution)/shard_map/ppermute | solution.py:35
  200.6 4.6 %collective-permute-start.25 = (f32[128,128]{1,0:T(8,128)S(1)}, f32[128,128]{1,0:T(8,128)S(1)}, u32[]{:S(2)}, u32[]{:S(2)}) collective-permute-start(f32[128,128]{1,0:T(8,128)S(1)} %fusion.4), channel_id=1, source_target_pairs={{0,128},{64,192},{128,0},{192,64},{1,129},{65,193},{129,1},{193,65... | collective-permute-start | bytes 196616 | tf_op jit(solution)/shard_map/ppermute | solution.py:35
  201.1 4.1 %collective-permute-start.24 = (f32[128,128]{1,0:T(8,128)S(1)}, f32[128,128]{1,0:T(8,128)S(1)}, u32[]{:S(2)}, u32[]{:S(2)}) collective-permute-start(f32[128,128]{1,0:T(8,128)S(1)} %fusion.4), channel_id=1, source_target_pairs={{0,64},{64,0},{128,192},{192,128},{1,65},{65,1},{129,193},{193,129... | collective-permute-start | bytes 196616 | tf_op jit(solution)/shard_map/ppermute | solution.py:35
  205.3 4.4 %collective-permute-start.27 = (f32[512,128]{1,0:T(8,128)S(1)}, f32[512,128]{1,0:T(8,128)S(1)}, u32[]{:S(2)}, u32[]{:S(2)}) collective-permute-start(f32[512,128]{1,0:T(8,128)S(1)} %pad_maximum_fusion.4), channel_id=1, source_target_pairs={{0,32},{32,0},{1,33},{33,1},{2,34},{34,2},{3,35},{35,3},{4,36},{36... | collective-permute-start | bytes 786440 | tf_op jit(solution)/shard_map/ppermute | solution.py:35

commit v4 on v3

--- a/solution.py
+++ b/solution.py
@@ -9,14 +9,16 @@
 
 OUTER = 2
 INNER = 2
-NEAR = ("x", "zl")
+NEAR = ("zl", "x")
 FAR = "zh"
 DOC = ("y", "core")
 TERM = ("x", "zh", "zl")
 TERM_OWN = ("core", "y")
 F32 = jnp.float32
 PAD = 8
-ORDER = (1, 3, 2)
+ORDER = (3, 1, 2)
+SCATTER = (2, 1, 3)
+GATHER = (1, 3, 2)
 HELD = 512
 DOC_STEP = 256
 TERM_STEP = 512
@@ -134,7 +136,15 @@
         out_ref[at, rows:, :] = jnp.broadcast_to(sums, (PAD, rank))
 
 
-def first_doc(slab_ref, doc_ref, term_ref, out_ref, near_ref, doc_own, term_own, held, arrived):
+def first_doc(slab_ref, doc_in, term_in, out_ref, near_ref, doc_own, term_own, held, doc_ref, term_ref, arrived):
+    copies = [
+        pltpu.make_async_copy(term_in, term_ref, arrived.at[2]),
+        pltpu.make_async_copy(doc_in, doc_ref, arrived.at[3]),
+    ]
+    for copy in copies:
+        copy.start()
+    for copy in copies:
+        copy.wait()
     doc_kernel(True, True, slab_ref, near_ref, doc_ref, (term_ref,), out_ref, held, arrived)
     for axis, source, target in ((NEAR, doc_ref, doc_own), (TERM_OWN, term_ref, term_own)):
         rows = target.shape[0]
@@ -167,7 +177,7 @@
     return jax.ShapeDtypeStruct(shape, F32)
 
 
-def call(kernel, arrays, in_specs, outs, out_specs):
+def call(kernel, arrays, in_specs, outs, out_specs, extra=()):
     slab = arrays[0]
     return pl.pallas_call(
         kernel,
@@ -176,7 +186,8 @@
         out_specs=out_specs,
         scratch_shapes=[
             pltpu.VMEM((slab.shape[0] - HELD, slab.shape[1]), F32),
-            pltpu.SemaphoreType.DMA((3,)),
+            *extra,
+            pltpu.SemaphoreType.DMA((4,)),
         ],
         compiler_params=pltpu.CompilerParams(vmem_limit_bytes=LIMIT * 2**20),
     )(*arrays)
@@ -191,8 +202,9 @@
     core, row = (lax.axis_index(axis).astype(jnp.uint32) for axis in ("core", "y"))
     here, away = core * across, (1 - core) * across
     partner = [row ^ at for at in range(across)]
-    slab, doc_factor, term_factor, core, here, away, partner = lax.optimization_barrier(
-        (slab, doc_factor, term_factor, core, here, away, partner)
+    spots = [at ^ (at >> 1) for at in partner]
+    slab, doc_factor, term_factor, core, here, away, partner, spots = lax.optimization_barrier(
+        (slab, doc_factor, term_factor, core, here, away, partner, spots)
     )
     term_factor = (term_factor,)
     held = None
@@ -203,10 +215,11 @@
             if held is None:
                 blocks, held, doc_own, term_own = call(
                     first_doc,
-                    (slab, doc_factor, *term_factor),
-                    [APART, WHOLE, WHOLE],
+                    (slab, *(pltpu.with_memory_space_constraint(factor, pltpu.HBM) for factor in (doc_factor, *term_factor))),
+                    [APART] * 3,
                     (blocks, array(HELD, slab.shape[1]), array(docs, rank), array(terms, rank)),
                     (WHOLE,) * 4,
+                    [pltpu.VMEM(doc_factor.shape, F32), pltpu.VMEM(term_factor[0].shape, F32)],
                 )
             else:
                 blocks = call(
@@ -237,11 +250,10 @@
         other = lax.dynamic_slice_in_dim(blocks, away, across, 0)
         mine = mine + swap(other, "core")
         pieces = [lax.dynamic_index_in_dim(mine, at, 0, keepdims=False) for at in partner]
-        share = sum([swap(pieces[by], "y", by) for by in ORDER], pieces[0])
+        share = sum([swap(pieces[by], "y", by) for by in SCATTER], pieces[0])
         term_own = term_own * share[:terms] / share[terms]
-        pieces = {by: swap(term_own, "y", by) for by in ORDER}
-        pieces = jnp.stack([term_own] + [pieces[by] for by in range(1, across)])
-        mine = jnp.concatenate([lax.dynamic_index_in_dim(pieces, at, 0, keepdims=False) for at in partner], axis=0)
+        pieces = jnp.stack([term_own] + [swap(term_own, "y", by) for by in GATHER])
+        mine = jnp.concatenate([lax.dynamic_index_in_dim(pieces, at, 0, keepdims=False) for at in spots], axis=0)
         other = swap(mine, "core")
         term_factor = (mine, other)
     first = core == 0

time: 211 us -> 208 us (0.986)
  starting transfers between devices: 56.2 us -> 53.2 us
    ppermute x28, starting transfers between devices: 56.2 us -> 53.2 us  [swap(): lax.ppermute(value, axis, [(at, at ^ by) for at in range(lax.axis_size(ax...]
  transfers between devices with their start and end apart: 28 -> 28, of which waited for: 23 -> 22; matrix products, arithmetic and copies ran while one was open for 0% -> 0% of each run, Pallas kernels for 0% -> 0%
where the time goes in v4:
time: 208 us; the launch traced here: 207 us
  blocking collectives  93.9 us (45%)
  starting transfers between devices  53.2 us (26%)
  waiting for transfers between devices  39 us (19%)
  Pallas kernels  18.3 us (9%)
    all_to_all x8, blocking collectives, exchange(): return lax.all_to_all(blocks, axis, split_axis=0, concat_axis=0, tiled=True)  93.9 us
    ppermute x28, starting transfers between devices, swap(): lax.ppermute(value, axis, [(at, at ^ by) for at in range(lax.axis_size(ax...  53.2 us
    ppermute x28, waiting for transfers between devices, swap(): lax.ppermute(value, axis, [(at, at ^ by) for at in range(lax.axis_size(ax...  39 us
    pallas_call x6, Pallas kernels, call(): pl.pallas_call(kernel, out_shape=outs, in_specs=in_specs, out_specs=out_s...  18.3 us
  transfers between devices with their start and end apart: 28, of which 22 were waited for; matrix products, arithmetic and copies ran while one was open for 0% of the time, Pallas kernels for 0%

profile of v4, /device:TPU:1, one launch (start us, length us, event | category | flops | bytes accessed | tf_op | source)
XLA Modules:
  0.0 207.1 jit_solution(9382472078740196418)
XLA Ops:
  0.7 4.4 %shard_map.50 = (f32[8,136,128]{2,1,0:T(8,128)S(1)}, f32[512,1024]{1,0:T(8,128)S(1)}, f32[128,128]{1,0:T(8,128)S(1)}, f32[128,128]{1,0:T(8,128)S(1)}) custom-call(f32[1024,1024]{1,0:T(8,128)} %slab_ref.5, f32[1024,128]{1,0:T(8,128)} %doc_in, f32[1024,128]{1,0:T(8,128)} %refs_0_.1), custom_call_target="tpu_custom_call" | custom-call | tf_op jit(solution)/shard_map/pallas_call | solution.py:182
  5.0 15.5 %all_to_all.40 = f32[8,136,128]{2,1,0:T(8,128)S(1)} all-to-all(f32[8,136,128]{2,1,0:T(8,128)S(1)} %get-tuple-element.27), channel_id=1, replica_groups=mesh['y'=4,'core'=2,'x'=4,'zh'=4,'zl'=2] {'zl','x'}, dimensions={0} | all-to-all | bytes 1114112 | tf_op jit(solution)/shard_map/all_to_all | solution.py:29
  20.5 6.1 %collective-permute-start.2 = (f32[136,128]{1,0:T(8,128)S(1)}, f32[136,128]{1,0:T(8,128)S(1)}, u32[]{:S(2)}, u32[]{:S(2)}) collective-permute-start(f32[136,128]{1,0:T(8,128)S(1)} %reduce_sum.36), channel_id=1, source_target_pairs={{0,4},{2,6},{4,0},{6,2},{1,5},{3,7},{5,1},{7,3},{8,12},{10,14},{12... | collective-permute-start | bytes 208904 | tf_op jit(solution)/shard_map/ppermute | solution.py:37
  26.6 1.2 collective-permute-start.1
  28.4 5.4 %collective-permute-done.1 = f32[136,128]{1,0:T(8,128)S(1)} collective-permute-done((f32[136,128]{1,0:T(8,128)S(1)}, f32[136,128]{1,0:T(8,128)S(1)}, u32[]{:S(2)}, u32[]{:S(2)}) %collective-permute-start.1) | collective-permute-done | bytes 69664 | tf_op jit(solution)/shard_map/ppermute | solution.py:37
  33.9 10.7 %all_to_all.41 = f32[8,128,128]{2,1,0:T(8,128)S(1)} all-to-all(f32[8,128,128]{2,1,0:T(8,128)S(1)} %broadcast_in_dim.12), channel_id=1, replica_groups=mesh['y'=4,'core'=2,'x'=4,'zh'=4,'zl'=2] {'zl','x'}, dimensions={0} | all-to-all | bytes 1048576 | tf_op jit(solution)/shard_map/all_to_all | solution.py:29
  44.6 2.6 %shard_map.51 = f32[8,128,128]{2,1,0:T(8,128)S(1)} custom-call(f32[1024,1024]{1,0:T(8,128)} %slab_ref.5, f32[512,1024]{1,0:T(8,128)S(1)} %get-tuple-element.25.near_ref, f32[1024,128]{1,0:T(8,128)S(1)} %bitcast.63, f32[1024,128]{1,0:T(8,128)S(1)} %copy-done), custom_call_target="tpu_custom_call" | custom-call | tf_op jit(solution)/shard_map/pallas_call | solution.py:182
  47.2 9.9 %all_to_all.42 = f32[8,128,128]{2,1,0:T(8,128)S(1)} all-to-all(f32[8,128,128]{2,1,0:T(8,128)S(1)} %shard_map.51), channel_id=1, replica_groups=mesh['y'=4,'core'=2,'x'=4,'zh'=4,'zl'=2] {'zl','x'}, dimensions={0} | all-to-all | bytes 1048576 | tf_op jit(solution)/shard_map/all_to_all | solution.py:29
  57.1 5.1 %collective-permute-start.5 = (f32[128,128]{1,0:T(8,128)S(1)}, f32[128,128]{1,0:T(8,128)S(1)}, u32[]{:S(2)}, u32[]{:S(2)}) collective-permute-start(f32[128,128]{1,0:T(8,128)S(1)} %reduce_sum.37), channel_id=1, source_target_pairs={{0,4},{2,6},{4,0},{6,2},{1,5},{3,7},{5,1},{7,3},{8,12},{10,14},{12... | collective-permute-start | bytes 196616 | tf_op jit(solution)/shard_map/ppermute | solution.py:37
  62.2 1.1 collective-permute-start.4
  64.2 2.7 %collective-permute-done.4 = f32[128,128]{1,0:T(8,128)S(1)} collective-permute-done((f32[128,128]{1,0:T(8,128)S(1)}, f32[128,128]{1,0:T(8,128)S(1)}, u32[]{:S(2)}, u32[]{:S(2)}) %collective-permute-start.4) | collective-permute-done | bytes 65568 | tf_op jit(solution)/shard_map/ppermute | solution.py:37
  66.9 1.7 collective-permute-done.3
  68.7 12.5 %all_to_all.43 = f32[8,128,128]{2,1,0:T(8,128)S(1)} all-to-all(f32[8,128,128]{2,1,0:T(8,128)S(1)} %broadcast_in_dim.13), channel_id=1, replica_groups=mesh['y'=4,'core'=2,'x'=4,'zh'=4,'zl'=2] {'zl','x'}, dimensions={0} | all-to-all | bytes 1048576 | tf_op jit(solution)/shard_map/all_to_all | solution.py:29
  81.2 2.9 %shard_map.52 = f32[8,136,128]{2,1,0:T(8,128)S(1)} custom-call(f32[1024,1024]{1,0:T(8,128)} %slab_ref.5, f32[512,1024]{1,0:T(8,128)S(1)} %get-tuple-element.25.near_ref, f32[1024,128]{1,0:T(8,128)S(1)} %bitcast.60, f32[1024,128]{1,0:T(8,128)S(1)} %copy-done), custom_call_target="tpu_custom_call" | custom-call | tf_op jit(solution)/shard_map/pallas_call | solution.py:182
  84.2 4.6 %collective-permute-start.6 = (f32[4,136,128]{2,1,0:T(8,128)S(1)}, f32[4,136,128]{2,1,0:T(8,128)S(1)}, u32[]{:S(2)}, u32[]{:S(2)}) collective-permute-start(f32[4,136,128]{2,1,0:T(8,128)S(1)} %constant_dynamic-slice_fusion.1), channel_id=1, source_target_pairs={{0,32},{32,0},{1,33},{33,1},{2,34},{34,2},{3,35},{35,3},{4,36},{36... | collective-permute-start | bytes 835592 | tf_op jit(solution)/shard_map/ppermute | solution.py:37
  88.8 1.2 collective-permute-done.6
  90.0 3.1 %collective-permute-start.7 = (f32[136,128]{1,0:T(8,128)S(1)}, f32[136,128]{1,0:T(8,128)S(1)}, u32[]{:S(2)}, u32[]{:S(2)}) collective-permute-start(f32[136,128]{1,0:T(8,128)S(1)} %get-tuple-element.47), channel_id=1, source_target_pairs={{0,128},{64,192},{128,0},{192,64},{1,129},{65,193},{129,1},{193,65... | collective-permute-start | bytes 208904 | tf_op jit(solution)/shard_map/ppermute | solution.py:37
  94.9 2.6 %collective-permute-done.9 = f32[136,128]{1,0:T(8,128)S(1)} collective-permute-done((f32[136,128]{1,0:T(8,128)S(1)}, f32[136,128]{1,0:T(8,128)S(1)}, u32[]{:S(2)}, u32[]{:S(2)}) %collective-permute-start.9) | collective-permute-done | bytes 69664 | tf_op jit(solution)/shard_map/ppermute | solution.py:37
  97.6 1.6 collective-permute-start.12
  99.2 2.1 collective-permute-start.11
  102.3 1.2 collective-permute-done.11
  103.5 1.4 collective-permute-done.10
  105.0 1.9 collective-permute-start.13
  106.8 1.2 collective-permute-done.13.refs_1_
  108.0 2.6 %shard_map.53 = f32[8,136,128]{2,1,0:T(8,128)S(1)} custom-call(f32[1024,1024]{1,0:T(8,128)} %slab_ref.5, f32[512,1024]{1,0:T(8,128)S(1)} %get-tuple-element.25.near_ref, f32[1024,128]{1,0:T(8,128)S(1)} %bitcast.61, f32[512,128]{1,0:T(8,128)S(1)} %pad_maximum_fusion.2.refs_0_, f32[512,128]{1,0:T(8,128)S(1)} %collective-permute-done.13.refs_1_), custom_call_target="tpu_custom_call" | custom-call | tf_op jit(solution)/shard_map/pallas_call | solution.py:182
  110.7 12.5 %all_to_all.44 = f32[8,136,128]{2,1,0:T(8,128)S(1)} all-to-all(f32[8,136,128]{2,1,0:T(8,128)S(1)} %shard_map.53), channel_id=1, replica_groups=mesh['y'=4,'core'=2,'x'=4,'zh'=4,'zl'=2] {'zl','x'}, dimensions={0} | all-to-all | bytes 1114112 | tf_op jit(solution)/shard_map/all_to_all | solution.py:29
  123.2 2.8 %collective-permute-start.16 = (f32[136,128]{1,0:T(8,128)S(1)}, f32[136,128]{1,0:T(8,128)S(1)}, u32[]{:S(2)}, u32[]{:S(2)}) collective-permute-start(f32[136,128]{1,0:T(8,128)S(1)} %reduce_sum.38), channel_id=1, source_target_pairs={{0,4},{2,6},{4,0},{6,2},{1,5},{3,7},{5,1},{7,3},{8,12},{10,14},{12... | collective-permute-start | bytes 208904 | tf_op jit(solution)/shard_map/ppermute | solution.py:37
  126.1 2.8 %collective-permute-start.14 = (f32[136,128]{1,0:T(8,128)S(1)}, f32[136,128]{1,0:T(8,128)S(1)}, u32[]{:S(2)}, u32[]{:S(2)}) collective-permute-start(f32[136,128]{1,0:T(8,128)S(1)} %reduce_sum.38), channel_id=1, source_target_pairs={{0,6},{2,4},{4,2},{6,0},{1,7},{3,5},{5,3},{7,1},{8,14},{10,12},{12... | collective-permute-start | bytes 208904 | tf_op jit(solution)/shard_map/ppermute | solution.py:37
  128.9 2.3 %collective-permute-done.16 = f32[136,128]{1,0:T(8,128)S(1)} collective-permute-done((f32[136,128]{1,0:T(8,128)S(1)}, f32[136,128]{1,0:T(8,128)S(1)}, u32[]{:S(2)}, u32[]{:S(2)}) %collective-permute-start.16) | collective-permute-done | bytes 69664 | tf_op jit(solution)/shard_map/ppermute | solution.py:37
  131.2 3.2 %collective-permute-done.15 = f32[136,128]{1,0:T(8,128)S(1)} collective-permute-done((f32[136,128]{1,0:T(8,128)S(1)}, f32[136,128]{1,0:T(8,128)S(1)}, u32[]{:S(2)}, u32[]{:S(2)}) %collective-permute-start.15) | collective-permute-done | bytes 69664 | tf_op jit(solution)/shard_map/ppermute | solution.py:37
  134.4 12.4 %all_to_all.45 = f32[8,128,128]{2,1,0:T(8,128)S(1)} all-to-all(f32[8,128,128]{2,1,0:T(8,128)S(1)} %broadcast_in_dim.14), channel_id=1, replica_groups=mesh['y'=4,'core'=2,'x'=4,'zh'=4,'zl'=2] {'zl','x'}, dimensions={0} | all-to-all | bytes 1048576 | tf_op jit(solution)/shard_map/all_to_all | solution.py:29
  146.8 2.6 %shard_map.54 = f32[8,128,128]{2,1,0:T(8,128)S(1)} custom-call(f32[1024,1024]{1,0:T(8,128)} %slab_ref.5, f32[512,1024]{1,0:T(8,128)S(1)} %get-tuple-element.25.near_ref, f32[1024,128]{1,0:T(8,128)S(1)} %bitcast.64, f32[512,128]{1,0:T(8,128)S(1)} %pad_maximum_fusion.2.refs_0_, f32[512,128]{1,0:T(8,128)S(1)} %collective-permute-done.13.refs_1_), custom_call_target="tpu_custom_call" | custom-call | tf_op jit(solution)/shard_map/pallas_call | solution.py:182
  149.4 10.4 %all_to_all.46 = f32[8,128,128]{2,1,0:T(8,128)S(1)} all-to-all(f32[8,128,128]{2,1,0:T(8,128)S(1)} %shard_map.54), channel_id=1, replica_groups=mesh['y'=4,'core'=2,'x'=4,'zh'=4,'zl'=2] {'zl','x'}, dimensions={0} | all-to-all | bytes 1048576 | tf_op jit(solution)/shard_map/all_to_all | solution.py:29
  159.8 2.1 %collective-permute-start.19 = (f32[128,128]{1,0:T(8,128)S(1)}, f32[128,128]{1,0:T(8,128)S(1)}, u32[]{:S(2)}, u32[]{:S(2)}) collective-permute-start(f32[128,128]{1,0:T(8,128)S(1)} %reduce_sum.39), channel_id=1, source_target_pairs={{0,4},{2,6},{4,0},{6,2},{1,5},{3,7},{5,1},{7,3},{8,12},{10,14},{12... | collective-permute-start | bytes 196616 | tf_op jit(solution)/shard_map/ppermute | solution.py:37
  162.5 3.1 %collective-permute-start.17 = (f32[128,128]{1,0:T(8,128)S(1)}, f32[128,128]{1,0:T(8,128)S(1)}, u32[]{:S(2)}, u32[]{:S(2)}) collective-permute-start(f32[128,128]{1,0:T(8,128)S(1)} %reduce_sum.39), channel_id=1, source_target_pairs={{0,6},{2,4},{4,2},{6,0},{1,7},{3,5},{5,3},{7,1},{8,14},{10,12},{12... | collective-permute-start | bytes 196616 | tf_op jit(solution)/shard_map/ppermute | solution.py:37
  165.6 2.3 %collective-permute-done.19 = f32[128,128]{1,0:T(8,128)S(1)} collective-permute-done((f32[128,128]{1,0:T(8,128)S(1)}, f32[128,128]{1,0:T(8,128)S(1)}, u32[]{:S(2)}, u32[]{:S(2)}) %collective-permute-start.19) | collective-permute-done | bytes 65568 | tf_op jit(solution)/shard_map/ppermute | solution.py:37
  169.0 10.2 %all_to_all.47 = f32[8,128,128]{2,1,0:T(8,128)S(1)} all-to-all(f32[8,128,128]{2,1,0:T(8,128)S(1)} %broadcast_in_dim.15), channel_id=1, replica_groups=mesh['y'=4,'core'=2,'x'=4,'zh'=4,'zl'=2] {'zl','x'}, dimensions={0} | all-to-all | bytes 1048576 | tf_op jit(solution)/shard_map/all_to_all | solution.py:29
  179.2 3.1 %shard_map.55 = (f32[8,136,128]{2,1,0:T(8,128)S(1)}, f32[1024,128]{1,0:T(8,128)}) custom-call(f32[1024,1024]{1,0:T(8,128)} %slab_ref.5, f32[512,1024]{1,0:T(8,128)S(1)} %get-tuple-element.25.near_ref, f32[1024,128]{1,0:T(8,128)S(1)} %bitcast.62, f32[512,128]{1,0:T(8,128)S(1)} %pad_maximum_fusion.2.refs_0_, f32[512,128]{1,0:T(8,128)S(1)} %collective-permute-done.13.refs_1_), custom_call_target="tpu_custom_call" | custom-call | tf_op jit(solution)/shard_map/pallas_call | solution.py:182
  182.4 5.8 %collective-permute-start.20 = (f32[4,136,128]{2,1,0:T(8,128)S(1)}, f32[4,136,128]{2,1,0:T(8,128)S(1)}, u32[]{:S(2)}, u32[]{:S(2)}) collective-permute-start(f32[4,136,128]{2,1,0:T(8,128)S(1)} %constant_dynamic-slice_fusion), channel_id=1, source_target_pairs={{0,32},{32,0},{1,33},{33,1},{2,34},{34,2},{3,35},{35,3},{4,36},{36... | collective-permute-start | bytes 835592 | tf_op jit(solution)/shard_map/ppermute | solution.py:37
  188.2 1.2 collective-permute-done.20
  189.4 1.9 collective-permute-start.21
  192.2 2.0 collective-permute-done.21
  194.2 1.6 collective-permute-done.23
  195.8 2.0 collective-permute-start.26
  197.9 1.6 collective-permute-start.25
  200.5 2.5 %collective-permute-done.25 = f32[128,128]{1,0:T(8,128)S(1)} collective-permute-done((f32[128,128]{1,0:T(8,128)S(1)}, f32[128,128]{1,0:T(8,128)S(1)}, u32[]{:S(2)}, u32[]{:S(2)}) %collective-permute-start.25) | collective-permute-done | bytes 65568 | tf_op jit(solution)/shard_map/ppermute | solution.py:37
  203.2 1.9 collective-permute-start.27
  205.0 1.2 collective-permute-done.27
  (60 shorter events, 9.6 us)
Async XLA Ops:
  0.7 43.9 %copy-start = (f32[1024,128]{1,0:T(8,128)S(1)}, f32[1024,128]{1,0:T(8,128)}, u32[]{:S(2)}) copy-start(f32[1024,128]{1,0:T(8,128)} %refs_0_.1) | copy-start | bytes 1572868
  20.5 7.8 %collective-permute-start.2 = (f32[136,128]{1,0:T(8,128)S(1)}, f32[136,128]{1,0:T(8,128)S(1)}, u32[]{:S(2)}, u32[]{:S(2)}) collective-permute-start(f32[136,128]{1,0:T(8,128)S(1)} %reduce_sum.36), channel_id=1, source_target_pairs={{0,4},{2,6},{4,0},{6,2},{1,5},{3,7},{5,1},{7,3},{8,12},{10,14},{12... | collective-permute-start | bytes 208904 | tf_op jit(solution)/shard_map/ppermute | solution.py:37
  26.6 7.1 %collective-permute-start.1 = (f32[136,128]{1,0:T(8,128)S(1)}, f32[136,128]{1,0:T(8,128)S(1)}, u32[]{:S(2)}, u32[]{:S(2)}) collective-permute-start(f32[136,128]{1,0:T(8,128)S(1)} %reduce_sum.36), channel_id=1, source_target_pairs={{0,2},{2,0},{4,6},{6,4},{1,3},{3,1},{5,7},{7,5},{8,10},{10,8},{12,... | collective-permute-start | bytes 208904 | tf_op jit(solution)/shard_map/ppermute | solution.py:37
  27.8 5.9 %collective-permute-start = (f32[136,128]{1,0:T(8,128)S(1)}, f32[136,128]{1,0:T(8,128)S(1)}, u32[]{:S(2)}, u32[]{:S(2)}) collective-permute-start(f32[136,128]{1,0:T(8,128)S(1)} %reduce_sum.36), channel_id=1, source_target_pairs={{0,6},{2,4},{4,2},{6,0},{1,7},{3,5},{5,3},{7,1},{8,14},{10,12},{12... | collective-permute-start | bytes 208904 | tf_op jit(solution)/shard_map/ppermute | solution.py:37
  57.1 7.1 %collective-permute-start.5 = (f32[128,128]{1,0:T(8,128)S(1)}, f32[128,128]{1,0:T(8,128)S(1)}, u32[]{:S(2)}, u32[]{:S(2)}) collective-permute-start(f32[128,128]{1,0:T(8,128)S(1)} %reduce_sum.37), channel_id=1, source_target_pairs={{0,4},{2,6},{4,0},{6,2},{1,5},{3,7},{5,1},{7,3},{8,12},{10,14},{12... | collective-permute-start | bytes 196616 | tf_op jit(solution)/shard_map/ppermute | solution.py:37
  62.2 4.7 %collective-permute-start.4 = (f32[128,128]{1,0:T(8,128)S(1)}, f32[128,128]{1,0:T(8,128)S(1)}, u32[]{:S(2)}, u32[]{:S(2)}) collective-permute-start(f32[128,128]{1,0:T(8,128)S(1)} %reduce_sum.37), channel_id=1, source_target_pairs={{0,2},{2,0},{4,6},{6,4},{1,3},{3,1},{5,7},{7,5},{8,10},{10,8},{12,... | collective-permute-start | bytes 196616 | tf_op jit(solution)/shard_map/ppermute | solution.py:37
  63.4 5.3 %collective-permute-start.3 = (f32[128,128]{1,0:T(8,128)S(1)}, f32[128,128]{1,0:T(8,128)S(1)}, u32[]{:S(2)}, u32[]{:S(2)}) collective-permute-start(f32[128,128]{1,0:T(8,128)S(1)} %reduce_sum.37), channel_id=1, source_target_pairs={{0,6},{2,4},{4,2},{6,0},{1,7},{3,5},{5,3},{7,1},{8,14},{10,12},{12... | collective-permute-start | bytes 196616 | tf_op jit(solution)/shard_map/ppermute | solution.py:37
  84.2 5.8 %collective-permute-start.6 = (f32[4,136,128]{2,1,0:T(8,128)S(1)}, f32[4,136,128]{2,1,0:T(8,128)S(1)}, u32[]{:S(2)}, u32[]{:S(2)}) collective-permute-start(f32[4,136,128]{2,1,0:T(8,128)S(1)} %constant_dynamic-slice_fusion.1), channel_id=1, source_target_pairs={{0,32},{32,0},{1,33},{33,1},{2,34},{34,2},{3,35},{35,3},{4,36},{36... | collective-permute-start | bytes 835592 | tf_op jit(solution)/shard_map/ppermute | solution.py:37
  90.0 4.9 %collective-permute-start.7 = (f32[136,128]{1,0:T(8,128)S(1)}, f32[136,128]{1,0:T(8,128)S(1)}, u32[]{:S(2)}, u32[]{:S(2)}) collective-permute-start(f32[136,128]{1,0:T(8,128)S(1)} %get-tuple-element.47), channel_id=1, source_target_pairs={{0,128},{64,192},{128,0},{192,64},{1,129},{65,193},{129,1},{193,65... | collective-permute-start | bytes 208904 | tf_op jit(solution)/shard_map/ppermute | solution.py:37
  93.2 4.4 %collective-permute-start.9 = (f32[136,128]{1,0:T(8,128)S(1)}, f32[136,128]{1,0:T(8,128)S(1)}, u32[]{:S(2)}, u32[]{:S(2)}) collective-permute-start(f32[136,128]{1,0:T(8,128)S(1)} %get-tuple-element.48), channel_id=1, source_target_pairs={{0,192},{64,128},{128,64},{192,0},{1,193},{65,129},{129,65},{193,1... | collective-permute-start | bytes 208904 | tf_op jit(solution)/shard_map/ppermute | solution.py:37
  94.0 3.6 %collective-permute-start.8 = (f32[136,128]{1,0:T(8,128)S(1)}, f32[136,128]{1,0:T(8,128)S(1)}, u32[]{:S(2)}, u32[]{:S(2)}) collective-permute-start(f32[136,128]{1,0:T(8,128)S(1)} %get-tuple-element.49), channel_id=1, source_target_pairs={{0,64},{64,0},{128,192},{192,128},{1,65},{65,1},{129,193},{193,129... | collective-permute-start | bytes 208904 | tf_op jit(solution)/shard_map/ppermute | solution.py:37
  97.6 4.7 %collective-permute-start.12 = (f32[128,128]{1,0:T(8,128)S(1)}, f32[128,128]{1,0:T(8,128)S(1)}, u32[]{:S(2)}, u32[]{:S(2)}) collective-permute-start(f32[128,128]{1,0:T(8,128)S(1)} %fusion.6), channel_id=1, source_target_pairs={{0,128},{64,192},{128,0},{192,64},{1,129},{65,193},{129,1},{193,65... | collective-permute-start | bytes 196616 | tf_op jit(solution)/shard_map/ppermute | solution.py:37
  99.2 4.3 %collective-permute-start.11 = (f32[128,128]{1,0:T(8,128)S(1)}, f32[128,128]{1,0:T(8,128)S(1)}, u32[]{:S(2)}, u32[]{:S(2)}) collective-permute-start(f32[128,128]{1,0:T(8,128)S(1)} %fusion.6), channel_id=1, source_target_pairs={{0,192},{64,128},{128,64},{192,0},{1,193},{65,129},{129,65},{193,1... | collective-permute-start | bytes 196616 | tf_op jit(solution)/shard_map/ppermute | solution.py:37
  101.2 3.7 %collective-permute-start.10 = (f32[128,128]{1,0:T(8,128)S(1)}, f32[128,128]{1,0:T(8,128)S(1)}, u32[]{:S(2)}, u32[]{:S(2)}) collective-permute-start(f32[128,128]{1,0:T(8,128)S(1)} %fusion.6), channel_id=1, source_target_pairs={{0,64},{64,0},{128,192},{192,128},{1,65},{65,1},{129,193},{193,129... | collective-permute-start | bytes 196616 | tf_op jit(solution)/shard_map/ppermute | solution.py:37
  105.0 3.0 %collective-permute-start.13 = (f32[512,128]{1,0:T(8,128)S(1)}, f32[512,128]{1,0:T(8,128)S(1)}, u32[]{:S(2)}, u32[]{:S(2)}) collective-permute-start(f32[512,128]{1,0:T(8,128)S(1)} %pad_maximum_fusion.2.refs_0_), channel_id=1, source_target_pairs={{0,32},{32,0},{1,33},{33,1},{2,34},{34,2},{3,35},{35,3},{4,36},{36... | collective-permute-start | bytes 786440 | tf_op jit(solution)/shard_map/ppermute | solution.py:37
  123.2 8.0 %collective-permute-start.16 = (f32[136,128]{1,0:T(8,128)S(1)}, f32[136,128]{1,0:T(8,128)S(1)}, u32[]{:S(2)}, u32[]{:S(2)}) collective-permute-start(f32[136,128]{1,0:T(8,128)S(1)} %reduce_sum.38), channel_id=1, source_target_pairs={{0,4},{2,6},{4,0},{6,2},{1,5},{3,7},{5,1},{7,3},{8,12},{10,14},{12... | collective-permute-start | bytes 208904 | tf_op jit(solution)/shard_map/ppermute | solution.py:37
  126.0 8.3 %collective-permute-start.15 = (f32[136,128]{1,0:T(8,128)S(1)}, f32[136,128]{1,0:T(8,128)S(1)}, u32[]{:S(2)}, u32[]{:S(2)}) collective-permute-start(f32[136,128]{1,0:T(8,128)S(1)} %reduce_sum.38), channel_id=1, source_target_pairs={{0,2},{2,0},{4,6},{6,4},{1,3},{3,1},{5,7},{7,5},{8,10},{10,8},{12,... | collective-permute-start | bytes 208904 | tf_op jit(solution)/shard_map/ppermute | solution.py:37
  126.1 8.2 %collective-permute-start.14 = (f32[136,128]{1,0:T(8,128)S(1)}, f32[136,128]{1,0:T(8,128)S(1)}, u32[]{:S(2)}, u32[]{:S(2)}) collective-permute-start(f32[136,128]{1,0:T(8,128)S(1)} %reduce_sum.38), channel_id=1, source_target_pairs={{0,6},{2,4},{4,2},{6,0},{1,7},{3,5},{5,3},{7,1},{8,14},{10,12},{12... | collective-permute-start | bytes 208904 | tf_op jit(solution)/shard_map/ppermute | solution.py:37
  159.8 8.0 %collective-permute-start.19 = (f32[128,128]{1,0:T(8,128)S(1)}, f32[128,128]{1,0:T(8,128)S(1)}, u32[]{:S(2)}, u32[]{:S(2)}) collective-permute-start(f32[128,128]{1,0:T(8,128)S(1)} %reduce_sum.39), channel_id=1, source_target_pairs={{0,4},{2,6},{4,0},{6,2},{1,5},{3,7},{5,1},{7,3},{8,12},{10,14},{12... | collective-permute-start | bytes 196616 | tf_op jit(solution)/shard_map/ppermute | solution.py:37
  161.9 5.9 %collective-permute-start.18 = (f32[128,128]{1,0:T(8,128)S(1)}, f32[128,128]{1,0:T(8,128)S(1)}, u32[]{:S(2)}, u32[]{:S(2)}) collective-permute-start(f32[128,128]{1,0:T(8,128)S(1)} %reduce_sum.39), channel_id=1, source_target_pairs={{0,2},{2,0},{4,6},{6,4},{1,3},{3,1},{5,7},{7,5},{8,10},{10,8},{12,... | collective-permute-start | bytes 196616 | tf_op jit(solution)/shard_map/ppermute | solution.py:37
  162.5 6.4 %collective-permute-start.17 = (f32[128,128]{1,0:T(8,128)S(1)}, f32[128,128]{1,0:T(8,128)S(1)}, u32[]{:S(2)}, u32[]{:S(2)}) collective-permute-start(f32[128,128]{1,0:T(8,128)S(1)} %reduce_sum.39), channel_id=1, source_target_pairs={{0,6},{2,4},{4,2},{6,0},{1,7},{3,5},{5,3},{7,1},{8,14},{10,12},{12... | collective-permute-start | bytes 196616 | tf_op jit(solution)/shard_map/ppermute | solution.py:37
  182.4 7.0 %collective-permute-start.20 = (f32[4,136,128]{2,1,0:T(8,128)S(1)}, f32[4,136,128]{2,1,0:T(8,128)S(1)}, u32[]{:S(2)}, u32[]{:S(2)}) collective-permute-start(f32[4,136,128]{2,1,0:T(8,128)S(1)} %constant_dynamic-slice_fusion), channel_id=1, source_target_pairs={{0,32},{32,0},{1,33},{33,1},{2,34},{34,2},{3,35},{35,3},{4,36},{36... | collective-permute-start | bytes 835592 | tf_op jit(solution)/shard_map/ppermute | solution.py:37
  189.4 4.8 %collective-permute-start.21 = (f32[136,128]{1,0:T(8,128)S(1)}, f32[136,128]{1,0:T(8,128)S(1)}, u32[]{:S(2)}, u32[]{:S(2)}) collective-permute-start(f32[136,128]{1,0:T(8,128)S(1)} %get-tuple-element.44), channel_id=1, source_target_pairs={{0,128},{64,192},{128,0},{192,64},{1,129},{65,193},{129,1},{193,65... | collective-permute-start | bytes 208904 | tf_op jit(solution)/shard_map/ppermute | solution.py:37
  191.3 4.4 %collective-permute-start.23 = (f32[136,128]{1,0:T(8,128)S(1)}, f32[136,128]{1,0:T(8,128)S(1)}, u32[]{:S(2)}, u32[]{:S(2)}) collective-permute-start(f32[136,128]{1,0:T(8,128)S(1)} %get-tuple-element.45), channel_id=1, source_target_pairs={{0,192},{64,128},{128,64},{192,0},{1,193},{65,129},{129,65},{193,1... | collective-permute-start | bytes 208904 | tf_op jit(solution)/shard_map/ppermute | solution.py:37
  192.2 3.6 %collective-permute-start.22 = (f32[136,128]{1,0:T(8,128)S(1)}, f32[136,128]{1,0:T(8,128)S(1)}, u32[]{:S(2)}, u32[]{:S(2)}) collective-permute-start(f32[136,128]{1,0:T(8,128)S(1)} %get-tuple-element.46), channel_id=1, source_target_pairs={{0,64},{64,0},{128,192},{192,128},{1,65},{65,1},{129,193},{193,129... | collective-permute-start | bytes 208904 | tf_op jit(solution)/shard_map/ppermute | solution.py:37
  195.8 4.7 %collective-permute-start.26 = (f32[128,128]{1,0:T(8,128)S(1)}, f32[128,128]{1,0:T(8,128)S(1)}, u32[]{:S(2)}, u32[]{:S(2)}) collective-permute-start(f32[128,128]{1,0:T(8,128)S(1)} %fusion.4), channel_id=1, source_target_pairs={{0,128},{64,192},{128,0},{192,64},{1,129},{65,193},{129,1},{193,65... | collective-permute-start | bytes 196616 | tf_op jit(solution)/shard_map/ppermute | solution.py:37
  197.9 5.2 %collective-permute-start.25 = (f32[128,128]{1,0:T(8,128)S(1)}, f32[128,128]{1,0:T(8,128)S(1)}, u32[]{:S(2)}, u32[]{:S(2)}) collective-permute-start(f32[128,128]{1,0:T(8,128)S(1)} %fusion.4), channel_id=1, source_target_pairs={{0,192},{64,128},{128,64},{192,0},{1,193},{65,129},{129,65},{193,1... | collective-permute-start | bytes 196616 | tf_op jit(solution)/shard_map/ppermute | solution.py:37
  199.4 3.6 %collective-permute-start.24 = (f32[128,128]{1,0:T(8,128)S(1)}, f32[128,128]{1,0:T(8,128)S(1)}, u32[]{:S(2)}, u32[]{:S(2)}) collective-permute-start(f32[128,128]{1,0:T(8,128)S(1)} %fusion.4), channel_id=1, source_target_pairs={{0,64},{64,0},{128,192},{192,128},{1,65},{65,1},{129,193},{193,129... | collective-permute-start | bytes 196616 | tf_op jit(solution)/shard_map/ppermute | solution.py:37
  203.2 3.0 %collective-permute-start.27 = (f32[512,128]{1,0:T(8,128)S(1)}, f32[512,128]{1,0:T(8,128)S(1)}, u32[]{:S(2)}, u32[]{:S(2)}) collective-permute-start(f32[512,128]{1,0:T(8,128)S(1)} %pad_maximum_fusion.4), channel_id=1, source_target_pairs={{0,32},{32,0},{1,33},{33,1},{2,34},{34,2},{3,35},{35,3},{4,36},{36... | collective-permute-start | bytes 786440 | tf_op jit(solution)/shard_map/ppermute | solution.py:37

commit v5 on v4

--- a/solution.py
+++ b/solution.py
@@ -61,18 +61,22 @@
     return jnp.concatenate([high, high, low, low], axis=1)
 
 
+def head_copy(slab_ref, near_ref, arrived):
+    return pltpu.make_async_copy(slab_ref.at[pl.ds(0, HELD)], near_ref, arrived.at[0])
+
+
+def tail_copy(slab_ref, held, arrived):
+    return pltpu.make_async_copy(slab_ref.at[pl.ds(HELD, held.shape[0])], held, arrived.at[1])
+
+
 def quotients(first, slab_ref, near_ref, docs, term_cat, held, arrived):
     split, step = near_ref.shape[0], docs[0][0].shape[0]
-    if first:
-        head = pltpu.make_async_copy(slab_ref.at[pl.ds(0, split)], near_ref, arrived.at[0])
-        head.start()
-    tail = pltpu.make_async_copy(
-        slab_ref.at[pl.ds(split, held.shape[0])], held, arrived.at[1]
-    )
-    tail.start()
+    tail = tail_copy(slab_ref, held, arrived)
+    if not first:
+        tail.start()
     products = [product_of(doc, term_cat) for doc in docs]
     if first:
-        head.wait()
+        head_copy(slab_ref, near_ref, arrived).wait()
     for at, product in enumerate(products):
         start = at * step
         if start == split:
@@ -141,10 +145,11 @@
         pltpu.make_async_copy(term_in, term_ref, arrived.at[2]),
         pltpu.make_async_copy(doc_in, doc_ref, arrived.at[3]),
     ]
-    for copy in copies:
+    for copy in (*copies, head_copy(slab_ref, near_ref, arrived)):
         copy.start()
     for copy in copies:
         copy.wait()
+    tail_copy(slab_ref, held, arrived).start()
     doc_kernel(True, True, slab_ref, near_ref, doc_ref, (term_ref,), out_ref, held, arrived)
     for axis, source, target in ((NEAR, doc_ref, doc_own), (TERM_OWN, term_ref, term_own)):
         rows = target.shape[0]

time: 208 us -> 207 us (level)
  no operation moved by 1% of the time
where the time goes in v5:
time: 207 us
  blocking collectives  93.9 us (45%)
  starting transfers between devices  53.3 us (26%)
  waiting for transfers between devices  39 us (19%)
  Pallas kernels  18 us (9%)
    all_to_all x8, blocking collectives, exchange(): return lax.all_to_all(blocks, axis, split_axis=0, concat_axis=0, tiled=True)  93.9 us
    ppermute x28, starting transfers between devices, swap(): lax.ppermute(value, axis, [(at, at ^ by) for at in range(lax.axis_size(ax...  53.3 us
    ppermute x28, waiting for transfers between devices, swap(): lax.ppermute(value, axis, [(at, at ^ by) for at in range(lax.axis_size(ax...  39 us
    pallas_call x6, Pallas kernels, call(): pl.pallas_call(kernel, out_shape=outs, in_specs=in_specs, out_specs=out_s...  18 us
  transfers between devices with their start and end apart: 28, of which 22 were waited for; matrix products, arithmetic and copies ran while one was open for 0% of the time, Pallas kernels for 0%

profile of v5, /device:TPU:1, one launch (start us, length us, event | category | flops | bytes accessed | tf_op | source)
XLA Modules:
  0.0 206.8 jit_solution(5428635786359167719)
XLA Ops:
  0.7 4.1 %shard_map.50 = (f32[8,136,128]{2,1,0:T(8,128)S(1)}, f32[512,1024]{1,0:T(8,128)S(1)}, f32[128,128]{1,0:T(8,128)S(1)}, f32[128,128]{1,0:T(8,128)S(1)}) custom-call(f32[1024,1024]{1,0:T(8,128)} %slab_ref.5, f32[1024,128]{1,0:T(8,128)} %doc_in, f32[1024,128]{1,0:T(8,128)} %refs_0_.1), custom_call_target="tpu_custom_call" | custom-call | tf_op jit(solution)/shard_map/pallas_call | solution.py:187
  4.8 15.5 %all_to_all.40 = f32[8,136,128]{2,1,0:T(8,128)S(1)} all-to-all(f32[8,136,128]{2,1,0:T(8,128)S(1)} %get-tuple-element.27), channel_id=1, replica_groups=mesh['y'=4,'core'=2,'x'=4,'zh'=4,'zl'=2] {'zl','x'}, dimensions={0} | all-to-all | bytes 1114112 | tf_op jit(solution)/shard_map/all_to_all | solution.py:29
  20.2 6.1 %collective-permute-start.2 = (f32[136,128]{1,0:T(8,128)S(1)}, f32[136,128]{1,0:T(8,128)S(1)}, u32[]{:S(2)}, u32[]{:S(2)}) collective-permute-start(f32[136,128]{1,0:T(8,128)S(1)} %reduce_sum.36), channel_id=1, source_target_pairs={{0,4},{2,6},{4,0},{6,2},{1,5},{3,7},{5,1},{7,3},{8,12},{10,14},{12... | collective-permute-start | bytes 208904 | tf_op jit(solution)/shard_map/ppermute | solution.py:37
  26.3 1.2 collective-permute-start.1
  28.1 5.4 %collective-permute-done.1 = f32[136,128]{1,0:T(8,128)S(1)} collective-permute-done((f32[136,128]{1,0:T(8,128)S(1)}, f32[136,128]{1,0:T(8,128)S(1)}, u32[]{:S(2)}, u32[]{:S(2)}) %collective-permute-start.1) | collective-permute-done | bytes 69664 | tf_op jit(solution)/shard_map/ppermute | solution.py:37
  33.6 10.7 %all_to_all.41 = f32[8,128,128]{2,1,0:T(8,128)S(1)} all-to-all(f32[8,128,128]{2,1,0:T(8,128)S(1)} %broadcast_in_dim.12), channel_id=1, replica_groups=mesh['y'=4,'core'=2,'x'=4,'zh'=4,'zl'=2] {'zl','x'}, dimensions={0} | all-to-all | bytes 1048576 | tf_op jit(solution)/shard_map/all_to_all | solution.py:29
  44.3 2.6 %shard_map.51 = f32[8,128,128]{2,1,0:T(8,128)S(1)} custom-call(f32[1024,1024]{1,0:T(8,128)} %slab_ref.5, f32[512,1024]{1,0:T(8,128)S(1)} %get-tuple-element.25.near_ref, f32[1024,128]{1,0:T(8,128)S(1)} %bitcast.63, f32[1024,128]{1,0:T(8,128)S(1)} %copy-done), custom_call_target="tpu_custom_call" | custom-call | tf_op jit(solution)/shard_map/pallas_call | solution.py:187
  46.9 9.9 %all_to_all.42 = f32[8,128,128]{2,1,0:T(8,128)S(1)} all-to-all(f32[8,128,128]{2,1,0:T(8,128)S(1)} %shard_map.51), channel_id=1, replica_groups=mesh['y'=4,'core'=2,'x'=4,'zh'=4,'zl'=2] {'zl','x'}, dimensions={0} | all-to-all | bytes 1048576 | tf_op jit(solution)/shard_map/all_to_all | solution.py:29
  56.8 5.1 %collective-permute-start.5 = (f32[128,128]{1,0:T(8,128)S(1)}, f32[128,128]{1,0:T(8,128)S(1)}, u32[]{:S(2)}, u32[]{:S(2)}) collective-permute-start(f32[128,128]{1,0:T(8,128)S(1)} %reduce_sum.37), channel_id=1, source_target_pairs={{0,4},{2,6},{4,0},{6,2},{1,5},{3,7},{5,1},{7,3},{8,12},{10,14},{12... | collective-permute-start | bytes 196616 | tf_op jit(solution)/shard_map/ppermute | solution.py:37
  61.9 1.2 collective-permute-start.4
  63.9 2.7 %collective-permute-done.4 = f32[128,128]{1,0:T(8,128)S(1)} collective-permute-done((f32[128,128]{1,0:T(8,128)S(1)}, f32[128,128]{1,0:T(8,128)S(1)}, u32[]{:S(2)}, u32[]{:S(2)}) %collective-permute-start.4) | collective-permute-done | bytes 65568 | tf_op jit(solution)/shard_map/ppermute | solution.py:37
  66.7 1.7 collective-permute-done.3
  68.4 12.4 %all_to_all.43 = f32[8,128,128]{2,1,0:T(8,128)S(1)} all-to-all(f32[8,128,128]{2,1,0:T(8,128)S(1)} %broadcast_in_dim.13), channel_id=1, replica_groups=mesh['y'=4,'core'=2,'x'=4,'zh'=4,'zl'=2] {'zl','x'}, dimensions={0} | all-to-all | bytes 1048576 | tf_op jit(solution)/shard_map/all_to_all | solution.py:29
  80.9 2.9 %shard_map.52 = f32[8,136,128]{2,1,0:T(8,128)S(1)} custom-call(f32[1024,1024]{1,0:T(8,128)} %slab_ref.5, f32[512,1024]{1,0:T(8,128)S(1)} %get-tuple-element.25.near_ref, f32[1024,128]{1,0:T(8,128)S(1)} %bitcast.60, f32[1024,128]{1,0:T(8,128)S(1)} %copy-done), custom_call_target="tpu_custom_call" | custom-call | tf_op jit(solution)/shard_map/pallas_call | solution.py:187
  83.9 4.6 %collective-permute-start.6 = (f32[4,136,128]{2,1,0:T(8,128)S(1)}, f32[4,136,128]{2,1,0:T(8,128)S(1)}, u32[]{:S(2)}, u32[]{:S(2)}) collective-permute-start(f32[4,136,128]{2,1,0:T(8,128)S(1)} %constant_dynamic-slice_fusion.1), channel_id=1, source_target_pairs={{0,32},{32,0},{1,33},{33,1},{2,34},{34,2},{3,35},{35,3},{4,36},{36... | collective-permute-start | bytes 835592 | tf_op jit(solution)/shard_map/ppermute | solution.py:37
  88.5 1.2 collective-permute-done.6
  89.7 3.2 %collective-permute-start.7 = (f32[136,128]{1,0:T(8,128)S(1)}, f32[136,128]{1,0:T(8,128)S(1)}, u32[]{:S(2)}, u32[]{:S(2)}) collective-permute-start(f32[136,128]{1,0:T(8,128)S(1)} %get-tuple-element.47), channel_id=1, source_target_pairs={{0,128},{64,192},{128,0},{192,64},{1,129},{65,193},{129,1},{193,65... | collective-permute-start | bytes 208904 | tf_op jit(solution)/shard_map/ppermute | solution.py:37
  94.7 2.6 %collective-permute-done.9 = f32[136,128]{1,0:T(8,128)S(1)} collective-permute-done((f32[136,128]{1,0:T(8,128)S(1)}, f32[136,128]{1,0:T(8,128)S(1)}, u32[]{:S(2)}, u32[]{:S(2)}) %collective-permute-start.9) | collective-permute-done | bytes 69664 | tf_op jit(solution)/shard_map/ppermute | solution.py:37
  97.3 1.6 collective-permute-start.12
  98.9 2.0 collective-permute-start.11
  102.0 1.2 collective-permute-done.11
  103.2 1.4 collective-permute-done.10
  104.7 1.8 collective-permute-start.13
  106.5 1.2 collective-permute-done.13.refs_1_
  107.7 2.6 %shard_map.53 = f32[8,136,128]{2,1,0:T(8,128)S(1)} custom-call(f32[1024,1024]{1,0:T(8,128)} %slab_ref.5, f32[512,1024]{1,0:T(8,128)S(1)} %get-tuple-element.25.near_ref, f32[1024,128]{1,0:T(8,128)S(1)} %bitcast.61, f32[512,128]{1,0:T(8,128)S(1)} %pad_maximum_fusion.2.refs_0_, f32[512,128]{1,0:T(8,128)S(1)} %collective-permute-done.13.refs_1_), custom_call_target="tpu_custom_call" | custom-call | tf_op jit(solution)/shard_map/pallas_call | solution.py:187
  110.3 12.4 %all_to_all.44 = f32[8,136,128]{2,1,0:T(8,128)S(1)} all-to-all(f32[8,136,128]{2,1,0:T(8,128)S(1)} %shard_map.53), channel_id=1, replica_groups=mesh['y'=4,'core'=2,'x'=4,'zh'=4,'zl'=2] {'zl','x'}, dimensions={0} | all-to-all | bytes 1114112 | tf_op jit(solution)/shard_map/all_to_all | solution.py:29
  122.8 2.9 %collective-permute-start.16 = (f32[136,128]{1,0:T(8,128)S(1)}, f32[136,128]{1,0:T(8,128)S(1)}, u32[]{:S(2)}, u32[]{:S(2)}) collective-permute-start(f32[136,128]{1,0:T(8,128)S(1)} %reduce_sum.38), channel_id=1, source_target_pairs={{0,4},{2,6},{4,0},{6,2},{1,5},{3,7},{5,1},{7,3},{8,12},{10,14},{12... | collective-permute-start | bytes 208904 | tf_op jit(solution)/shard_map/ppermute | solution.py:37
  125.8 2.8 %collective-permute-start.14 = (f32[136,128]{1,0:T(8,128)S(1)}, f32[136,128]{1,0:T(8,128)S(1)}, u32[]{:S(2)}, u32[]{:S(2)}) collective-permute-start(f32[136,128]{1,0:T(8,128)S(1)} %reduce_sum.38), channel_id=1, source_target_pairs={{0,6},{2,4},{4,2},{6,0},{1,7},{3,5},{5,3},{7,1},{8,14},{10,12},{12... | collective-permute-start | bytes 208904 | tf_op jit(solution)/shard_map/ppermute | solution.py:37
  128.6 2.3 %collective-permute-done.16 = f32[136,128]{1,0:T(8,128)S(1)} collective-permute-done((f32[136,128]{1,0:T(8,128)S(1)}, f32[136,128]{1,0:T(8,128)S(1)}, u32[]{:S(2)}, u32[]{:S(2)}) %collective-permute-start.16) | collective-permute-done | bytes 69664 | tf_op jit(solution)/shard_map/ppermute | solution.py:37
  130.8 3.2 %collective-permute-done.15 = f32[136,128]{1,0:T(8,128)S(1)} collective-permute-done((f32[136,128]{1,0:T(8,128)S(1)}, f32[136,128]{1,0:T(8,128)S(1)}, u32[]{:S(2)}, u32[]{:S(2)}) %collective-permute-start.15) | collective-permute-done | bytes 69664 | tf_op jit(solution)/shard_map/ppermute | solution.py:37
  134.1 12.3 %all_to_all.45 = f32[8,128,128]{2,1,0:T(8,128)S(1)} all-to-all(f32[8,128,128]{2,1,0:T(8,128)S(1)} %broadcast_in_dim.14), channel_id=1, replica_groups=mesh['y'=4,'core'=2,'x'=4,'zh'=4,'zl'=2] {'zl','x'}, dimensions={0} | all-to-all | bytes 1048576 | tf_op jit(solution)/shard_map/all_to_all | solution.py:29
  146.4 2.6 %shard_map.54 = f32[8,128,128]{2,1,0:T(8,128)S(1)} custom-call(f32[1024,1024]{1,0:T(8,128)} %slab_ref.5, f32[512,1024]{1,0:T(8,128)S(1)} %get-tuple-element.25.near_ref, f32[1024,128]{1,0:T(8,128)S(1)} %bitcast.64, f32[512,128]{1,0:T(8,128)S(1)} %pad_maximum_fusion.2.refs_0_, f32[512,128]{1,0:T(8,128)S(1)} %collective-permute-done.13.refs_1_), custom_call_target="tpu_custom_call" | custom-call | tf_op jit(solution)/shard_map/pallas_call | solution.py:187
  149.1 10.4 %all_to_all.46 = f32[8,128,128]{2,1,0:T(8,128)S(1)} all-to-all(f32[8,128,128]{2,1,0:T(8,128)S(1)} %shard_map.54), channel_id=1, replica_groups=mesh['y'=4,'core'=2,'x'=4,'zh'=4,'zl'=2] {'zl','x'}, dimensions={0} | all-to-all | bytes 1048576 | tf_op jit(solution)/shard_map/all_to_all | solution.py:29
  159.5 2.2 %collective-permute-start.19 = (f32[128,128]{1,0:T(8,128)S(1)}, f32[128,128]{1,0:T(8,128)S(1)}, u32[]{:S(2)}, u32[]{:S(2)}) collective-permute-start(f32[128,128]{1,0:T(8,128)S(1)} %reduce_sum.39), channel_id=1, source_target_pairs={{0,4},{2,6},{4,0},{6,2},{1,5},{3,7},{5,1},{7,3},{8,12},{10,14},{12... | collective-permute-start | bytes 196616 | tf_op jit(solution)/shard_map/ppermute | solution.py:37
  161.9 3.4 %collective-permute-start.17 = (f32[128,128]{1,0:T(8,128)S(1)}, f32[128,128]{1,0:T(8,128)S(1)}, u32[]{:S(2)}, u32[]{:S(2)}) collective-permute-start(f32[128,128]{1,0:T(8,128)S(1)} %reduce_sum.39), channel_id=1, source_target_pairs={{0,6},{2,4},{4,2},{6,0},{1,7},{3,5},{5,3},{7,1},{8,14},{10,12},{12... | collective-permute-start | bytes 196616 | tf_op jit(solution)/shard_map/ppermute | solution.py:37
  165.3 2.2 %collective-permute-done.19 = f32[128,128]{1,0:T(8,128)S(1)} collective-permute-done((f32[128,128]{1,0:T(8,128)S(1)}, f32[128,128]{1,0:T(8,128)S(1)}, u32[]{:S(2)}, u32[]{:S(2)}) %collective-permute-start.19) | collective-permute-done | bytes 65568 | tf_op jit(solution)/shard_map/ppermute | solution.py:37
  168.7 10.3 %all_to_all.47 = f32[8,128,128]{2,1,0:T(8,128)S(1)} all-to-all(f32[8,128,128]{2,1,0:T(8,128)S(1)} %broadcast_in_dim.15), channel_id=1, replica_groups=mesh['y'=4,'core'=2,'x'=4,'zh'=4,'zl'=2] {'zl','x'}, dimensions={0} | all-to-all | bytes 1048576 | tf_op jit(solution)/shard_map/all_to_all | solution.py:29
  178.9 3.1 %shard_map.55 = (f32[8,136,128]{2,1,0:T(8,128)S(1)}, f32[1024,128]{1,0:T(8,128)}) custom-call(f32[1024,1024]{1,0:T(8,128)} %slab_ref.5, f32[512,1024]{1,0:T(8,128)S(1)} %get-tuple-element.25.near_ref, f32[1024,128]{1,0:T(8,128)S(1)} %bitcast.62, f32[512,128]{1,0:T(8,128)S(1)} %pad_maximum_fusion.2.refs_0_, f32[512,128]{1,0:T(8,128)S(1)} %collective-permute-done.13.refs_1_), custom_call_target="tpu_custom_call" | custom-call | tf_op jit(solution)/shard_map/pallas_call | solution.py:187
  182.1 5.8 %collective-permute-start.20 = (f32[4,136,128]{2,1,0:T(8,128)S(1)}, f32[4,136,128]{2,1,0:T(8,128)S(1)}, u32[]{:S(2)}, u32[]{:S(2)}) collective-permute-start(f32[4,136,128]{2,1,0:T(8,128)S(1)} %constant_dynamic-slice_fusion), channel_id=1, source_target_pairs={{0,32},{32,0},{1,33},{33,1},{2,34},{34,2},{3,35},{35,3},{4,36},{36... | collective-permute-start | bytes 835592 | tf_op jit(solution)/shard_map/ppermute | solution.py:37
  187.9 1.2 collective-permute-done.20
  189.2 1.8 collective-permute-start.21
  192.0 1.9 collective-permute-done.21
  193.9 1.6 collective-permute-done.23
  195.6 2.1 %collective-permute-start.26 = (f32[128,128]{1,0:T(8,128)S(1)}, f32[128,128]{1,0:T(8,128)S(1)}, u32[]{:S(2)}, u32[]{:S(2)}) collective-permute-start(f32[128,128]{1,0:T(8,128)S(1)} %fusion.4), channel_id=1, source_target_pairs={{0,128},{64,192},{128,0},{192,64},{1,129},{65,193},{129,1},{193,65... | collective-permute-start | bytes 196616 | tf_op jit(solution)/shard_map/ppermute | solution.py:37
  197.7 1.5 collective-permute-start.25
  200.3 2.5 %collective-permute-done.25 = f32[128,128]{1,0:T(8,128)S(1)} collective-permute-done((f32[128,128]{1,0:T(8,128)S(1)}, f32[128,128]{1,0:T(8,128)S(1)}, u32[]{:S(2)}, u32[]{:S(2)}) %collective-permute-start.25) | collective-permute-done | bytes 65568 | tf_op jit(solution)/shard_map/ppermute | solution.py:37
  202.8 1.9 collective-permute-start.27
  204.7 1.2 collective-permute-done.27
  (60 shorter events, 9.4 us)
Async XLA Ops:
  0.7 43.6 %copy-start = (f32[1024,128]{1,0:T(8,128)S(1)}, f32[1024,128]{1,0:T(8,128)}, u32[]{:S(2)}) copy-start(f32[1024,128]{1,0:T(8,128)} %refs_0_.1) | copy-start | bytes 1572868
  20.2 7.8 %collective-permute-start.2 = (f32[136,128]{1,0:T(8,128)S(1)}, f32[136,128]{1,0:T(8,128)S(1)}, u32[]{:S(2)}, u32[]{:S(2)}) collective-permute-start(f32[136,128]{1,0:T(8,128)S(1)} %reduce_sum.36), channel_id=1, source_target_pairs={{0,4},{2,6},{4,0},{6,2},{1,5},{3,7},{5,1},{7,3},{8,12},{10,14},{12... | collective-permute-start | bytes 208904 | tf_op jit(solution)/shard_map/ppermute | solution.py:37
  26.3 7.1 %collective-permute-start.1 = (f32[136,128]{1,0:T(8,128)S(1)}, f32[136,128]{1,0:T(8,128)S(1)}, u32[]{:S(2)}, u32[]{:S(2)}) collective-permute-start(f32[136,128]{1,0:T(8,128)S(1)} %reduce_sum.36), channel_id=1, source_target_pairs={{0,2},{2,0},{4,6},{6,4},{1,3},{3,1},{5,7},{7,5},{8,10},{10,8},{12,... | collective-permute-start | bytes 208904 | tf_op jit(solution)/shard_map/ppermute | solution.py:37
  27.5 6.0 %collective-permute-start = (f32[136,128]{1,0:T(8,128)S(1)}, f32[136,128]{1,0:T(8,128)S(1)}, u32[]{:S(2)}, u32[]{:S(2)}) collective-permute-start(f32[136,128]{1,0:T(8,128)S(1)} %reduce_sum.36), channel_id=1, source_target_pairs={{0,6},{2,4},{4,2},{6,0},{1,7},{3,5},{5,3},{7,1},{8,14},{10,12},{12... | collective-permute-start | bytes 208904 | tf_op jit(solution)/shard_map/ppermute | solution.py:37
  56.8 7.1 %collective-permute-start.5 = (f32[128,128]{1,0:T(8,128)S(1)}, f32[128,128]{1,0:T(8,128)S(1)}, u32[]{:S(2)}, u32[]{:S(2)}) collective-permute-start(f32[128,128]{1,0:T(8,128)S(1)} %reduce_sum.37), channel_id=1, source_target_pairs={{0,4},{2,6},{4,0},{6,2},{1,5},{3,7},{5,1},{7,3},{8,12},{10,14},{12... | collective-permute-start | bytes 196616 | tf_op jit(solution)/shard_map/ppermute | solution.py:37
  61.9 4.7 %collective-permute-start.4 = (f32[128,128]{1,0:T(8,128)S(1)}, f32[128,128]{1,0:T(8,128)S(1)}, u32[]{:S(2)}, u32[]{:S(2)}) collective-permute-start(f32[128,128]{1,0:T(8,128)S(1)} %reduce_sum.37), channel_id=1, source_target_pairs={{0,2},{2,0},{4,6},{6,4},{1,3},{3,1},{5,7},{7,5},{8,10},{10,8},{12,... | collective-permute-start | bytes 196616 | tf_op jit(solution)/shard_map/ppermute | solution.py:37
  63.1 5.3 %collective-permute-start.3 = (f32[128,128]{1,0:T(8,128)S(1)}, f32[128,128]{1,0:T(8,128)S(1)}, u32[]{:S(2)}, u32[]{:S(2)}) collective-permute-start(f32[128,128]{1,0:T(8,128)S(1)} %reduce_sum.37), channel_id=1, source_target_pairs={{0,6},{2,4},{4,2},{6,0},{1,7},{3,5},{5,3},{7,1},{8,14},{10,12},{12... | collective-permute-start | bytes 196616 | tf_op jit(solution)/shard_map/ppermute | solution.py:37
  83.9 5.8 %collective-permute-start.6 = (f32[4,136,128]{2,1,0:T(8,128)S(1)}, f32[4,136,128]{2,1,0:T(8,128)S(1)}, u32[]{:S(2)}, u32[]{:S(2)}) collective-permute-start(f32[4,136,128]{2,1,0:T(8,128)S(1)} %constant_dynamic-slice_fusion.1), channel_id=1, source_target_pairs={{0,32},{32,0},{1,33},{33,1},{2,34},{34,2},{3,35},{35,3},{4,36},{36... | collective-permute-start | bytes 835592 | tf_op jit(solution)/shard_map/ppermute | solution.py:37
  89.7 4.9 %collective-permute-start.7 = (f32[136,128]{1,0:T(8,128)S(1)}, f32[136,128]{1,0:T(8,128)S(1)}, u32[]{:S(2)}, u32[]{:S(2)}) collective-permute-start(f32[136,128]{1,0:T(8,128)S(1)} %get-tuple-element.47), channel_id=1, source_target_pairs={{0,128},{64,192},{128,0},{192,64},{1,129},{65,193},{129,1},{193,65... | collective-permute-start | bytes 208904 | tf_op jit(solution)/shard_map/ppermute | solution.py:37
  92.9 4.4 %collective-permute-start.9 = (f32[136,128]{1,0:T(8,128)S(1)}, f32[136,128]{1,0:T(8,128)S(1)}, u32[]{:S(2)}, u32[]{:S(2)}) collective-permute-start(f32[136,128]{1,0:T(8,128)S(1)} %get-tuple-element.48), channel_id=1, source_target_pairs={{0,192},{64,128},{128,64},{192,0},{1,193},{65,129},{129,65},{193,1... | collective-permute-start | bytes 208904 | tf_op jit(solution)/shard_map/ppermute | solution.py:37
  93.7 3.6 %collective-permute-start.8 = (f32[136,128]{1,0:T(8,128)S(1)}, f32[136,128]{1,0:T(8,128)S(1)}, u32[]{:S(2)}, u32[]{:S(2)}) collective-permute-start(f32[136,128]{1,0:T(8,128)S(1)} %get-tuple-element.49), channel_id=1, source_target_pairs={{0,64},{64,0},{128,192},{192,128},{1,65},{65,1},{129,193},{193,129... | collective-permute-start | bytes 208904 | tf_op jit(solution)/shard_map/ppermute | solution.py:37
  97.3 4.7 %collective-permute-start.12 = (f32[128,128]{1,0:T(8,128)S(1)}, f32[128,128]{1,0:T(8,128)S(1)}, u32[]{:S(2)}, u32[]{:S(2)}) collective-permute-start(f32[128,128]{1,0:T(8,128)S(1)} %fusion.6), channel_id=1, source_target_pairs={{0,128},{64,192},{128,0},{192,64},{1,129},{65,193},{129,1},{193,65... | collective-permute-start | bytes 196616 | tf_op jit(solution)/shard_map/ppermute | solution.py:37
  98.9 4.3 %collective-permute-start.11 = (f32[128,128]{1,0:T(8,128)S(1)}, f32[128,128]{1,0:T(8,128)S(1)}, u32[]{:S(2)}, u32[]{:S(2)}) collective-permute-start(f32[128,128]{1,0:T(8,128)S(1)} %fusion.6), channel_id=1, source_target_pairs={{0,192},{64,128},{128,64},{192,0},{1,193},{65,129},{129,65},{193,1... | collective-permute-start | bytes 196616 | tf_op jit(solution)/shard_map/ppermute | solution.py:37
  100.9 3.8 %collective-permute-start.10 = (f32[128,128]{1,0:T(8,128)S(1)}, f32[128,128]{1,0:T(8,128)S(1)}, u32[]{:S(2)}, u32[]{:S(2)}) collective-permute-start(f32[128,128]{1,0:T(8,128)S(1)} %fusion.6), channel_id=1, source_target_pairs={{0,64},{64,0},{128,192},{192,128},{1,65},{65,1},{129,193},{193,129... | collective-permute-start | bytes 196616 | tf_op jit(solution)/shard_map/ppermute | solution.py:37
  104.7 3.0 %collective-permute-start.13 = (f32[512,128]{1,0:T(8,128)S(1)}, f32[512,128]{1,0:T(8,128)S(1)}, u32[]{:S(2)}, u32[]{:S(2)}) collective-permute-start(f32[512,128]{1,0:T(8,128)S(1)} %pad_maximum_fusion.2.refs_0_), channel_id=1, source_target_pairs={{0,32},{32,0},{1,33},{33,1},{2,34},{34,2},{3,35},{35,3},{4,36},{36... | collective-permute-start | bytes 786440 | tf_op jit(solution)/shard_map/ppermute | solution.py:37
  122.8 8.0 %collective-permute-start.16 = (f32[136,128]{1,0:T(8,128)S(1)}, f32[136,128]{1,0:T(8,128)S(1)}, u32[]{:S(2)}, u32[]{:S(2)}) collective-permute-start(f32[136,128]{1,0:T(8,128)S(1)} %reduce_sum.38), channel_id=1, source_target_pairs={{0,4},{2,6},{4,0},{6,2},{1,5},{3,7},{5,1},{7,3},{8,12},{10,14},{12... | collective-permute-start | bytes 208904 | tf_op jit(solution)/shard_map/ppermute | solution.py:37
  125.7 8.4 %collective-permute-start.15 = (f32[136,128]{1,0:T(8,128)S(1)}, f32[136,128]{1,0:T(8,128)S(1)}, u32[]{:S(2)}, u32[]{:S(2)}) collective-permute-start(f32[136,128]{1,0:T(8,128)S(1)} %reduce_sum.38), channel_id=1, source_target_pairs={{0,2},{2,0},{4,6},{6,4},{1,3},{3,1},{5,7},{7,5},{8,10},{10,8},{12,... | collective-permute-start | bytes 208904 | tf_op jit(solution)/shard_map/ppermute | solution.py:37
  125.8 8.2 %collective-permute-start.14 = (f32[136,128]{1,0:T(8,128)S(1)}, f32[136,128]{1,0:T(8,128)S(1)}, u32[]{:S(2)}, u32[]{:S(2)}) collective-permute-start(f32[136,128]{1,0:T(8,128)S(1)} %reduce_sum.38), channel_id=1, source_target_pairs={{0,6},{2,4},{4,2},{6,0},{1,7},{3,5},{5,3},{7,1},{8,14},{10,12},{12... | collective-permute-start | bytes 208904 | tf_op jit(solution)/shard_map/ppermute | solution.py:37
  159.5 7.9 %collective-permute-start.19 = (f32[128,128]{1,0:T(8,128)S(1)}, f32[128,128]{1,0:T(8,128)S(1)}, u32[]{:S(2)}, u32[]{:S(2)}) collective-permute-start(f32[128,128]{1,0:T(8,128)S(1)} %reduce_sum.39), channel_id=1, source_target_pairs={{0,4},{2,6},{4,0},{6,2},{1,5},{3,7},{5,1},{7,3},{8,12},{10,14},{12... | collective-permute-start | bytes 196616 | tf_op jit(solution)/shard_map/ppermute | solution.py:37
  161.7 5.8 %collective-permute-start.18 = (f32[128,128]{1,0:T(8,128)S(1)}, f32[128,128]{1,0:T(8,128)S(1)}, u32[]{:S(2)}, u32[]{:S(2)}) collective-permute-start(f32[128,128]{1,0:T(8,128)S(1)} %reduce_sum.39), channel_id=1, source_target_pairs={{0,2},{2,0},{4,6},{6,4},{1,3},{3,1},{5,7},{7,5},{8,10},{10,8},{12,... | collective-permute-start | bytes 196616 | tf_op jit(solution)/shard_map/ppermute | solution.py:37
  161.9 6.7 %collective-permute-start.17 = (f32[128,128]{1,0:T(8,128)S(1)}, f32[128,128]{1,0:T(8,128)S(1)}, u32[]{:S(2)}, u32[]{:S(2)}) collective-permute-start(f32[128,128]{1,0:T(8,128)S(1)} %reduce_sum.39), channel_id=1, source_target_pairs={{0,6},{2,4},{4,2},{6,0},{1,7},{3,5},{5,3},{7,1},{8,14},{10,12},{12... | collective-permute-start | bytes 196616 | tf_op jit(solution)/shard_map/ppermute | solution.py:37
  182.1 7.0 %collective-permute-start.20 = (f32[4,136,128]{2,1,0:T(8,128)S(1)}, f32[4,136,128]{2,1,0:T(8,128)S(1)}, u32[]{:S(2)}, u32[]{:S(2)}) collective-permute-start(f32[4,136,128]{2,1,0:T(8,128)S(1)} %constant_dynamic-slice_fusion), channel_id=1, source_target_pairs={{0,32},{32,0},{1,33},{33,1},{2,34},{34,2},{3,35},{35,3},{4,36},{36... | collective-permute-start | bytes 835592 | tf_op jit(solution)/shard_map/ppermute | solution.py:37
  189.2 4.8 %collective-permute-start.21 = (f32[136,128]{1,0:T(8,128)S(1)}, f32[136,128]{1,0:T(8,128)S(1)}, u32[]{:S(2)}, u32[]{:S(2)}) collective-permute-start(f32[136,128]{1,0:T(8,128)S(1)} %get-tuple-element.44), channel_id=1, source_target_pairs={{0,128},{64,192},{128,0},{192,64},{1,129},{65,193},{129,1},{193,65... | collective-permute-start | bytes 208904 | tf_op jit(solution)/shard_map/ppermute | solution.py:37
  191.0 4.5 %collective-permute-start.23 = (f32[136,128]{1,0:T(8,128)S(1)}, f32[136,128]{1,0:T(8,128)S(1)}, u32[]{:S(2)}, u32[]{:S(2)}) collective-permute-start(f32[136,128]{1,0:T(8,128)S(1)} %get-tuple-element.45), channel_id=1, source_target_pairs={{0,192},{64,128},{128,64},{192,0},{1,193},{65,129},{129,65},{193,1... | collective-permute-start | bytes 208904 | tf_op jit(solution)/shard_map/ppermute | solution.py:37
  192.0 3.5 %collective-permute-start.22 = (f32[136,128]{1,0:T(8,128)S(1)}, f32[136,128]{1,0:T(8,128)S(1)}, u32[]{:S(2)}, u32[]{:S(2)}) collective-permute-start(f32[136,128]{1,0:T(8,128)S(1)} %get-tuple-element.46), channel_id=1, source_target_pairs={{0,64},{64,0},{128,192},{192,128},{1,65},{65,1},{129,193},{193,129... | collective-permute-start | bytes 208904 | tf_op jit(solution)/shard_map/ppermute | solution.py:37
  195.6 4.7 %collective-permute-start.26 = (f32[128,128]{1,0:T(8,128)S(1)}, f32[128,128]{1,0:T(8,128)S(1)}, u32[]{:S(2)}, u32[]{:S(2)}) collective-permute-start(f32[128,128]{1,0:T(8,128)S(1)} %fusion.4), channel_id=1, source_target_pairs={{0,128},{64,192},{128,0},{192,64},{1,129},{65,193},{129,1},{193,65... | collective-permute-start | bytes 196616 | tf_op jit(solution)/shard_map/ppermute | solution.py:37
  197.7 5.1 %collective-permute-start.25 = (f32[128,128]{1,0:T(8,128)S(1)}, f32[128,128]{1,0:T(8,128)S(1)}, u32[]{:S(2)}, u32[]{:S(2)}) collective-permute-start(f32[128,128]{1,0:T(8,128)S(1)} %fusion.4), channel_id=1, source_target_pairs={{0,192},{64,128},{128,64},{192,0},{1,193},{65,129},{129,65},{193,1... | collective-permute-start | bytes 196616 | tf_op jit(solution)/shard_map/ppermute | solution.py:37
  199.2 3.5 %collective-permute-start.24 = (f32[128,128]{1,0:T(8,128)S(1)}, f32[128,128]{1,0:T(8,128)S(1)}, u32[]{:S(2)}, u32[]{:S(2)}) collective-permute-start(f32[128,128]{1,0:T(8,128)S(1)} %fusion.4), channel_id=1, source_target_pairs={{0,64},{64,0},{128,192},{192,128},{1,65},{65,1},{129,193},{193,129... | collective-permute-start | bytes 196616 | tf_op jit(solution)/shard_map/ppermute | solution.py:37
  202.8 3.1 %collective-permute-start.27 = (f32[512,128]{1,0:T(8,128)S(1)}, f32[512,128]{1,0:T(8,128)S(1)}, u32[]{:S(2)}, u32[]{:S(2)}) collective-permute-start(f32[512,128]{1,0:T(8,128)S(1)} %pad_maximum_fusion.4), channel_id=1, source_target_pairs={{0,32},{32,0},{1,33},{33,1},{2,34},{34,2},{3,35},{35,3},{4,36},{36... | collective-permute-start | bytes 786440 | tf_op jit(solution)/shard_map/ppermute | solution.py:37

commit v6 on v5

--- a/solution.py
+++ b/solution.py
@@ -16,7 +16,7 @@
 TERM_OWN = ("core", "y")
 F32 = jnp.float32
 PAD = 8
-ORDER = (3, 1, 2)
+ORDER = (1, 3, 2)
 SCATTER = (2, 1, 3)
 GATHER = (1, 3, 2)
 HELD = 512

time: 207 us -> 207 us (level)
  starting transfers between devices: 53.3 us -> 51 us
    ppermute x28, starting transfers between devices: 53.3 us -> 51 us  [swap(): lax.ppermute(value, axis, [(at, at ^ by) for at in range(lax.axis_size(ax...]
  transfers between devices with their start and end apart: 28 -> 28, of which waited for: 22 -> 24; matrix products, arithmetic and copies ran while one was open for 0% -> 0% of each run, Pallas kernels for 0% -> 0%
where the time goes in v6:
time: 207 us
  blocking collectives  94.9 us (46%)
  starting transfers between devices  51 us (25%)
  waiting for transfers between devices  40.3 us (19%)
  Pallas kernels  18.1 us (9%)
    all_to_all x8, blocking collectives, exchange(): return lax.all_to_all(blocks, axis, split_axis=0, concat_axis=0, tiled=True)  94.9 us
    ppermute x28, starting transfers between devices, swap(): lax.ppermute(value, axis, [(at, at ^ by) for at in range(lax.axis_size(ax...  51 us
    ppermute x28, waiting for transfers between devices, swap(): lax.ppermute(value, axis, [(at, at ^ by) for at in range(lax.axis_size(ax...  40.3 us
    pallas_call x6, Pallas kernels, call(): pl.pallas_call(kernel, out_shape=outs, in_specs=in_specs, out_specs=out_s...  18.1 us
  transfers between devices with their start and end apart: 28, of which 24 were waited for; matrix products, arithmetic and copies ran while one was open for 0% of the time, Pallas kernels for 0%

profile of v6, /device:TPU:1, one launch (start us, length us, event | category | flops | bytes accessed | tf_op | source)
XLA Modules:
  0.0 206.8 jit_solution(14814023497733624659)
XLA Ops:
  0.7 4.1 %shard_map.50 = (f32[8,136,128]{2,1,0:T(8,128)S(1)}, f32[512,1024]{1,0:T(8,128)S(1)}, f32[128,128]{1,0:T(8,128)S(1)}, f32[128,128]{1,0:T(8,128)S(1)}) custom-call(f32[1024,1024]{1,0:T(8,128)} %slab_ref.5, f32[1024,128]{1,0:T(8,128)} %doc_in, f32[1024,128]{1,0:T(8,128)} %refs_0_.1), custom_call_target="tpu_custom_call" | custom-call | tf_op jit(solution)/shard_map/pallas_call | solution.py:187
  4.8 15.5 %all_to_all.40 = f32[8,136,128]{2,1,0:T(8,128)S(1)} all-to-all(f32[8,136,128]{2,1,0:T(8,128)S(1)} %get-tuple-element.27), channel_id=1, replica_groups=mesh['y'=4,'core'=2,'x'=4,'zh'=4,'zl'=2] {'zl','x'}, dimensions={0} | all-to-all | bytes 1114112 | tf_op jit(solution)/shard_map/all_to_all | solution.py:29
  20.2 6.1 %collective-permute-start.2 = (f32[136,128]{1,0:T(8,128)S(1)}, f32[136,128]{1,0:T(8,128)S(1)}, u32[]{:S(2)}, u32[]{:S(2)}) collective-permute-start(f32[136,128]{1,0:T(8,128)S(1)} %reduce_sum.36), channel_id=1, source_target_pairs={{0,4},{2,6},{4,0},{6,2},{1,5},{3,7},{5,1},{7,3},{8,12},{10,14},{12... | collective-permute-start | bytes 208904 | tf_op jit(solution)/shard_map/ppermute | solution.py:37
  28.1 4.4 %collective-permute-done.1 = f32[136,128]{1,0:T(8,128)S(1)} collective-permute-done((f32[136,128]{1,0:T(8,128)S(1)}, f32[136,128]{1,0:T(8,128)S(1)}, u32[]{:S(2)}, u32[]{:S(2)}) %collective-permute-start.1) | collective-permute-done | bytes 69664 | tf_op jit(solution)/shard_map/ppermute | solution.py:37
  33.0 10.7 %all_to_all.41 = f32[8,128,128]{2,1,0:T(8,128)S(1)} all-to-all(f32[8,128,128]{2,1,0:T(8,128)S(1)} %broadcast_in_dim.12), channel_id=1, replica_groups=mesh['y'=4,'core'=2,'x'=4,'zh'=4,'zl'=2] {'zl','x'}, dimensions={0} | all-to-all | bytes 1048576 | tf_op jit(solution)/shard_map/all_to_all | solution.py:29
  43.7 2.6 %shard_map.51 = f32[8,128,128]{2,1,0:T(8,128)S(1)} custom-call(f32[1024,1024]{1,0:T(8,128)} %slab_ref.5, f32[512,1024]{1,0:T(8,128)S(1)} %get-tuple-element.25.near_ref, f32[1024,128]{1,0:T(8,128)S(1)} %bitcast.63, f32[1024,128]{1,0:T(8,128)S(1)} %copy-done), custom_call_target="tpu_custom_call" | custom-call | tf_op jit(solution)/shard_map/pallas_call | solution.py:187
  46.4 10.8 %all_to_all.42 = f32[8,128,128]{2,1,0:T(8,128)S(1)} all-to-all(f32[8,128,128]{2,1,0:T(8,128)S(1)} %shard_map.51), channel_id=1, replica_groups=mesh['y'=4,'core'=2,'x'=4,'zh'=4,'zl'=2] {'zl','x'}, dimensions={0} | all-to-all | bytes 1048576 | tf_op jit(solution)/shard_map/all_to_all | solution.py:29
  57.2 5.4 %collective-permute-start.5 = (f32[128,128]{1,0:T(8,128)S(1)}, f32[128,128]{1,0:T(8,128)S(1)}, u32[]{:S(2)}, u32[]{:S(2)}) collective-permute-start(f32[128,128]{1,0:T(8,128)S(1)} %reduce_sum.37), channel_id=1, source_target_pairs={{0,4},{2,6},{4,0},{6,2},{1,5},{3,7},{5,1},{7,3},{8,12},{10,14},{12... | collective-permute-start | bytes 196616 | tf_op jit(solution)/shard_map/ppermute | solution.py:37
  64.3 3.6 %collective-permute-done.4 = f32[128,128]{1,0:T(8,128)S(1)} collective-permute-done((f32[128,128]{1,0:T(8,128)S(1)}, f32[128,128]{1,0:T(8,128)S(1)}, u32[]{:S(2)}, u32[]{:S(2)}) %collective-permute-start.4) | collective-permute-done | bytes 65568 | tf_op jit(solution)/shard_map/ppermute | solution.py:37
  67.8 1.5 collective-permute-done.3
  69.4 10.7 %all_to_all.43 = f32[8,128,128]{2,1,0:T(8,128)S(1)} all-to-all(f32[8,128,128]{2,1,0:T(8,128)S(1)} %broadcast_in_dim.13), channel_id=1, replica_groups=mesh['y'=4,'core'=2,'x'=4,'zh'=4,'zl'=2] {'zl','x'}, dimensions={0} | all-to-all | bytes 1048576 | tf_op jit(solution)/shard_map/all_to_all | solution.py:29
  80.1 2.9 %shard_map.52 = f32[8,136,128]{2,1,0:T(8,128)S(1)} custom-call(f32[1024,1024]{1,0:T(8,128)} %slab_ref.5, f32[512,1024]{1,0:T(8,128)S(1)} %get-tuple-element.25.near_ref, f32[1024,128]{1,0:T(8,128)S(1)} %bitcast.60, f32[1024,128]{1,0:T(8,128)S(1)} %copy-done), custom_call_target="tpu_custom_call" | custom-call | tf_op jit(solution)/shard_map/pallas_call | solution.py:187
  83.1 4.6 %collective-permute-start.6 = (f32[4,136,128]{2,1,0:T(8,128)S(1)}, f32[4,136,128]{2,1,0:T(8,128)S(1)}, u32[]{:S(2)}, u32[]{:S(2)}) collective-permute-start(f32[4,136,128]{2,1,0:T(8,128)S(1)} %constant_dynamic-slice_fusion.1), channel_id=1, source_target_pairs={{0,32},{32,0},{1,33},{33,1},{2,34},{34,2},{3,35},{35,3},{4,36},{36... | collective-permute-start | bytes 835592 | tf_op jit(solution)/shard_map/ppermute | solution.py:37
  87.7 1.2 collective-permute-done.6
  88.9 3.2 %collective-permute-start.7 = (f32[136,128]{1,0:T(8,128)S(1)}, f32[136,128]{1,0:T(8,128)S(1)}, u32[]{:S(2)}, u32[]{:S(2)}) collective-permute-start(f32[136,128]{1,0:T(8,128)S(1)} %get-tuple-element.47), channel_id=1, source_target_pairs={{0,128},{64,192},{128,0},{192,64},{1,129},{65,193},{129,1},{193,65... | collective-permute-start | bytes 208904 | tf_op jit(solution)/shard_map/ppermute | solution.py:37
  93.9 2.6 %collective-permute-done.9 = f32[136,128]{1,0:T(8,128)S(1)} collective-permute-done((f32[136,128]{1,0:T(8,128)S(1)}, f32[136,128]{1,0:T(8,128)S(1)}, u32[]{:S(2)}, u32[]{:S(2)}) %collective-permute-start.9) | collective-permute-done | bytes 69664 | tf_op jit(solution)/shard_map/ppermute | solution.py:37
  96.6 1.6 collective-permute-start.12
  98.1 2.0 collective-permute-start.11
  101.3 1.2 collective-permute-done.11
  102.4 1.4 collective-permute-done.10
  104.0 1.8 collective-permute-start.13
  105.8 1.2 collective-permute-done.13.refs_1_
  106.9 2.7 %shard_map.53 = f32[8,136,128]{2,1,0:T(8,128)S(1)} custom-call(f32[1024,1024]{1,0:T(8,128)} %slab_ref.5, f32[512,1024]{1,0:T(8,128)S(1)} %get-tuple-element.25.near_ref, f32[1024,128]{1,0:T(8,128)S(1)} %bitcast.61, f32[512,128]{1,0:T(8,128)S(1)} %pad_maximum_fusion.2.refs_0_, f32[512,128]{1,0:T(8,128)S(1)} %collective-permute-done.13.refs_1_), custom_call_target="tpu_custom_call" | custom-call | tf_op jit(solution)/shard_map/pallas_call | solution.py:187
  109.6 12.5 %all_to_all.44 = f32[8,136,128]{2,1,0:T(8,128)S(1)} all-to-all(f32[8,136,128]{2,1,0:T(8,128)S(1)} %shard_map.53), channel_id=1, replica_groups=mesh['y'=4,'core'=2,'x'=4,'zh'=4,'zl'=2] {'zl','x'}, dimensions={0} | all-to-all | bytes 1114112 | tf_op jit(solution)/shard_map/all_to_all | solution.py:29
  122.1 3.0 %collective-permute-start.16 = (f32[136,128]{1,0:T(8,128)S(1)}, f32[136,128]{1,0:T(8,128)S(1)}, u32[]{:S(2)}, u32[]{:S(2)}) collective-permute-start(f32[136,128]{1,0:T(8,128)S(1)} %reduce_sum.38), channel_id=1, source_target_pairs={{0,4},{2,6},{4,0},{6,2},{1,5},{3,7},{5,1},{7,3},{8,12},{10,14},{12... | collective-permute-start | bytes 208904 | tf_op jit(solution)/shard_map/ppermute | solution.py:37
  125.1 1.3 collective-permute-start.15
  126.4 1.5 collective-permute-start.14
  127.9 1.5 collective-permute-done.16
  129.3 2.5 %collective-permute-done.15 = f32[136,128]{1,0:T(8,128)S(1)} collective-permute-done((f32[136,128]{1,0:T(8,128)S(1)}, f32[136,128]{1,0:T(8,128)S(1)}, u32[]{:S(2)}, u32[]{:S(2)}) %collective-permute-start.15) | collective-permute-done | bytes 69664 | tf_op jit(solution)/shard_map/ppermute | solution.py:37
  131.8 2.4 %collective-permute-done.14 = f32[136,128]{1,0:T(8,128)S(1)} collective-permute-done((f32[136,128]{1,0:T(8,128)S(1)}, f32[136,128]{1,0:T(8,128)S(1)}, u32[]{:S(2)}, u32[]{:S(2)}) %collective-permute-start.14) | collective-permute-done | bytes 69664 | tf_op jit(solution)/shard_map/ppermute | solution.py:37
  134.3 11.3 %all_to_all.45 = f32[8,128,128]{2,1,0:T(8,128)S(1)} all-to-all(f32[8,128,128]{2,1,0:T(8,128)S(1)} %broadcast_in_dim.14), channel_id=1, replica_groups=mesh['y'=4,'core'=2,'x'=4,'zh'=4,'zl'=2] {'zl','x'}, dimensions={0} | all-to-all | bytes 1048576 | tf_op jit(solution)/shard_map/all_to_all | solution.py:29
  145.6 2.7 %shard_map.54 = f32[8,128,128]{2,1,0:T(8,128)S(1)} custom-call(f32[1024,1024]{1,0:T(8,128)} %slab_ref.5, f32[512,1024]{1,0:T(8,128)S(1)} %get-tuple-element.25.near_ref, f32[1024,128]{1,0:T(8,128)S(1)} %bitcast.64, f32[512,128]{1,0:T(8,128)S(1)} %pad_maximum_fusion.2.refs_0_, f32[512,128]{1,0:T(8,128)S(1)} %collective-permute-done.13.refs_1_), custom_call_target="tpu_custom_call" | custom-call | tf_op jit(solution)/shard_map/pallas_call | solution.py:187
  148.3 11.7 %all_to_all.46 = f32[8,128,128]{2,1,0:T(8,128)S(1)} all-to-all(f32[8,128,128]{2,1,0:T(8,128)S(1)} %shard_map.54), channel_id=1, replica_groups=mesh['y'=4,'core'=2,'x'=4,'zh'=4,'zl'=2] {'zl','x'}, dimensions={0} | all-to-all | bytes 1048576 | tf_op jit(solution)/shard_map/all_to_all | solution.py:29
  160.0 3.4 %collective-permute-start.19 = (f32[128,128]{1,0:T(8,128)S(1)}, f32[128,128]{1,0:T(8,128)S(1)}, u32[]{:S(2)}, u32[]{:S(2)}) collective-permute-start(f32[128,128]{1,0:T(8,128)S(1)} %reduce_sum.39), channel_id=1, source_target_pairs={{0,4},{2,6},{4,0},{6,2},{1,5},{3,7},{5,1},{7,3},{8,12},{10,14},{12... | collective-permute-start | bytes 196616 | tf_op jit(solution)/shard_map/ppermute | solution.py:37
  163.5 2.3 %collective-permute-start.17 = (f32[128,128]{1,0:T(8,128)S(1)}, f32[128,128]{1,0:T(8,128)S(1)}, u32[]{:S(2)}, u32[]{:S(2)}) collective-permute-start(f32[128,128]{1,0:T(8,128)S(1)} %reduce_sum.39), channel_id=1, source_target_pairs={{0,2},{2,0},{4,6},{6,4},{1,3},{3,1},{5,7},{7,5},{8,10},{10,8},{12,... | collective-permute-start | bytes 196616 | tf_op jit(solution)/shard_map/ppermute | solution.py:37
  165.7 2.3 %collective-permute-done.19 = f32[128,128]{1,0:T(8,128)S(1)} collective-permute-done((f32[128,128]{1,0:T(8,128)S(1)}, f32[128,128]{1,0:T(8,128)S(1)}, u32[]{:S(2)}, u32[]{:S(2)}) %collective-permute-start.19) | collective-permute-done | bytes 65568 | tf_op jit(solution)/shard_map/ppermute | solution.py:37
  168.0 1.3 collective-permute-done.18
  169.4 11.8 %all_to_all.47 = f32[8,128,128]{2,1,0:T(8,128)S(1)} all-to-all(f32[8,128,128]{2,1,0:T(8,128)S(1)} %broadcast_in_dim.15), channel_id=1, replica_groups=mesh['y'=4,'core'=2,'x'=4,'zh'=4,'zl'=2] {'zl','x'}, dimensions={0} | all-to-all | bytes 1048576 | tf_op jit(solution)/shard_map/all_to_all | solution.py:29
  181.2 3.1 %shard_map.55 = (f32[8,136,128]{2,1,0:T(8,128)S(1)}, f32[1024,128]{1,0:T(8,128)}) custom-call(f32[1024,1024]{1,0:T(8,128)} %slab_ref.5, f32[512,1024]{1,0:T(8,128)S(1)} %get-tuple-element.25.near_ref, f32[1024,128]{1,0:T(8,128)S(1)} %bitcast.62, f32[512,128]{1,0:T(8,128)S(1)} %pad_maximum_fusion.2.refs_0_, f32[512,128]{1,0:T(8,128)S(1)} %collective-permute-done.13.refs_1_), custom_call_target="tpu_custom_call" | custom-call | tf_op jit(solution)/shard_map/pallas_call | solution.py:187
  184.4 3.7 %collective-permute-start.20 = (f32[4,136,128]{2,1,0:T(8,128)S(1)}, f32[4,136,128]{2,1,0:T(8,128)S(1)}, u32[]{:S(2)}, u32[]{:S(2)}) collective-permute-start(f32[4,136,128]{2,1,0:T(8,128)S(1)} %constant_dynamic-slice_fusion), channel_id=1, source_target_pairs={{0,32},{32,0},{1,33},{33,1},{2,34},{34,2},{3,35},{35,3},{4,36},{36... | collective-permute-start | bytes 835592 | tf_op jit(solution)/shard_map/ppermute | solution.py:37
  188.0 1.2 collective-permute-done.20
  189.3 1.8 collective-permute-start.21
  192.0 2.0 collective-permute-done.21
  194.0 1.6 collective-permute-done.23
  195.7 2.2 %collective-permute-start.26 = (f32[128,128]{1,0:T(8,128)S(1)}, f32[128,128]{1,0:T(8,128)S(1)}, u32[]{:S(2)}, u32[]{:S(2)}) collective-permute-start(f32[128,128]{1,0:T(8,128)S(1)} %fusion.4), channel_id=1, source_target_pairs={{0,128},{64,192},{128,0},{192,64},{1,129},{65,193},{129,1},{193,65... | collective-permute-start | bytes 196616 | tf_op jit(solution)/shard_map/ppermute | solution.py:37
  197.8 1.4 collective-permute-start.25
  200.4 2.5 %collective-permute-done.25 = f32[128,128]{1,0:T(8,128)S(1)} collective-permute-done((f32[128,128]{1,0:T(8,128)S(1)}, f32[128,128]{1,0:T(8,128)S(1)}, u32[]{:S(2)}, u32[]{:S(2)}) %collective-permute-start.25) | collective-permute-done | bytes 65568 | tf_op jit(solution)/shard_map/ppermute | solution.py:37
  203.0 1.8 collective-permute-start.27
  (60 shorter events, 11.7 us)
Async XLA Ops:
  0.7 43.1 %copy-start = (f32[1024,128]{1,0:T(8,128)S(1)}, f32[1024,128]{1,0:T(8,128)}, u32[]{:S(2)}) copy-start(f32[1024,128]{1,0:T(8,128)} %refs_0_.1) | copy-start | bytes 1572868
  20.2 7.8 %collective-permute-start.2 = (f32[136,128]{1,0:T(8,128)S(1)}, f32[136,128]{1,0:T(8,128)S(1)}, u32[]{:S(2)}, u32[]{:S(2)}) collective-permute-start(f32[136,128]{1,0:T(8,128)S(1)} %reduce_sum.36), channel_id=1, source_target_pairs={{0,4},{2,6},{4,0},{6,2},{1,5},{3,7},{5,1},{7,3},{8,12},{10,14},{12... | collective-permute-start | bytes 208904 | tf_op jit(solution)/shard_map/ppermute | solution.py:37
  26.3 6.2 %collective-permute-start.1 = (f32[136,128]{1,0:T(8,128)S(1)}, f32[136,128]{1,0:T(8,128)S(1)}, u32[]{:S(2)}, u32[]{:S(2)}) collective-permute-start(f32[136,128]{1,0:T(8,128)S(1)} %reduce_sum.36), channel_id=1, source_target_pairs={{0,6},{2,4},{4,2},{6,0},{1,7},{3,5},{5,3},{7,1},{8,14},{10,12},{12... | collective-permute-start | bytes 208904 | tf_op jit(solution)/shard_map/ppermute | solution.py:37
  26.6 6.3 %collective-permute-start = (f32[136,128]{1,0:T(8,128)S(1)}, f32[136,128]{1,0:T(8,128)S(1)}, u32[]{:S(2)}, u32[]{:S(2)}) collective-permute-start(f32[136,128]{1,0:T(8,128)S(1)} %reduce_sum.36), channel_id=1, source_target_pairs={{0,2},{2,0},{4,6},{6,4},{1,3},{3,1},{5,7},{7,5},{8,10},{10,8},{12,... | collective-permute-start | bytes 208904 | tf_op jit(solution)/shard_map/ppermute | solution.py:37
  57.2 7.1 %collective-permute-start.5 = (f32[128,128]{1,0:T(8,128)S(1)}, f32[128,128]{1,0:T(8,128)S(1)}, u32[]{:S(2)}, u32[]{:S(2)}) collective-permute-start(f32[128,128]{1,0:T(8,128)S(1)} %reduce_sum.37), channel_id=1, source_target_pairs={{0,4},{2,6},{4,0},{6,2},{1,5},{3,7},{5,1},{7,3},{8,12},{10,14},{12... | collective-permute-start | bytes 196616 | tf_op jit(solution)/shard_map/ppermute | solution.py:37
  62.6 5.3 %collective-permute-start.4 = (f32[128,128]{1,0:T(8,128)S(1)}, f32[128,128]{1,0:T(8,128)S(1)}, u32[]{:S(2)}, u32[]{:S(2)}) collective-permute-start(f32[128,128]{1,0:T(8,128)S(1)} %reduce_sum.37), channel_id=1, source_target_pairs={{0,6},{2,4},{4,2},{6,0},{1,7},{3,5},{5,3},{7,1},{8,14},{10,12},{12... | collective-permute-start | bytes 196616 | tf_op jit(solution)/shard_map/ppermute | solution.py:37
  63.6 5.8 %collective-permute-start.3 = (f32[128,128]{1,0:T(8,128)S(1)}, f32[128,128]{1,0:T(8,128)S(1)}, u32[]{:S(2)}, u32[]{:S(2)}) collective-permute-start(f32[128,128]{1,0:T(8,128)S(1)} %reduce_sum.37), channel_id=1, source_target_pairs={{0,2},{2,0},{4,6},{6,4},{1,3},{3,1},{5,7},{7,5},{8,10},{10,8},{12,... | collective-permute-start | bytes 196616 | tf_op jit(solution)/shard_map/ppermute | solution.py:37
  83.1 5.8 %collective-permute-start.6 = (f32[4,136,128]{2,1,0:T(8,128)S(1)}, f32[4,136,128]{2,1,0:T(8,128)S(1)}, u32[]{:S(2)}, u32[]{:S(2)}) collective-permute-start(f32[4,136,128]{2,1,0:T(8,128)S(1)} %constant_dynamic-slice_fusion.1), channel_id=1, source_target_pairs={{0,32},{32,0},{1,33},{33,1},{2,34},{34,2},{3,35},{35,3},{4,36},{36... | collective-permute-start | bytes 835592 | tf_op jit(solution)/shard_map/ppermute | solution.py:37
  88.9 4.9 %collective-permute-start.7 = (f32[136,128]{1,0:T(8,128)S(1)}, f32[136,128]{1,0:T(8,128)S(1)}, u32[]{:S(2)}, u32[]{:S(2)}) collective-permute-start(f32[136,128]{1,0:T(8,128)S(1)} %get-tuple-element.47), channel_id=1, source_target_pairs={{0,128},{64,192},{128,0},{192,64},{1,129},{65,193},{129,1},{193,65... | collective-permute-start | bytes 208904 | tf_op jit(solution)/shard_map/ppermute | solution.py:37
  92.1 4.4 %collective-permute-start.9 = (f32[136,128]{1,0:T(8,128)S(1)}, f32[136,128]{1,0:T(8,128)S(1)}, u32[]{:S(2)}, u32[]{:S(2)}) collective-permute-start(f32[136,128]{1,0:T(8,128)S(1)} %get-tuple-element.48), channel_id=1, source_target_pairs={{0,192},{64,128},{128,64},{192,0},{1,193},{65,129},{129,65},{193,1... | collective-permute-start | bytes 208904 | tf_op jit(solution)/shard_map/ppermute | solution.py:37
  92.9 3.6 %collective-permute-start.8 = (f32[136,128]{1,0:T(8,128)S(1)}, f32[136,128]{1,0:T(8,128)S(1)}, u32[]{:S(2)}, u32[]{:S(2)}) collective-permute-start(f32[136,128]{1,0:T(8,128)S(1)} %get-tuple-element.49), channel_id=1, source_target_pairs={{0,64},{64,0},{128,192},{192,128},{1,65},{65,1},{129,193},{193,129... | collective-permute-start | bytes 208904 | tf_op jit(solution)/shard_map/ppermute | solution.py:37
  96.6 4.7 %collective-permute-start.12 = (f32[128,128]{1,0:T(8,128)S(1)}, f32[128,128]{1,0:T(8,128)S(1)}, u32[]{:S(2)}, u32[]{:S(2)}) collective-permute-start(f32[128,128]{1,0:T(8,128)S(1)} %fusion.6), channel_id=1, source_target_pairs={{0,128},{64,192},{128,0},{192,64},{1,129},{65,193},{129,1},{193,65... | collective-permute-start | bytes 196616 | tf_op jit(solution)/shard_map/ppermute | solution.py:37
  98.1 4.3 %collective-permute-start.11 = (f32[128,128]{1,0:T(8,128)S(1)}, f32[128,128]{1,0:T(8,128)S(1)}, u32[]{:S(2)}, u32[]{:S(2)}) collective-permute-start(f32[128,128]{1,0:T(8,128)S(1)} %fusion.6), channel_id=1, source_target_pairs={{0,192},{64,128},{128,64},{192,0},{1,193},{65,129},{129,65},{193,1... | collective-permute-start | bytes 196616 | tf_op jit(solution)/shard_map/ppermute | solution.py:37
  100.1 3.8 %collective-permute-start.10 = (f32[128,128]{1,0:T(8,128)S(1)}, f32[128,128]{1,0:T(8,128)S(1)}, u32[]{:S(2)}, u32[]{:S(2)}) collective-permute-start(f32[128,128]{1,0:T(8,128)S(1)} %fusion.6), channel_id=1, source_target_pairs={{0,64},{64,0},{128,192},{192,128},{1,65},{65,1},{129,193},{193,129... | collective-permute-start | bytes 196616 | tf_op jit(solution)/shard_map/ppermute | solution.py:37
  104.0 3.0 %collective-permute-start.13 = (f32[512,128]{1,0:T(8,128)S(1)}, f32[512,128]{1,0:T(8,128)S(1)}, u32[]{:S(2)}, u32[]{:S(2)}) collective-permute-start(f32[512,128]{1,0:T(8,128)S(1)} %pad_maximum_fusion.2.refs_0_), channel_id=1, source_target_pairs={{0,32},{32,0},{1,33},{33,1},{2,34},{34,2},{3,35},{35,3},{4,36},{36... | collective-permute-start | bytes 786440 | tf_op jit(solution)/shard_map/ppermute | solution.py:37
  122.1 7.2 %collective-permute-start.16 = (f32[136,128]{1,0:T(8,128)S(1)}, f32[136,128]{1,0:T(8,128)S(1)}, u32[]{:S(2)}, u32[]{:S(2)}) collective-permute-start(f32[136,128]{1,0:T(8,128)S(1)} %reduce_sum.38), channel_id=1, source_target_pairs={{0,4},{2,6},{4,0},{6,2},{1,5},{3,7},{5,1},{7,3},{8,12},{10,14},{12... | collective-permute-start | bytes 208904 | tf_op jit(solution)/shard_map/ppermute | solution.py:37
  125.1 6.8 %collective-permute-start.15 = (f32[136,128]{1,0:T(8,128)S(1)}, f32[136,128]{1,0:T(8,128)S(1)}, u32[]{:S(2)}, u32[]{:S(2)}) collective-permute-start(f32[136,128]{1,0:T(8,128)S(1)} %reduce_sum.38), channel_id=1, source_target_pairs={{0,6},{2,4},{4,2},{6,0},{1,7},{3,5},{5,3},{7,1},{8,14},{10,12},{12... | collective-permute-start | bytes 208904 | tf_op jit(solution)/shard_map/ppermute | solution.py:37
  126.4 7.9 %collective-permute-start.14 = (f32[136,128]{1,0:T(8,128)S(1)}, f32[136,128]{1,0:T(8,128)S(1)}, u32[]{:S(2)}, u32[]{:S(2)}) collective-permute-start(f32[136,128]{1,0:T(8,128)S(1)} %reduce_sum.38), channel_id=1, source_target_pairs={{0,2},{2,0},{4,6},{6,4},{1,3},{3,1},{5,7},{7,5},{8,10},{10,8},{12,... | collective-permute-start | bytes 208904 | tf_op jit(solution)/shard_map/ppermute | solution.py:37
  160.0 8.0 %collective-permute-start.19 = (f32[128,128]{1,0:T(8,128)S(1)}, f32[128,128]{1,0:T(8,128)S(1)}, u32[]{:S(2)}, u32[]{:S(2)}) collective-permute-start(f32[128,128]{1,0:T(8,128)S(1)} %reduce_sum.39), channel_id=1, source_target_pairs={{0,4},{2,6},{4,0},{6,2},{1,5},{3,7},{5,1},{7,3},{8,12},{10,14},{12... | collective-permute-start | bytes 196616 | tf_op jit(solution)/shard_map/ppermute | solution.py:37
  163.5 5.9 %collective-permute-start.18 = (f32[128,128]{1,0:T(8,128)S(1)}, f32[128,128]{1,0:T(8,128)S(1)}, u32[]{:S(2)}, u32[]{:S(2)}) collective-permute-start(f32[128,128]{1,0:T(8,128)S(1)} %reduce_sum.39), channel_id=1, source_target_pairs={{0,6},{2,4},{4,2},{6,0},{1,7},{3,5},{5,3},{7,1},{8,14},{10,12},{12... | collective-permute-start | bytes 196616 | tf_op jit(solution)/shard_map/ppermute | solution.py:37
  163.5 5.9 %collective-permute-start.17 = (f32[128,128]{1,0:T(8,128)S(1)}, f32[128,128]{1,0:T(8,128)S(1)}, u32[]{:S(2)}, u32[]{:S(2)}) collective-permute-start(f32[128,128]{1,0:T(8,128)S(1)} %reduce_sum.39), channel_id=1, source_target_pairs={{0,2},{2,0},{4,6},{6,4},{1,3},{3,1},{5,7},{7,5},{8,10},{10,8},{12,... | collective-permute-start | bytes 196616 | tf_op jit(solution)/shard_map/ppermute | solution.py:37
  184.4 4.9 %collective-permute-start.20 = (f32[4,136,128]{2,1,0:T(8,128)S(1)}, f32[4,136,128]{2,1,0:T(8,128)S(1)}, u32[]{:S(2)}, u32[]{:S(2)}) collective-permute-start(f32[4,136,128]{2,1,0:T(8,128)S(1)} %constant_dynamic-slice_fusion), channel_id=1, source_target_pairs={{0,32},{32,0},{1,33},{33,1},{2,34},{34,2},{3,35},{35,3},{4,36},{36... | collective-permute-start | bytes 835592 | tf_op jit(solution)/shard_map/ppermute | solution.py:37
  189.3 4.8 %collective-permute-start.21 = (f32[136,128]{1,0:T(8,128)S(1)}, f32[136,128]{1,0:T(8,128)S(1)}, u32[]{:S(2)}, u32[]{:S(2)}) collective-permute-start(f32[136,128]{1,0:T(8,128)S(1)} %get-tuple-element.44), channel_id=1, source_target_pairs={{0,128},{64,192},{128,0},{192,64},{1,129},{65,193},{129,1},{193,65... | collective-permute-start | bytes 208904 | tf_op jit(solution)/shard_map/ppermute | solution.py:37
  191.1 4.5 %collective-permute-start.23 = (f32[136,128]{1,0:T(8,128)S(1)}, f32[136,128]{1,0:T(8,128)S(1)}, u32[]{:S(2)}, u32[]{:S(2)}) collective-permute-start(f32[136,128]{1,0:T(8,128)S(1)} %get-tuple-element.45), channel_id=1, source_target_pairs={{0,192},{64,128},{128,64},{192,0},{1,193},{65,129},{129,65},{193,1... | collective-permute-start | bytes 208904 | tf_op jit(solution)/shard_map/ppermute | solution.py:37
  192.0 3.6 %collective-permute-start.22 = (f32[136,128]{1,0:T(8,128)S(1)}, f32[136,128]{1,0:T(8,128)S(1)}, u32[]{:S(2)}, u32[]{:S(2)}) collective-permute-start(f32[136,128]{1,0:T(8,128)S(1)} %get-tuple-element.46), channel_id=1, source_target_pairs={{0,64},{64,0},{128,192},{192,128},{1,65},{65,1},{129,193},{193,129... | collective-permute-start | bytes 208904 | tf_op jit(solution)/shard_map/ppermute | solution.py:37
  195.7 4.7 %collective-permute-start.26 = (f32[128,128]{1,0:T(8,128)S(1)}, f32[128,128]{1,0:T(8,128)S(1)}, u32[]{:S(2)}, u32[]{:S(2)}) collective-permute-start(f32[128,128]{1,0:T(8,128)S(1)} %fusion.4), channel_id=1, source_target_pairs={{0,128},{64,192},{128,0},{192,64},{1,129},{65,193},{129,1},{193,65... | collective-permute-start | bytes 196616 | tf_op jit(solution)/shard_map/ppermute | solution.py:37
  197.8 5.0 %collective-permute-start.25 = (f32[128,128]{1,0:T(8,128)S(1)}, f32[128,128]{1,0:T(8,128)S(1)}, u32[]{:S(2)}, u32[]{:S(2)}) collective-permute-start(f32[128,128]{1,0:T(8,128)S(1)} %fusion.4), channel_id=1, source_target_pairs={{0,192},{64,128},{128,64},{192,0},{1,193},{65,129},{129,65},{193,1... | collective-permute-start | bytes 196616 | tf_op jit(solution)/shard_map/ppermute | solution.py:37
  199.3 3.6 %collective-permute-start.24 = (f32[128,128]{1,0:T(8,128)S(1)}, f32[128,128]{1,0:T(8,128)S(1)}, u32[]{:S(2)}, u32[]{:S(2)}) collective-permute-start(f32[128,128]{1,0:T(8,128)S(1)} %fusion.4), channel_id=1, source_target_pairs={{0,64},{64,0},{128,192},{192,128},{1,65},{65,1},{129,193},{193,129... | collective-permute-start | bytes 196616 | tf_op jit(solution)/shard_map/ppermute | solution.py:37
  203.0 3.0 %collective-permute-start.27 = (f32[512,128]{1,0:T(8,128)S(1)}, f32[512,128]{1,0:T(8,128)S(1)}, u32[]{:S(2)}, u32[]{:S(2)}) collective-permute-start(f32[512,128]{1,0:T(8,128)S(1)} %pad_maximum_fusion.4), channel_id=1, source_target_pairs={{0,32},{32,0},{1,33},{33,1},{2,34},{34,2},{3,35},{35,3},{4,36},{36... | collective-permute-start | bytes 786440 | tf_op jit(solution)/shard_map/ppermute | solution.py:37
